TPU v7x, 128 devices: a whole 4x4x4 slice. The times are simulated.
128 devices in a mesh: req: 8 (over x_lo, y), grp: 16 (over z, x_hi, core).
Axes of the slice: x: 4 (x_hi: 2, x_lo: 2; x = x_hi * 2 + x_lo), y: 4, z: 4, core: 2. Of those that a mesh axis runs over, the one named last changes fastest.
Arguments:
- residual: bfloat16 [8, 16, 128, 4096], P('req', 'grp'), may hold values from -64 to 64
- suffix_proj: bfloat16 [8, 16, 3, 128, 4096], P('req', 'grp'), may hold values from -256 to 256
- prefix_cache: bfloat16 [8, 16, 2, 128, 4096], P('req', 'grp'), may hold values from -8 to 8
- owner_req: int32 [16], replicated, may hold values from 0 to 7, as said below
- lengths: int32 [8, 16], P('req', 'grp'), may hold values from 8 to 128, as said below
- norm_gain: float32 [4096], replicated, may hold values from 0.1 to 1.9
- up_weight: bfloat16 [12288, 4096], P('grp'), may hold values from -0.09375 to 0.09375
- down_weight: bfloat16 [12288, 4096], P('grp'), may hold values from -0.0546875 to 0.0546875
Outputs:
- output: bfloat16 [8, 16, 128, 4096], P('req', 'grp')
Inputs may be any that keep to these rules, and one draw needn't show every extreme that they name: owner_req[g] is the req index whose cache block holds group g's prefix. The first lengths[r, g] of the 128 slots of a request are live; in every req index one request fills all 128 slots.
All inputs are finite; a program needn't handle non-finite values.
Results may differ from a plain program's by a relative error of at most 0.014.
Values may be sent and summed in bfloat16 or wider, within the bound.
No kernel may reach another device: no remote copies, remote signals or barrier semaphores. Data moves between devices by JAX's collectives and lax.ppermute only.
A program may use at most 128 MiB of HBM per device.

v0:
```python
import functools
import math

import jax
import jax.numpy as jnp
from jax import lax
from jax.experimental import pallas as pl
from jax.experimental.pallas import tpu as pltpu
from jax.sharding import PartitionSpec as P


HEADS = 32
NORM_EPS = 1e-05
AXES = ("req", "grp")
F32, BF16 = jnp.float32, jnp.bfloat16
VMEM_LIMIT = 60 * 1024 * 1024


def pairs(move):
    table = []
    for r in range(8):
        for g in range(16):
            xl, y, z, xh, c = r // 4, r % 4, g // 4, (g // 2) % 2, g % 2
            a, b, d, e, f = move(xl, y, z, xh, c)
            table.append((r * 16 + g, (a * 4 + b % 4) * 16 + (d % 4) * 4 + e * 2 + f))
    return tuple(table)


Z_UP = pairs(lambda xl, y, z, xh, c: (xl, y, z + 1, xh, c))
Z_DOWN = pairs(lambda xl, y, z, xh, c: (xl, y, z - 1, xh, c))
Y_UP = pairs(lambda xl, y, z, xh, c: (xl, y + 1, z, xh, c))
Y_DOWN = pairs(lambda xl, y, z, xh, c: (xl, y - 1, z, xh, c))
X_LOW = pairs(lambda xl, y, z, xh, c: (1 - xl, y, z, xh, c))
X_CUT = pairs(lambda xl, y, z, xh, c: (1 - xl, y, z, 1 - xh, c))
CORE = pairs(lambda xl, y, z, xh, c: (xl, y, z, xh, 1 - c))


def req_offset(dx, dy):
    return pairs(lambda xl, y, z, xh, c: ((xl + dx) % 2, y + dy, z, xh, c))


OFFSETS = tuple((dx, dy) for dx in range(2) for dy in (0, 1, 3, 2))


def send(value, table):
    return lax.ppermute(value, AXES, table)


def vmem():
    return pl.BlockSpec(memory_space=pltpu.VMEM)


def smem():
    return pl.BlockSpec(memory_space=pltpu.SMEM)


def hbm():
    return pl.BlockSpec(memory_space=pl.ANY)


def params():
    return pltpu.CompilerParams(vmem_limit_bytes=VMEM_LIMIT)


def cost(flops, nbytes):
    return pl.CostEstimate(flops=int(flops), bytes_accessed=int(nbytes), transcendentals=0)


def cut_kernel(index_ref, cache_ref, *outs):
    for place, out in enumerate(outs):
        row = pl.multiple_of(index_ref[place] * 32, 32)
        out[...] = cache_ref[pl.ds(row, 32), :]


def cut_slices(index, cache):
    width = cache.shape[1]
    return pl.pallas_call(
        cut_kernel,
        out_shape=[jax.ShapeDtypeStruct((32, width), BF16)] * 8,
        in_specs=[smem(), vmem()],
        out_specs=[vmem()] * 8,
        compiler_params=params(),
        cost_estimate=cost(0, 4 * cache.size),
        name="cut_slices",
    )(index, cache)


GROUP = 8


def suffix_kernel(slope_ref, proj_ref, context_ref, max_ref, total_ref):
    step = pl.program_id(0)
    row = lax.broadcasted_iota(jnp.int32, (128, 128), 0)
    col = lax.broadcasted_iota(jnp.int32, (128, 128), 1)
    offset = (col - row).astype(F32)
    seen = col <= row
    tops, totals = jnp.zeros((128, 128), F32), jnp.zeros((128, 128), F32)
    for j in range(GROUP):
        part = slice(j * 128, (j + 1) * 128)
        scores = lax.dot_general(
            proj_ref[0, :, part], proj_ref[1, :, part], (((1,), (1,)), ((), ())), preferred_element_type=F32
        )
        scores = scores * (1.0 / math.sqrt(128)) + slope_ref[step * GROUP + j] * offset
        scores = jnp.where(seen, scores, -jnp.inf)
        top = jnp.max(scores, axis=1, keepdims=True)
        weights = jnp.exp(scores - top)
        total = jnp.sum(weights, axis=1, keepdims=True)
        context_ref[:, part] = jnp.dot(weights.astype(BF16), proj_ref[2, :, part], preferred_element_type=F32)
        tops = jnp.where(col == j, top, tops)
        totals = jnp.where(col == j, total, totals)
    max_ref[0] = tops
    total_ref[0] = totals


def suffix_part(slopes, proj):
    width = proj.shape[2]
    steps = HEADS // GROUP
    stats = jax.ShapeDtypeStruct((steps, 128, 128), F32)
    stats_spec = pl.BlockSpec((1, 128, 128), lambda i: (i, 0, 0))
    return pl.pallas_call(
        suffix_kernel,
        grid=(steps,),
        out_shape=[jax.ShapeDtypeStruct((128, width), F32), stats, stats],
        in_specs=[smem(), pl.BlockSpec((3, 128, width // steps), lambda i: (0, 0, i))],
        out_specs=[pl.BlockSpec((128, width // steps), lambda i: (0, i)), stats_spec, stats_spec],
        compiler_params=params(),
        cost_estimate=cost(4 * 128 * 128 * width, 5 * 128 * width * 2),
        name="suffix_part",
    )(slopes, proj)


def prefix_kernel(
    slope_ref, place_ref, query_ref, context_ref, max_ref, total_ref, residual_ref, gain_ref,
    s0, s1, s2, s3, s4, s5, s6, s7, state_ref, normed_ref, cached,
):
    for place, piece in enumerate((s0, s1, s2, s3, s4, s5, s6, s7)):
        start = pl.multiple_of(place_ref[place] * 32, 32)
        cached[pl.ds(start, 32), :] = piece[...]
    row = lax.broadcasted_iota(jnp.int32, (128, 128), 0)
    col = lax.broadcasted_iota(jnp.int32, (128, 128), 1)
    offset = (col - row - 128).astype(F32)

    def heads(i, running):
        for j in range(GROUP):
            h = i * GROUP + j
            part = pl.ds(pl.multiple_of(h * 128, 128), 128)
            scores = lax.dot_general(
                query_ref[0, :, part], cached[0:128, part], (((1,), (1,)), ((), ())), preferred_element_type=F32
            )
            scores = scores * (1.0 / math.sqrt(128)) + slope_ref[h] * offset
            top = jnp.max(scores, axis=1, keepdims=True)
            weights = jnp.exp(scores - top)
            total = jnp.sum(weights, axis=1, keepdims=True)
            context = jnp.dot(weights.astype(BF16), cached[128:256, part], preferred_element_type=F32)
            other, other_total = max_ref[i, :, j : j + 1], total_ref[i, :, j : j + 1]
            joint = jnp.maximum(top, other)
            first, second = jnp.exp(top - joint), jnp.exp(other - joint)
            share = 1.0 / (first * total + second * other_total)
            merged = (first * share) * context + (second * share) * context_ref[:, part]
            state = (residual_ref[:, part].astype(F32) + merged).astype(BF16)
            state_ref[:, part] = state
            running = running + state.astype(F32)
        return running

    sums = lax.fori_loop(0, HEADS // GROUP, heads, jnp.zeros((128, 128), F32))
    width = state_ref.shape[1]
    mean = jnp.sum(sums, axis=1, keepdims=True) * (1.0 / width)
    squares = jnp.zeros((128, 128), F32)
    for h in range(HEADS):
        part = slice(h * 128, (h + 1) * 128)
        center = state_ref[:, part].astype(F32) - mean
        squares = squares + center * center
    spread = lax.rsqrt(jnp.sum(squares, axis=1, keepdims=True) * (1.0 / width) + NORM_EPS)
    for h in range(HEADS):
        part = slice(h * 128, (h + 1) * 128)
        center = state_ref[:, part].astype(F32) - mean
        normed_ref[:, part] = (center * spread * gain_ref[:, part]).astype(BF16)


def prefix_part(slopes, places, query, suffix, residual, gain, pieces):
    width = query.shape[2]
    return pl.pallas_call(
        prefix_kernel,
        grid=(1,),
        out_shape=[jax.ShapeDtypeStruct((128, width), BF16)] * 2,
        in_specs=[smem(), smem(), pl.BlockSpec((1, 128, width), lambda i: (0, 0, 0))] + [vmem()] * 13,
        out_specs=[vmem()] * 2,
        scratch_shapes=[pltpu.VMEM((256, width), BF16)],
        compiler_params=params(),
        cost_estimate=cost(4 * 128 * 128 * width, 12 * 128 * width * 2),
        name="prefix_part",
    )(slopes, places, query, *suffix, residual, gain.reshape(1, width), *pieces)


UNIT_TILE = 256
COLUMN_TILE = 1024


def unit_copies(units):
    ups, downs, filled = [], [], 0
    for up_at, up_row, down_at, down_row, count in units:
        done = 0
        while done < count:
            take = min(count - done, UNIT_TILE - filled % UNIT_TILE)
            ups.append((up_at, up_row + done, take, filled))
            downs.append((down_at, down_row + done, take, filled))
            done += take
            filled += take
    return ups, downs, filled


def ffn_kernel(token_rows, source_count, ups, downs, with_acc, split, *refs):
    tokens = refs[: len(token_rows)]
    sources = refs[len(token_rows) : len(token_rows) + source_count]
    rest = refs[len(token_rows) + source_count :]
    start_ref = rest[0] if with_acc else None
    rest = rest[1:] if with_acc else rest
    out_count = len(split)
    outs = rest[:out_count]
    rows_buf, up_buf, down_buf, hidden, acc, result, token_sem, up_sem, down_sem, acc_sem, out_sem = rest[out_count:]
    _, width = rows_buf.shape
    at = 0
    moves = []
    for i, count in enumerate(token_rows):
        move = pltpu.make_async_copy(tokens[i], rows_buf.at[pl.ds(at, count), :], token_sem.at[i])
        move.start()
        moves.append(move)
        at += count
    for index, row, count, place in ups:
        pltpu.make_async_copy(
            sources[index].at[pl.ds(row, count), :], up_buf.at[pl.ds(place, count), :], up_sem.at[place // UNIT_TILE]
        ).start()
    for index, row, count, place in downs:
        pltpu.make_async_copy(
            sources[index].at[pl.ds(row, count), :], down_buf.at[pl.ds(place, count), :], down_sem
        ).start()
    if with_acc:
        begin = pltpu.make_async_copy(start_ref, acc, acc_sem)
        begin.start()
    for move in moves:
        move.wait()

    @pl.loop(0, up_buf.shape[0] // UNIT_TILE)
    def _(tile):
        part = pl.ds(pl.multiple_of(tile * UNIT_TILE, UNIT_TILE), UNIT_TILE)
        pltpu.make_async_copy(up_buf.at[part, :], up_buf.at[part, :], up_sem.at[tile]).wait()
        pre = lax.dot_general(
            rows_buf[...], up_buf[part, :], (((1,), (1,)), ((), ())), preferred_element_type=F32
        )
        hidden[:, part] = (0.5 * pre * (1.0 + lax.erf(pre * math.sqrt(0.5)))).astype(BF16)

    pltpu.make_async_copy(down_buf, down_buf, down_sem).wait()
    if with_acc:
        begin.wait()

    def stores(n):
        cols = pl.ds(pl.multiple_of(n * COLUMN_TILE, COLUMN_TILE), COLUMN_TILE)
        at = 0
        for i, count in enumerate(split):
            yield pltpu.make_async_copy(result.at[pl.ds(at, count), cols], outs[i].at[:, cols], out_sem.at[n, i])
            at += count

    @pl.loop(0, width // COLUMN_TILE)
    def _(n):
        cols = pl.ds(pl.multiple_of(n * COLUMN_TILE, COLUMN_TILE), COLUMN_TILE)
        value = jnp.dot(hidden[...], down_buf[:, cols], preferred_element_type=F32)
        if with_acc:
            value = value + acc[:, cols]
        result[:, cols] = value.astype(result.dtype)
        for copy in stores(n):
            copy.start()

    @pl.loop(0, width // COLUMN_TILE)
    def _(n):
        for copy in stores(n):
            copy.wait()


def ffn(tokens, arrays, units, start=None, split=None):
    ups, downs, filled = unit_copies(units)
    rows = tuple(token.shape[0] for token in tokens)
    total, width = sum(rows), tokens[0].shape[1]
    kind = BF16 if split else F32
    split = split or (total,)
    result = pl.pallas_call(
        functools.partial(ffn_kernel, rows, len(arrays), ups, downs, start is not None, split),
        out_shape=[jax.ShapeDtypeStruct((count, width), kind) for count in split],
        in_specs=[hbm()] * (len(tokens) + len(arrays) + (start is not None)),
        out_specs=[hbm()] * len(split),
        scratch_shapes=[
            pltpu.VMEM((total, width), BF16),
            pltpu.VMEM((filled, width), BF16),
            pltpu.VMEM((filled, width), BF16),
            pltpu.VMEM((total, filled), BF16),
            pltpu.VMEM((total if start is not None else 8, width), F32),
            pltpu.VMEM((total, width), kind),
            pltpu.SemaphoreType.DMA((len(tokens),)),
            pltpu.SemaphoreType.DMA((filled // UNIT_TILE,)),
            pltpu.SemaphoreType.DMA,
            pltpu.SemaphoreType.DMA,
            pltpu.SemaphoreType.DMA((width // COLUMN_TILE, len(split))),
        ],
        compiler_params=params(),
        cost_estimate=cost(4 * total * filled * width, 2 * total * width * 3 + 4 * filled * width),
    )(*tokens, *arrays, *(() if start is None else (start,)))
    return result if len(split) > 1 else result[0]


def rows_of(value, start, count):
    return lax.dynamic_slice_in_dim(value, start, count, 0)


def body(residual, suffix_proj, prefix_cache, owner_req, lengths, norm_gain, up, down):
    width = residual.shape[3]
    me = lax.axis_index("req")
    group = lax.axis_index("grp")
    xl, y = me // 4, me % 4
    owner = lax.dynamic_index_in_dim(owner_req, group, 0, keepdims=False)
    slopes = jnp.exp2(-8.0 * jnp.arange(1, HEADS + 1, dtype=F32) / HEADS)

    dests = jnp.stack([((xl + dx) % 2) * 4 + (y + dy) % 4 for dx, dy in OFFSETS]).astype(jnp.int32)
    origins = jnp.stack([((xl + dx) % 2) * 4 + (y - dy) % 4 for dx, dy in OFFSETS]).astype(jnp.int32)
    cuts = cut_slices(dests, prefix_cache.reshape(256, width))
    kept = cuts[0]
    for place in range(1, 8):
        got = send(cuts[place], req_offset(*OFFSETS[place]))
        kept = jnp.where(origins[place] == owner, got, kept)
    pieces = [kept] + [send(kept, req_offset(*OFFSETS[place])) for place in range(1, 8)]

    other = (1 - xl) * 4 + y
    first = other * 64
    shard_send = jnp.concatenate(
        [rows_of(up, first, 32), rows_of(down, first, 32), rows_of(up, first + 32, 32), rows_of(down, first + 32, 32)]
    )
    shard = send(shard_send, X_CUT)
    direct_a = send(jnp.concatenate([up[512:640], down[512:640]]), X_CUT)
    direct_b = send(jnp.concatenate([up[640:768], down[640:768]]), X_CUT)

    suffix = suffix_part(slopes, suffix_proj[0, 0])
    states, normed = prefix_part(
        slopes, origins, suffix_proj[0, 0], suffix, residual[0, 0], norm_gain, pieces
    )

    shard, _ = lax.optimization_barrier((shard, pieces))
    a_own, b_own = shard[:64], shard[64:]
    a_x = send(a_own, X_LOW)
    b_m, b_p = send(b_own, Y_UP), send(b_own, Y_DOWN)
    a_pair = jnp.concatenate([a_own, a_x])
    a_m, a_p = send(a_pair, Y_UP), send(a_pair, Y_DOWN)
    b_2u, b_2d = send(b_m[:32], Y_UP), send(b_p[32:], Y_DOWN)
    b_x = send(jnp.concatenate([b_own, b_m, b_p]), X_LOW)
    a_2u, a_2d = send(a_m[:64], Y_UP), send(a_p[64:], Y_DOWN)
    b_x2 = send(jnp.concatenate([b_2u, b_2d]), X_LOW)
    far = [shard, direct_a, direct_b, a_x, b_m, b_p, a_m, a_p, b_2u, b_2d, b_x, a_2u, a_2d, b_x2]
    far_units = [
        (0, 0, 0, 32, 32), (0, 64, 0, 96, 32), (1, 0, 1, 128, 128), (3, 0, 3, 32, 32),
        (4, 0, 4, 32, 32), (5, 0, 5, 32, 32), (6, 0, 6, 32, 32), (6, 64, 6, 96, 32),
        (7, 0, 7, 32, 32), (7, 64, 7, 96, 32), (8, 0, 9, 0, 32),
        (10, 0, 10, 32, 32), (10, 64, 10, 96, 32), (10, 128, 10, 160, 32),
        (11, 0, 11, 32, 32), (12, 0, 12, 32, 32), (13, 0, 13, 32, 32), (2, 0, 2, 128, 128),
    ]
    near, near_units = [up, down], [(0, 0, 1, 0, 768)]

    t_m, t_p = send(normed, Z_UP), send(normed, Z_DOWN)
    t_0c = send(normed, CORE)
    t_2u, t_2d = send(t_m[:64], Z_UP), send(t_p[64:], Z_DOWN)
    t_mc, t_pc = send(t_m, CORE), send(t_p, CORE)
    t_2uc, t_2dc = send(t_2u, CORE), send(t_2d, CORE)
    own = [normed, t_0c]
    side = [t_m, t_p, t_mc, t_pc]
    far_z = [t_2u, t_2d, t_2uc, t_2dc]
    y_own = ffn(own, near, near_units)
    y_side = ffn(side, near, near_units)
    y_far = ffn(far_z, near, near_units)
    far_mine, far_other = ffn(far_z, far, far_units, y_far, (128, 128))
    m_mine, p_mine, m_other, p_other = ffn(side, far, far_units, y_side, (128, 128, 128, 128))
    own_mine, own_other = ffn(own, far, far_units, y_own, (128, 128))

    def plus(*values):
        return functools.reduce(lambda a, b: a + b, [value.astype(F32) for value in values])

    far_sum = plus(far_mine, send(far_other, CORE)).astype(BF16)
    to_p, to_m = send(far_sum[:64], Z_UP), send(far_sum[64:], Z_DOWN)
    low, high = ((0, 64), (0, 0)), ((64, 0), (0, 0))
    p_all = plus(p_mine, send(p_other, CORE), jnp.pad(to_p, low)).astype(BF16)
    m_all = plus(m_mine, send(m_other, CORE), jnp.pad(to_m, high)).astype(BF16)
    from_m, from_p = send(p_all, Z_UP), send(m_all, Z_DOWN)
    own_core = send(own_other, CORE)
    live = jnp.arange(128, dtype=jnp.int32) < lengths[0, 0]
    combined = plus(states, own_mine, own_core, from_m, from_p)
    return jnp.where(live[:, None], combined, 0.0).astype(BF16)[None, None]


def solution(mesh):
    placed = (
        P("req", "grp", None, None),
        P("req", "grp", None, None, None),
        P("req", "grp", None, None, None),
        P(),
        P("req", "grp"),
        P(),
        P("grp", None),
        P("grp", None),
    )
    return jax.shard_map(body, mesh=mesh, in_specs=placed, out_specs=P("req", "grp", None, None), check_vma=False)
```

profile of v0, /device:TPU:0, one launch (start us, length us, event | category | flops | bytes accessed | tf_op | source)
XLA Modules:
  0.0 299.2 jit_solution(10513532990928675541)
XLA Ops:
  0.6 3.1 %cut_slices.1 = (bf16[32,4096]{1,0:T(8,128)(2,1)}, bf16[32,4096]{1,0:T(8,128)(2,1)}, bf16[32,4096]{1,0:T(8,128)(2,1)}, bf16[32,4096]{1,0:T(8,128)(2,1)}, bf16[32...) custom-call(s32[8]{0:T(128)} %stack.65.index_ref, ...), custom_call_target="tpu_custom_call" | custom-call | bytes 4194304 | tf_op jit(solution)/shard_map/cut_slices/pallas_call | solution.py:77
  3.7 4.3 %collective-permute-start = (bf16[32,4096]{1,0:T(8,128)(2,1)}, bf16[32,4096]{1,0:T(8,128)(2,1)S(1)}, u32[]{:S(2)}, u32[]{:S(2)}) collective-permute-start(bf16[32,4096]{1,0:T(8,128)(2,1)} %get-tuple-element.30), channel_id=1, source_target_pairs={{0,96},{1,97},{2,98},{3,99},{4,100},{5,101},{6,102},{7,103},{8,104... | collective-permute-start | bytes 786440 | tf_op jit(solution)/shard_map/ppermute | solution.py:46
  8.0 1.0 collective-permute-start.1
  9.0 1.9 collective-permute-start.2
  16.7 1.3 constant_dynamic-slice_fusion.2
  18.0 2.7 collective-permute-start.5
  20.7 0.9 collective-permute-done.1
  21.6 1.2 collective-permute-start.6
  22.9 1.1 pad_maximum_fusion.3
  23.9 4.0 %collective-permute-done.2 = bf16[32,4096]{1,0:T(8,128)(2,1)S(1)} collective-permute-done((bf16[32,4096]{1,0:T(8,128)(2,1)}, bf16[32,4096]{1,0:T(8,128)(2,1)S(1)}, u32[]{:S(2)}, u32[]{:S(2)}) %collective-permute-start.2) | collective-permute-done | bytes 262176 | tf_op jit(solution)/shard_map/ppermute | solution.py:46
  27.9 2.8 collective-permute-start.15
  30.7 1.1 collective-permute-done.3
  32.5 0.9 collective-permute-start.7
  33.4 2.4 collective-permute-start.8
  35.8 1.0 collective-permute-start.9
  36.8 4.0 %fusion.1 = (bf16[128,4096]{1,0:T(8,128)(2,1)}, bf16[128,4096]{1,0:T(8,128)(2,1)S(1)}, bf16[128,4096]{1,0:T(8,128)(2,1)S(1)}, bf16[128,4096]{1,0:T(8,128)(2,1)}) fusion(bf16[768,4096]{1,0:T(8,128)(2,1)} %refs_4_.3, bf16[768,4096]{1,0:T(8,128)(2,1)} %refs_5_.3), kind=kLoop, calls=%fused_computation.18 | loop fusion | bytes 8388608 | tf_op jit(solution)/shard_map/slice | solution.py:337
  40.8 1.5 collective-permute-start.10
  42.3 1.2 collective-permute-start.11
  43.5 3.1 %collective-permute-done.8.s2 = bf16[32,4096]{1,0:T(8,128)(2,1)S(1)} collective-permute-done((bf16[32,4096]{1,0:T(8,128)(2,1)S(1)}, bf16[32,4096]{1,0:T(8,128)(2,1)S(1)}, u32[]{:S(2)}, u32[]{:S(2)}) %collective-permute-start.8) | collective-permute-done | bytes 262176 | tf_op jit(solution)/shard_map/ppermute | solution.py:46
  46.6 4.6 %collective-permute-start.12 = (bf16[32,4096]{1,0:T(8,128)(2,1)S(1)}, bf16[32,4096]{1,0:T(8,128)(2,1)}, u32[]{:S(2)}, u32[]{:S(2)}) collective-permute-start(bf16[32,4096]{1,0:T(8,128)(2,1)S(1)} %select_select_fusion.s0), channel_id=1, source_target_pairs={{0,112},{1,113},{2,114},{3,115},{4,116},{5,117},{6,118},{7,119},{8... | collective-permute-start | bytes 786440 | tf_op jit(solution)/shard_map/ppermute | solution.py:46
  51.3 1.5 pad_maximum_fusion
  54.0 10.3 %suffix_part.1 = (f32[128,4096]{1,0:T(8,128)}, f32[4,128,128]{2,1,0:T(8,128)}, f32[4,128,128]{2,1,0:T(8,128)}) custom-call(f32[32]{0:T(128)} %multiply_exponential_fusion.slope_ref, bf16[3,128,4096]{2,1,0:T(8,128)(2,1)} %bitcast.23), custom_call_target="tpu_custom_call" | custom-call | flops 268435456 | bytes 5242880 | tf_op jit(solution)/shard_map/suffix_part/pallas_call | solution.py:120
  64.2 2.2 collective-permute-start.16
  66.8 14.8 %prefix_part.1 = (bf16[128,4096]{1,0:T(8,128)(2,1)}, bf16[128,4096]{1,0:T(8,128)(2,1)}) custom-call(f32[32]{0:T(128)} %multiply_exponential_fusion.slope_ref, s32[8]{0:T(128)} %stack.58.place_ref, bf16[3,128,4096]{2,1,0:T(8,128)(2,1)} %bitcast.24, f32[128,4096]{1,0:T(8,128)} %get-tuple-element.27.context_ref, f32[4,128,128]{2,1,0:T(8,128)} %get-tuple-element.28.max_ref, ...), custom_call_target="tpu_custom_call" | custom-call | flops 268435456 | bytes 12582912 | tf_op jit(solution)/shard_map/prefix_part/pallas_call | solution.py:182
  81.6 2.0 collective-permute-start.30
  84.6 2.8 collective-permute-start.17
  87.4 2.7 collective-permute-start.20
  90.1 6.5 %collective-permute-done.19.refs_6_.refs_8_ = bf16[64,4096]{1,0:T(8,128)(2,1)S(1)} collective-permute-done((bf16[64,4096]{1,0:T(8,128)(2,1)S(1)}, bf16[64,4096]{1,0:T(8,128)(2,1)S(1)}, u32[]{:S(2)}, u32[]{:S(2)}) %collective-permute-start.19) | collective-permute-done | bytes 524320 | tf_op jit(solution)/shard_map/ppermute | solution.py:46
  96.6 2.4 collective-permute-start.31
  99.0 1.5 collective-permute-start.18
  100.5 6.9 %collective-permute-done.30.refs_0_ = bf16[128,4096]{1,0:T(8,128)(2,1)} collective-permute-done((bf16[128,4096]{1,0:T(8,128)(2,1)}, bf16[128,4096]{1,0:T(8,128)(2,1)}, u32[]{:S(2)}, u32[]{:S(2)}) %collective-permute-start.30) | collective-permute-done | bytes 1048608 | tf_op jit(solution)/shard_map/ppermute | solution.py:46
  107.6 1.1 slice.60
  108.7 1.3 pad_maximum_fusion.2
  110.0 8.8 %collective-permute-done.31.refs_1_ = bf16[128,4096]{1,0:T(8,128)(2,1)} collective-permute-done((bf16[128,4096]{1,0:T(8,128)(2,1)S(1)}, bf16[128,4096]{1,0:T(8,128)(2,1)}, u32[]{:S(2)}, u32[]{:S(2)}) %collective-permute-start.31) | collective-permute-done | bytes 1048608 | tf_op jit(solution)/shard_map/ppermute | solution.py:46
  118.8 1.8 collective-permute-start.35
  120.7 1.1 slice.61
  121.8 2.0 collective-permute-start.21
  123.8 3.2 %collective-permute-done.24.refs_11_.refs_13_ = bf16[32,4096]{1,0:T(8,128)(2,1)S(1)} collective-permute-done((bf16[32,4096]{1,0:T(8,128)(2,1)S(1)}, bf16[32,4096]{1,0:T(8,128)(2,1)S(1)}, u32[]{:S(2)}, u32[]{:S(2)}) %collective-permute-start.24) | collective-permute-done | bytes 262176 | tf_op jit(solution)/shard_map/ppermute | solution.py:46
  127.7 1.5 collective-permute-start.25
  129.3 26.3 %collective-permute-done.17.refs_4_.refs_6_ = bf16[256,4096]{1,0:T(8,128)(2,1)} collective-permute-done((bf16[256,4096]{1,0:T(8,128)(2,1)S(1)}, bf16[256,4096]{1,0:T(8,128)(2,1)}, u32[]{:S(2)}, u32[]{:S(2)}) %collective-permute-start.17) | collective-permute-done | bytes 2097184 | tf_op jit(solution)/shard_map/ppermute | solution.py:46
  155.5 4.0 %collective-permute-start.36 = (bf16[64,4096]{1,0:T(8,128)(2,1)S(1)}, bf16[64,4096]{1,0:T(8,128)(2,1)S(1)}, u32[]{:S(2)}, u32[]{:S(2)}) collective-permute-start(bf16[64,4096]{1,0:T(8,128)(2,1)S(1)} %slice.61), channel_id=1, source_target_pairs={{0,12},{1,13},{2,14},{3,15},{4,0},{5,1},{6,2},{7,3},{8,4},{9,5},{1... | collective-permute-start | bytes 1572872 | tf_op jit(solution)/shard_map/ppermute | solution.py:46
  159.6 7.7 %collective-permute-done.36.refs_1_ = bf16[64,4096]{1,0:T(8,128)(2,1)S(1)} collective-permute-done((bf16[64,4096]{1,0:T(8,128)(2,1)S(1)}, bf16[64,4096]{1,0:T(8,128)(2,1)S(1)}, u32[]{:S(2)}, u32[]{:S(2)}) %collective-permute-start.36) | collective-permute-done | bytes 524320 | tf_op jit(solution)/shard_map/ppermute | solution.py:46
  167.3 2.6 collective-permute-done.28.refs_15_.refs_17_
  171.0 0.9 slice.58
  171.9 0.9 slice.59
  172.8 1.9 collective-permute-start.26
  174.7 0.8 copy-done.18
  175.5 2.6 collective-permute-start.27
  178.0 9.7 %shard_map.86.refs_18_ = f32[256,4096]{1,0:T(8,128)} custom-call(bf16[64,4096]{1,0:T(8,128)(2,1)} %copy-done.15, bf16[64,4096]{1,0:T(8,128)(2,1)} %copy-done.16, bf16[64,4096]{1,0:T(8,128)(2,1)} %copy-done.17, bf16[64,4096]{1,0:T(8,128)(2,1)} %copy-done.18, bf16[768,4096]{1,0:T(8,128)(2,1)} %refs_4_.3, bf16[768,4096]{1,0:T(8,128)(2,1)} %refs_5_.3), custom_call_target="tpu_custom_call" | custom-call | flops 3221225472 | bytes 18874368 | tf_op jit(solution)/shard_map/pallas_call | solution.py:285
  187.9 1.4 collective-permute-done.26.refs_13_.refs_15_
  190.0 10.3 %shard_map.87 = (bf16[128,4096]{1,0:T(8,128)(2,1)}, bf16[128,4096]{1,0:T(8,128)(2,1)}) custom-call(bf16[64,4096]{1,0:T(8,128)(2,1)} %copy-done.15, bf16[64,4096]{1,0:T(8,128)(2,1)} %copy-done.16, bf16[64,4096]{1,0:T(8,128)(2,1)} %copy-done.17, bf16[64,4096]{1,0:T(8,128)(2,1)} %copy-done.18, bf16[128,4096]{1,0:T(8,128)(2,1)} %copy-done.1, ...), custom_call_target="tpu_custom_call" | custom-call | flops 3221225472 | bytes 18874368 | tf_op jit(solution)/shard_map/pallas_call | solution.py:285
  200.5 13.9 %shard_map.84.refs_18_ = f32[512,4096]{1,0:T(8,128)} custom-call(bf16[128,4096]{1,0:T(8,128)(2,1)} %collective-permute-done.30.refs_0_, bf16[128,4096]{1,0:T(8,128)(2,1)} %collective-permute-done.31.refs_1_, bf16[128,4096]{1,0:T(8,128)(2,1)} %collective-permute-done.32.refs_2_, bf16[128,4096]{1,0:T(8,128)(2,1)} %collective-permute-done.33.refs_3_, ...), custom_call_target="tpu_custom_call" | custom-call | flops 6442450944 | bytes 25165824 | tf_op jit(solution)/shard_map/pallas_call | solution.py:285
  214.4 14.4 %shard_map.85 = (bf16[128,4096]{1,0:T(8,128)(2,1)}, bf16[128,4096]{1,0:T(8,128)(2,1)}, bf16[128,4096]{1,0:T(8,128)(2,1)}, bf16[128,4096]{1,0:T(8,128)(2,1)}) custom-call(bf16[128,4096]{1,0:T(8,128)(2,1)} %collective-permute-done.30.refs_0_, bf16[128,4096]{1,0:T(8,128)(2,1)} %collective-permute-done.31.refs_1_, ...), custom_call_target="tpu_custom_call" | custom-call | flops 6442450944 | bytes 25165824 | tf_op jit(solution)/shard_map/pallas_call | solution.py:285
  229.4 1.5 add_convert_fusion.2
  230.8 1.0 fusion.3
  231.9 2.6 collective-permute-start.43
  234.5 1.0 copy-done.12
  235.5 9.7 %shard_map.82.refs_16_ = f32[256,4096]{1,0:T(8,128)} custom-call(bf16[128,4096]{1,0:T(8,128)(2,1)} %get-tuple-element.39.refs_0_, bf16[128,4096]{1,0:T(8,128)(2,1)} %copy-done.12, bf16[768,4096]{1,0:T(8,128)(2,1)} %refs_4_.3, bf16[768,4096]{1,0:T(8,128)(2,1)} %refs_5_.3), custom_call_target="tpu_custom_call" | custom-call | flops 3221225472 | bytes 18874368 | tf_op jit(solution)/shard_map/pallas_call | solution.py:285
  245.3 10.2 %shard_map.83 = (bf16[128,4096]{1,0:T(8,128)(2,1)}, bf16[128,4096]{1,0:T(8,128)(2,1)}) custom-call(bf16[128,4096]{1,0:T(8,128)(2,1)} %get-tuple-element.39.refs_0_, bf16[128,4096]{1,0:T(8,128)(2,1)} %copy-done.12, bf16[128,4096]{1,0:T(8,128)(2,1)} %copy-done.1, bf16[256,4096]{1,0:T(8,128)(2,1)} %copy-done, ...), custom_call_target="tpu_custom_call" | custom-call | flops 3221225472 | bytes 18874368 | tf_op jit(solution)/shard_map/pallas_call | solution.py:285
  256.4 3.3 %collective-permute-start.44 = (bf16[128,4096]{1,0:T(8,128)(2,1)S(1)}, bf16[128,4096]{1,0:T(8,128)(2,1)S(1)}, u32[]{:S(2)}, u32[]{:S(2)}) collective-permute-start(bf16[128,4096]{1,0:T(8,128)(2,1)S(1)} %add_convert_fusion), channel_id=1, source_target_pairs={{0,12},{1,13},{2,14},{3,15},{4,0},{5,1},{6,2},{7,3},{8,4},{9,5},{1... | collective-permute-start | bytes 3145736 | tf_op jit(solution)/shard_map/ppermute | solution.py:46
  259.7 11.6 %collective-permute-done.40 = bf16[64,4096]{1,0:T(8,128)(2,1)S(1)} collective-permute-done((bf16[64,4096]{1,0:T(8,128)(2,1)}, bf16[64,4096]{1,0:T(8,128)(2,1)S(1)}, u32[]{:S(2)}, u32[]{:S(2)}) %collective-permute-start.40) | collective-permute-done | bytes 524320 | tf_op jit(solution)/shard_map/ppermute | solution.py:46
  272.5 9.6 %collective-permute-done.44 = bf16[128,4096]{1,0:T(8,128)(2,1)S(1)} collective-permute-done((bf16[128,4096]{1,0:T(8,128)(2,1)S(1)}, bf16[128,4096]{1,0:T(8,128)(2,1)S(1)}, u32[]{:S(2)}, u32[]{:S(2)}) %collective-permute-start.44) | collective-permute-done | bytes 1048608 | tf_op jit(solution)/shard_map/ppermute | solution.py:46
  282.1 15.2 %collective-permute-done.41 = bf16[128,4096]{1,0:T(8,128)(2,1)S(1)} collective-permute-done((bf16[128,4096]{1,0:T(8,128)(2,1)S(1)}, bf16[128,4096]{1,0:T(8,128)(2,1)S(1)}, u32[]{:S(2)}, u32[]{:S(2)}) %collective-permute-start.41) | collective-permute-done | bytes 1048608 | tf_op jit(solution)/shard_map/ppermute | solution.py:46
  297.3 1.9 fusion
  (125 shorter events, 11.0 us)
Async XLA Ops:
  0.0 12.2 %copy-start.31 = (s32[16]{0:T(128)S(1)}, s32[16]{0:T(128)}, u32[]{:S(2)}) copy-start(s32[16]{0:T(128)} %param.11) | copy-start | bytes 196
  3.7 14.4 %copy-start.30 = (bf16[32,4096]{1,0:T(8,128)(2,1)S(1)}, bf16[32,4096]{1,0:T(8,128)(2,1)}, u32[]{:S(2)}) copy-start(bf16[32,4096]{1,0:T(8,128)(2,1)} %get-tuple-element.35) | copy-start | bytes 786436
  3.7 18.0 %copy-start.29 = (bf16[32,4096]{1,0:T(8,128)(2,1)S(1)}, bf16[32,4096]{1,0:T(8,128)(2,1)}, u32[]{:S(2)}) copy-start(bf16[32,4096]{1,0:T(8,128)(2,1)} %get-tuple-element.36) | copy-start | bytes 786436
  3.7 14.3 %collective-permute-start = (bf16[32,4096]{1,0:T(8,128)(2,1)}, bf16[32,4096]{1,0:T(8,128)(2,1)S(1)}, u32[]{:S(2)}, u32[]{:S(2)}) collective-permute-start(bf16[32,4096]{1,0:T(8,128)(2,1)} %get-tuple-element.30), channel_id=1, source_target_pairs={{0,96},{1,97},{2,98},{3,99},{4,100},{5,101},{6,102},{7,103},{8,104... | collective-permute-start | bytes 786440 | tf_op jit(solution)/shard_map/ppermute | solution.py:46
  8.0 13.7 %collective-permute-start.1 = (bf16[32,4096]{1,0:T(8,128)(2,1)}, bf16[32,4096]{1,0:T(8,128)(2,1)S(1)}, u32[]{:S(2)}, u32[]{:S(2)}) collective-permute-start(bf16[32,4096]{1,0:T(8,128)(2,1)} %get-tuple-element.31), channel_id=1, source_target_pairs={{0,112},{1,113},{2,114},{3,115},{4,116},{5,117},{6,118},{7,119},{8... | collective-permute-start | bytes 786440 | tf_op jit(solution)/shard_map/ppermute | solution.py:46
  9.0 18.9 %collective-permute-start.2 = (bf16[32,4096]{1,0:T(8,128)(2,1)}, bf16[32,4096]{1,0:T(8,128)(2,1)S(1)}, u32[]{:S(2)}, u32[]{:S(2)}) collective-permute-start(bf16[32,4096]{1,0:T(8,128)(2,1)} %get-tuple-element.32), channel_id=1, source_target_pairs={{0,80},{1,81},{2,82},{3,83},{4,84},{5,85},{6,86},{7,87},{8,88},{9,... | collective-permute-start | bytes 786440 | tf_op jit(solution)/shard_map/ppermute | solution.py:46
  10.9 20.9 %collective-permute-start.3 = (bf16[32,4096]{1,0:T(8,128)(2,1)}, bf16[32,4096]{1,0:T(8,128)(2,1)S(1)}, u32[]{:S(2)}, u32[]{:S(2)}) collective-permute-start(bf16[32,4096]{1,0:T(8,128)(2,1)} %get-tuple-element.33), channel_id=1, source_target_pairs={{0,64},{1,65},{2,66},{3,67},{4,68},{5,69},{6,70},{7,71},{8,72},{9,... | collective-permute-start | bytes 786440 | tf_op jit(solution)/shard_map/ppermute | solution.py:46
  11.4 20.4 %collective-permute-start.4 = (bf16[32,4096]{1,0:T(8,128)(2,1)}, bf16[32,4096]{1,0:T(8,128)(2,1)S(1)}, u32[]{:S(2)}, u32[]{:S(2)}) collective-permute-start(bf16[32,4096]{1,0:T(8,128)(2,1)} %get-tuple-element.34), channel_id=1, source_target_pairs={{0,32},{1,33},{2,34},{3,35},{4,36},{5,37},{6,38},{7,39},{8,40},{9,... | collective-permute-start | bytes 786440 | tf_op jit(solution)/shard_map/ppermute | solution.py:46
  16.7 15.7 %copy-start.28 = (bf16[32,4096]{1,0:T(8,128)(2,1)S(1)}, bf16[32,4096]{1,0:T(8,128)(2,1)}, u32[]{:S(2)}) copy-start(bf16[32,4096]{1,0:T(8,128)(2,1)} %get-tuple-element.37) | copy-start | bytes 786436
  18.0 13.7 %collective-permute-start.5 = (bf16[32,4096]{1,0:T(8,128)(2,1)S(1)}, bf16[32,4096]{1,0:T(8,128)(2,1)S(1)}, u32[]{:S(2)}, u32[]{:S(2)}) collective-permute-start(bf16[32,4096]{1,0:T(8,128)(2,1)S(1)} %copy-done.30), channel_id=1, source_target_pairs={{0,48},{1,49},{2,50},{3,51},{4,52},{5,53},{6,54},{7,55},{8,56},{9,... | collective-permute-start | bytes 786440 | tf_op jit(solution)/shard_map/ppermute | solution.py:46
  21.6 10.7 %collective-permute-start.6 = (bf16[32,4096]{1,0:T(8,128)(2,1)S(1)}, bf16[32,4096]{1,0:T(8,128)(2,1)S(1)}, u32[]{:S(2)}, u32[]{:S(2)}) collective-permute-start(bf16[32,4096]{1,0:T(8,128)(2,1)S(1)} %copy-done.29), channel_id=1, source_target_pairs={{0,16},{1,17},{2,18},{3,19},{4,20},{5,21},{6,22},{7,23},{8,24},{9,... | collective-permute-start | bytes 786440 | tf_op jit(solution)/shard_map/ppermute | solution.py:46
  27.9 55.7 %collective-permute-start.15 = (bf16[128,4096]{1,0:T(8,128)(2,1)}, bf16[128,4096]{1,0:T(8,128)(2,1)S(1)}, u32[]{:S(2)}, u32[]{:S(2)}) collective-permute-start(bf16[128,4096]{1,0:T(8,128)(2,1)} %pad_maximum_fusion.3), channel_id=1, source_target_pairs={{0,66},{1,67},{2,64},{3,65},{4,70},{5,71},{6,68},{7,69},{8,74},{9,... | collective-permute-start | bytes 3145736 | tf_op jit(solution)/shard_map/ppermute | solution.py:46
  32.5 18.8 %copy-start.24 = (bf16[32,4096]{1,0:T(8,128)(2,1)}, bf16[32,4096]{1,0:T(8,128)(2,1)S(1)}, u32[]{:S(2)}) copy-start(bf16[32,4096]{1,0:T(8,128)(2,1)S(1)} %select_select_fusion.s0) | copy-start | bytes 786436
  32.5 9.8 %collective-permute-start.7 = (bf16[32,4096]{1,0:T(8,128)(2,1)S(1)}, bf16[32,4096]{1,0:T(8,128)(2,1)S(1)}, u32[]{:S(2)}, u32[]{:S(2)}) collective-permute-start(bf16[32,4096]{1,0:T(8,128)(2,1)S(1)} %select_select_fusion.s0), channel_id=1, source_target_pairs={{0,16},{1,17},{2,18},{3,19},{4,20},{5,21},{6,22},{7,23},{8,24},{9,... | collective-permute-start | bytes 786440 | tf_op jit(solution)/shard_map/ppermute | solution.py:46
  33.4 13.2 %collective-permute-start.8 = (bf16[32,4096]{1,0:T(8,128)(2,1)S(1)}, bf16[32,4096]{1,0:T(8,128)(2,1)S(1)}, u32[]{:S(2)}, u32[]{:S(2)}) collective-permute-start(bf16[32,4096]{1,0:T(8,128)(2,1)S(1)} %select_select_fusion.s0), channel_id=1, source_target_pairs={{0,48},{1,49},{2,50},{3,51},{4,52},{5,53},{6,54},{7,55},{8,56},{9,... | collective-permute-start | bytes 786440 | tf_op jit(solution)/shard_map/ppermute | solution.py:46
  35.8 15.4 %collective-permute-start.9 = (bf16[32,4096]{1,0:T(8,128)(2,1)S(1)}, bf16[32,4096]{1,0:T(8,128)(2,1)S(1)}, u32[]{:S(2)}, u32[]{:S(2)}) collective-permute-start(bf16[32,4096]{1,0:T(8,128)(2,1)S(1)} %select_select_fusion.s0), channel_id=1, source_target_pairs={{0,32},{1,33},{2,34},{3,35},{4,36},{5,37},{6,38},{7,39},{8,40},{9,... | collective-permute-start | bytes 786440 | tf_op jit(solution)/shard_map/ppermute | solution.py:46
  40.8 23.4 %collective-permute-start.10 = (bf16[32,4096]{1,0:T(8,128)(2,1)S(1)}, bf16[32,4096]{1,0:T(8,128)(2,1)}, u32[]{:S(2)}, u32[]{:S(2)}) collective-permute-start(bf16[32,4096]{1,0:T(8,128)(2,1)S(1)} %select_select_fusion.s0), channel_id=1, source_target_pairs={{0,64},{1,65},{2,66},{3,67},{4,68},{5,69},{6,70},{7,71},{8,72},{9,... | collective-permute-start | bytes 786440 | tf_op jit(solution)/shard_map/ppermute | solution.py:46
  42.3 10.6 %copy-start.25 = (bf16[32,4096]{1,0:T(8,128)(2,1)}, bf16[32,4096]{1,0:T(8,128)(2,1)S(1)}, u32[]{:S(2)}) copy-start(bf16[32,4096]{1,0:T(8,128)(2,1)S(1)} %collective-permute-done.7.s1) | copy-start | bytes 786436
  42.3 24.1 %collective-permute-start.11 = (bf16[32,4096]{1,0:T(8,128)(2,1)S(1)}, bf16[32,4096]{1,0:T(8,128)(2,1)}, u32[]{:S(2)}, u32[]{:S(2)}) collective-permute-start(bf16[32,4096]{1,0:T(8,128)(2,1)S(1)} %select_select_fusion.s0), channel_id=1, source_target_pairs={{0,80},{1,81},{2,82},{3,83},{4,84},{5,85},{6,86},{7,87},{8,88},{9,... | collective-permute-start | bytes 786440 | tf_op jit(solution)/shard_map/ppermute | solution.py:46
  46.6 6.3 %copy-start.26 = (bf16[32,4096]{1,0:T(8,128)(2,1)}, bf16[32,4096]{1,0:T(8,128)(2,1)S(1)}, u32[]{:S(2)}) copy-start(bf16[32,4096]{1,0:T(8,128)(2,1)S(1)} %collective-permute-done.8.s2) | copy-start | bytes 786436
  46.6 19.8 %collective-permute-start.12 = (bf16[32,4096]{1,0:T(8,128)(2,1)S(1)}, bf16[32,4096]{1,0:T(8,128)(2,1)}, u32[]{:S(2)}, u32[]{:S(2)}) collective-permute-start(bf16[32,4096]{1,0:T(8,128)(2,1)S(1)} %select_select_fusion.s0), channel_id=1, source_target_pairs={{0,112},{1,113},{2,114},{3,115},{4,116},{5,117},{6,118},{7,119},{8... | collective-permute-start | bytes 786440 | tf_op jit(solution)/shard_map/ppermute | solution.py:46
  51.3 15.6 %collective-permute-start.13 = (bf16[32,4096]{1,0:T(8,128)(2,1)S(1)}, bf16[32,4096]{1,0:T(8,128)(2,1)}, u32[]{:S(2)}, u32[]{:S(2)}) collective-permute-start(bf16[32,4096]{1,0:T(8,128)(2,1)S(1)} %select_select_fusion.s0), channel_id=1, source_target_pairs={{0,96},{1,97},{2,98},{3,99},{4,100},{5,101},{6,102},{7,103},{8,104... | collective-permute-start | bytes 786440 | tf_op jit(solution)/shard_map/ppermute | solution.py:46
  64.2 63.5 %collective-permute-start.16 = (bf16[256,4096]{1,0:T(8,128)(2,1)}, bf16[256,4096]{1,0:T(8,128)(2,1)S(1)}, u32[]{:S(2)}, u32[]{:S(2)}) collective-permute-start(bf16[256,4096]{1,0:T(8,128)(2,1)} %pad_maximum_fusion), channel_id=1, source_target_pairs={{0,66},{1,67},{2,64},{3,65},{4,70},{5,71},{6,68},{7,69},{8,74},{9,... | collective-permute-start | bytes 6291464 | tf_op jit(solution)/shard_map/ppermute | solution.py:46
  81.6 25.8 %collective-permute-start.30 = (bf16[128,4096]{1,0:T(8,128)(2,1)}, bf16[128,4096]{1,0:T(8,128)(2,1)}, u32[]{:S(2)}, u32[]{:S(2)}) collective-permute-start(bf16[128,4096]{1,0:T(8,128)(2,1)} %get-tuple-element.39.refs_0_), channel_id=1, source_target_pairs={{0,4},{1,5},{2,6},{3,7},{4,8},{5,9},{6,10},{7,11},{8,12},{9,13},{1... | collective-permute-start | bytes 3145736 | tf_op jit(solution)/shard_map/ppermute | solution.py:46
  83.7 12.8 %collective-permute-start.19 = (bf16[64,4096]{1,0:T(8,128)(2,1)S(1)}, bf16[64,4096]{1,0:T(8,128)(2,1)S(1)}, u32[]{:S(2)}, u32[]{:S(2)}) collective-permute-start(bf16[64,4096]{1,0:T(8,128)(2,1)S(1)} %get-tuple-element.59), channel_id=1, source_target_pairs={{0,16},{1,17},{2,18},{3,19},{4,20},{5,21},{6,22},{7,23},{8,24},{9,... | collective-permute-start | bytes 1572872 | tf_op jit(solution)/shard_map/ppermute | solution.py:46
  84.2 12.4 %copy-start.11 = (bf16[128,4096]{1,0:T(8,128)(2,1)S(1)}, bf16[128,4096]{1,0:T(8,128)(2,1)}, u32[]{:S(2)}) copy-start(bf16[128,4096]{1,0:T(8,128)(2,1)} %get-tuple-element.39.refs_0_) | copy-start | bytes 3145732
  84.6 70.9 %collective-permute-start.17 = (bf16[256,4096]{1,0:T(8,128)(2,1)S(1)}, bf16[256,4096]{1,0:T(8,128)(2,1)}, u32[]{:S(2)}, u32[]{:S(2)}) collective-permute-start(bf16[256,4096]{1,0:T(8,128)(2,1)S(1)} %pad_maximum_fusion.1), channel_id=1, source_target_pairs={{0,66},{1,67},{2,64},{3,65},{4,70},{5,71},{6,68},{7,69},{8,74},{9,... | collective-permute-start | bytes 6291464 | tf_op jit(solution)/shard_map/ppermute | solution.py:46
  87.4 11.6 %collective-permute-start.20 = (bf16[64,4096]{1,0:T(8,128)(2,1)S(1)}, bf16[64,4096]{1,0:T(8,128)(2,1)S(1)}, u32[]{:S(2)}, u32[]{:S(2)}) collective-permute-start(bf16[64,4096]{1,0:T(8,128)(2,1)S(1)} %get-tuple-element.59), channel_id=1, source_target_pairs={{0,48},{1,49},{2,50},{3,51},{4,52},{5,53},{6,54},{7,55},{8,56},{9,... | collective-permute-start | bytes 1572872 | tf_op jit(solution)/shard_map/ppermute | solution.py:46
  96.6 13.4 %copy-start.5 = (bf16[64,4096]{1,0:T(8,128)(2,1)}, bf16[64,4096]{1,0:T(8,128)(2,1)S(1)}, u32[]{:S(2)}) copy-start(bf16[64,4096]{1,0:T(8,128)(2,1)S(1)} %collective-permute-done.19.refs_6_.refs_8_) | copy-start | bytes 1572868
  96.6 22.2 %collective-permute-start.31 = (bf16[128,4096]{1,0:T(8,128)(2,1)S(1)}, bf16[128,4096]{1,0:T(8,128)(2,1)}, u32[]{:S(2)}, u32[]{:S(2)}) collective-permute-start(bf16[128,4096]{1,0:T(8,128)(2,1)S(1)} %copy-done.11), channel_id=1, source_target_pairs={{0,12},{1,13},{2,14},{3,15},{4,0},{5,1},{6,2},{7,3},{8,4},{9,5},{1... | collective-permute-start | bytes 3145736 | tf_op jit(solution)/shard_map/ppermute | solution.py:46
  99.0 11.0 %copy-start.6 = (bf16[64,4096]{1,0:T(8,128)(2,1)}, bf16[64,4096]{1,0:T(8,128)(2,1)S(1)}, u32[]{:S(2)}) copy-start(bf16[64,4096]{1,0:T(8,128)(2,1)S(1)} %collective-permute-done.20.refs_7_.refs_9_) | copy-start | bytes 1572868
  99.0 19.8 %collective-permute-start.18 = (bf16[64,4096]{1,0:T(8,128)(2,1)S(1)}, bf16[64,4096]{1,0:T(8,128)(2,1)S(1)}, u32[]{:S(2)}, u32[]{:S(2)}) collective-permute-start(bf16[64,4096]{1,0:T(8,128)(2,1)S(1)} %get-tuple-element.60), channel_id=1, source_target_pairs={{0,64},{1,65},{2,66},{3,67},{4,68},{5,69},{6,70},{7,71},{8,72},{9,... | collective-permute-start | bytes 1572872 | tf_op jit(solution)/shard_map/ppermute | solution.py:46
  107.4 14.4 %collective-permute-start.23 = (bf16[32,4096]{1,0:T(8,128)(2,1)S(1)}, bf16[32,4096]{1,0:T(8,128)(2,1)S(1)}, u32[]{:S(2)}, u32[]{:S(2)}) collective-permute-start(bf16[32,4096]{1,0:T(8,128)(2,1)S(1)} %slice.56), channel_id=1, source_target_pairs={{0,16},{1,17},{2,18},{3,19},{4,20},{5,21},{6,22},{7,23},{8,24},{9,... | collective-permute-start | bytes 786440 | tf_op jit(solution)/shard_map/ppermute | solution.py:46
  118.8 8.3 %collective-permute-start.24 = (bf16[32,4096]{1,0:T(8,128)(2,1)S(1)}, bf16[32,4096]{1,0:T(8,128)(2,1)S(1)}, u32[]{:S(2)}, u32[]{:S(2)}) collective-permute-start(bf16[32,4096]{1,0:T(8,128)(2,1)S(1)} %slice.57), channel_id=1, source_target_pairs={{0,48},{1,49},{2,50},{3,51},{4,52},{5,53},{6,54},{7,55},{8,56},{9,... | collective-permute-start | bytes 786440 | tf_op jit(solution)/shard_map/ppermute | solution.py:46
  118.8 8.3 %copy-start.7 = (bf16[64,4096]{1,0:T(8,128)(2,1)}, bf16[64,4096]{1,0:T(8,128)(2,1)S(1)}, u32[]{:S(2)}) copy-start(bf16[64,4096]{1,0:T(8,128)(2,1)S(1)} %collective-permute-done.18.refs_5_.refs_7_) | copy-start | bytes 1572868
  118.8 40.8 %collective-permute-start.35 = (bf16[64,4096]{1,0:T(8,128)(2,1)S(1)}, bf16[64,4096]{1,0:T(8,128)(2,1)S(1)}, u32[]{:S(2)}, u32[]{:S(2)}) collective-permute-start(bf16[64,4096]{1,0:T(8,128)(2,1)S(1)} %slice.60), channel_id=1, source_target_pairs={{0,4},{1,5},{2,6},{3,7},{4,8},{5,9},{6,10},{7,11},{8,12},{9,13},{1... | collective-permute-start | bytes 1572872 | tf_op jit(solution)/shard_map/ppermute | solution.py:46
  121.8 65.9 %copy-start.9 = (bf16[32,4096]{1,0:T(8,128)(2,1)}, bf16[32,4096]{1,0:T(8,128)(2,1)S(1)}, u32[]{:S(2)}) copy-start(bf16[32,4096]{1,0:T(8,128)(2,1)S(1)} %collective-permute-done.23.refs_10_.refs_12_) | copy-start | bytes 786436
  121.8 48.1 %collective-permute-start.21 = (bf16[128,4096]{1,0:T(8,128)(2,1)S(1)}, bf16[128,4096]{1,0:T(8,128)(2,1)S(1)}, u32[]{:S(2)}, u32[]{:S(2)}) collective-permute-start(bf16[128,4096]{1,0:T(8,128)(2,1)S(1)} %pad_maximum_fusion.4), channel_id=1, source_target_pairs={{0,16},{1,17},{2,18},{3,19},{4,20},{5,21},{6,22},{7,23},{8,24},{9,... | collective-permute-start | bytes 3145736 | tf_op jit(solution)/shard_map/ppermute | solution.py:46
  127.0 43.3 %collective-permute-start.22 = (bf16[128,4096]{1,0:T(8,128)(2,1)S(1)}, bf16[128,4096]{1,0:T(8,128)(2,1)S(1)}, u32[]{:S(2)}, u32[]{:S(2)}) collective-permute-start(bf16[128,4096]{1,0:T(8,128)(2,1)S(1)} %pad_maximum_fusion.4), channel_id=1, source_target_pairs={{0,48},{1,49},{2,50},{3,51},{4,52},{5,53},{6,54},{7,55},{8,56},{9,... | collective-permute-start | bytes 3145736 | tf_op jit(solution)/shard_map/ppermute | solution.py:46
  127.7 60.0 %copy-start = (bf16[256,4096]{1,0:T(8,128)(2,1)}, bf16[256,4096]{1,0:T(8,128)(2,1)S(1)}, u32[]{:S(2)}) copy-start(bf16[256,4096]{1,0:T(8,128)(2,1)S(1)} %collective-permute-done.16.refs_3_.refs_5_) | copy-start | bytes 6291460
  127.7 60.0 %collective-permute-start.25 = (bf16[192,4096]{1,0:T(8,128)(2,1)}, bf16[192,4096]{1,0:T(8,128)(2,1)S(1)}, u32[]{:S(2)}, u32[]{:S(2)}) collective-permute-start(bf16[192,4096]{1,0:T(8,128)(2,1)} %pad_maximum_fusion.2), channel_id=1, source_target_pairs={{0,64},{1,65},{2,66},{3,67},{4,68},{5,69},{6,70},{7,71},{8,72},{9,... | collective-permute-start | bytes 4718600 | tf_op jit(solution)/shard_map/ppermute | solution.py:46
  155.5 11.8 %collective-permute-start.36 = (bf16[64,4096]{1,0:T(8,128)(2,1)S(1)}, bf16[64,4096]{1,0:T(8,128)(2,1)S(1)}, u32[]{:S(2)}, u32[]{:S(2)}) collective-permute-start(bf16[64,4096]{1,0:T(8,128)(2,1)S(1)} %slice.61), channel_id=1, source_target_pairs={{0,12},{1,13},{2,14},{3,15},{4,0},{5,1},{6,2},{7,3},{8,4},{9,5},{1... | collective-permute-start | bytes 1572872 | tf_op jit(solution)/shard_map/ppermute | solution.py:46
  159.6 13.2 %copy-start.15 = (bf16[64,4096]{1,0:T(8,128)(2,1)}, bf16[64,4096]{1,0:T(8,128)(2,1)S(1)}, u32[]{:S(2)}) copy-start(bf16[64,4096]{1,0:T(8,128)(2,1)S(1)} %collective-permute-done.35.refs_0_) | copy-start | bytes 1572868
  159.6 10.3 %collective-permute-start.28 = (bf16[64,4096]{1,0:T(8,128)(2,1)S(1)}, bf16[64,4096]{1,0:T(8,128)(2,1)S(1)}, u32[]{:S(2)}, u32[]{:S(2)}) collective-permute-start(bf16[64,4096]{1,0:T(8,128)(2,1)S(1)} %pad_maximum_fusion.5), channel_id=1, source_target_pairs={{0,64},{1,65},{2,66},{3,67},{4,68},{5,69},{6,70},{7,71},{8,72},{9,... | collective-permute-start | bytes 1572872 | tf_op jit(solution)/shard_map/ppermute | solution.py:46
  167.3 5.5 %collective-permute-start.37 = (bf16[64,4096]{1,0:T(8,128)(2,1)S(1)}, bf16[64,4096]{1,0:T(8,128)(2,1)S(1)}, u32[]{:S(2)}, u32[]{:S(2)}) collective-permute-start(bf16[64,4096]{1,0:T(8,128)(2,1)S(1)} %collective-permute-done.35.refs_0_), channel_id=1, source_target_pairs={{0,1},{1,0},{2,3},{3,2},{4,5},{5,4},{6,7},{7,6},{8,9},{9,8},{10,11... | collective-permute-start | bytes 1572872 | tf_op jit(solution)/shard_map/ppermute | solution.py:46
  169.9 4.8 %collective-permute-start.38 = (bf16[64,4096]{1,0:T(8,128)(2,1)S(1)}, bf16[64,4096]{1,0:T(8,128)(2,1)S(1)}, u32[]{:S(2)}, u32[]{:S(2)}) collective-permute-start(bf16[64,4096]{1,0:T(8,128)(2,1)S(1)} %collective-permute-done.36.refs_1_), channel_id=1, source_target_pairs={{0,1},{1,0},{2,3},{3,2},{4,5},{5,4},{6,7},{7,6},{8,9},{9,8},{10,11... | collective-permute-start | bytes 1572872 | tf_op jit(solution)/shard_map/ppermute | solution.py:46
  169.9 30.6 %collective-permute-start.32 = (bf16[128,4096]{1,0:T(8,128)(2,1)}, bf16[128,4096]{1,0:T(8,128)(2,1)}, u32[]{:S(2)}, u32[]{:S(2)}) collective-permute-start(bf16[128,4096]{1,0:T(8,128)(2,1)} %collective-permute-done.30.refs_0_), channel_id=1, source_target_pairs={{0,1},{1,0},{2,3},{3,2},{4,5},{5,4},{6,7},{7,6},{8,9},{9,8},{10,11... | collective-permute-start | bytes 3145736 | tf_op jit(solution)/shard_map/ppermute | solution.py:46
  170.6 29.8 %collective-permute-start.33 = (bf16[128,4096]{1,0:T(8,128)(2,1)}, bf16[128,4096]{1,0:T(8,128)(2,1)}, u32[]{:S(2)}, u32[]{:S(2)}) collective-permute-start(bf16[128,4096]{1,0:T(8,128)(2,1)} %collective-permute-done.31.refs_1_), channel_id=1, source_target_pairs={{0,1},{1,0},{2,3},{3,2},{4,5},{5,4},{6,7},{7,6},{8,9},{9,8},{10,11... | collective-permute-start | bytes 3145736 | tf_op jit(solution)/shard_map/ppermute | solution.py:46
  172.8 16.5 %collective-permute-start.26 = (bf16[64,4096]{1,0:T(8,128)(2,1)}, bf16[64,4096]{1,0:T(8,128)(2,1)}, u32[]{:S(2)}, u32[]{:S(2)}) collective-permute-start(bf16[64,4096]{1,0:T(8,128)(2,1)} %slice.58), channel_id=1, source_target_pairs={{0,16},{1,17},{2,18},{3,19},{4,20},{5,21},{6,22},{7,23},{8,24},{9,... | collective-permute-start | bytes 1572872 | tf_op jit(solution)/shard_map/ppermute | solution.py:46
  175.5 14.6 %collective-permute-start.27 = (bf16[64,4096]{1,0:T(8,128)(2,1)}, bf16[64,4096]{1,0:T(8,128)(2,1)}, u32[]{:S(2)}, u32[]{:S(2)}) collective-permute-start(bf16[64,4096]{1,0:T(8,128)(2,1)} %slice.59), channel_id=1, source_target_pairs={{0,48},{1,49},{2,50},{3,51},{4,52},{5,53},{6,54},{7,55},{8,56},{9,... | collective-permute-start | bytes 1572872 | tf_op jit(solution)/shard_map/ppermute | solution.py:46
  187.7 46.8 %collective-permute-start.14 = (bf16[128,4096]{1,0:T(8,128)(2,1)}, bf16[128,4096]{1,0:T(8,128)(2,1)S(1)}, u32[]{:S(2)}, u32[]{:S(2)}) collective-permute-start(bf16[128,4096]{1,0:T(8,128)(2,1)} %get-tuple-element.39.refs_0_), channel_id=1, source_target_pairs={{0,1},{1,0},{2,3},{3,2},{4,5},{5,4},{6,7},{7,6},{8,9},{9,8},{10,11... | collective-permute-start | bytes 3145736 | tf_op jit(solution)/shard_map/ppermute | solution.py:46
  200.4 29.0 %collective-permute-start.39 = (bf16[128,4096]{1,0:T(8,128)(2,1)}, bf16[128,4096]{1,0:T(8,128)(2,1)}, u32[]{:S(2)}, u32[]{:S(2)}) collective-permute-start(bf16[128,4096]{1,0:T(8,128)(2,1)} %get-tuple-element.46), channel_id=1, source_target_pairs={{0,1},{1,0},{2,3},{3,2},{4,5},{5,4},{6,7},{7,6},{8,9},{9,8},{10,11... | collective-permute-start | bytes 3145736 | tf_op jit(solution)/shard_map/ppermute | solution.py:46
  214.4 14.9 %copy-start.23 = (bf16[128,4096]{1,0:T(8,128)(2,1)S(1)}, bf16[128,4096]{1,0:T(8,128)(2,1)}, u32[]{:S(2)}) copy-start(bf16[128,4096]{1,0:T(8,128)(2,1)} %get-tuple-element.45) | copy-start | bytes 3145732
  228.8 27.2 %collective-permute-start.42 = (bf16[128,4096]{1,0:T(8,128)(2,1)}, bf16[128,4096]{1,0:T(8,128)(2,1)S(1)}, u32[]{:S(2)}, u32[]{:S(2)}) collective-permute-start(bf16[128,4096]{1,0:T(8,128)(2,1)} %get-tuple-element.48), channel_id=1, source_target_pairs={{0,1},{1,0},{2,3},{3,2},{4,5},{5,4},{6,7},{7,6},{8,9},{9,8},{10,11... | collective-permute-start | bytes 3145736 | tf_op jit(solution)/shard_map/ppermute | solution.py:46
  231.9 24.2 %collective-permute-start.43 = (bf16[64,4096]{1,0:T(8,128)(2,1)}, bf16[64,4096]{1,0:T(8,128)(2,1)S(1)}, u32[]{:S(2)}, u32[]{:S(2)}) collective-permute-start(bf16[64,4096]{1,0:T(8,128)(2,1)} %get-tuple-element.58), channel_id=1, source_target_pairs={{0,12},{1,13},{2,14},{3,15},{4,0},{5,1},{6,2},{7,3},{8,4},{9,5},{1... | collective-permute-start | bytes 1572872 | tf_op jit(solution)/shard_map/ppermute | solution.py:46
  245.2 10.8 %copy-start.22 = (bf16[128,4096]{1,0:T(8,128)(2,1)S(1)}, bf16[128,4096]{1,0:T(8,128)(2,1)}, u32[]{:S(2)}) copy-start(bf16[128,4096]{1,0:T(8,128)(2,1)} %get-tuple-element.47) | copy-start | bytes 3145732
  245.2 14.5 %collective-permute-start.34 = (bf16[128,4096]{1,0:T(8,128)(2,1)}, bf16[128,4096]{1,0:T(8,128)(2,1)S(1)}, u32[]{:S(2)}, u32[]{:S(2)}) collective-permute-start(bf16[128,4096]{1,0:T(8,128)(2,1)} %get-tuple-element.44), channel_id=1, source_target_pairs={{0,1},{1,0},{2,3},{3,2},{4,5},{5,4},{6,7},{7,6},{8,9},{9,8},{10,11... | collective-permute-start | bytes 3145736 | tf_op jit(solution)/shard_map/ppermute | solution.py:46
  255.5 15.9 %copy-start.20 = (bf16[128,4096]{1,0:T(8,128)(2,1)S(1)}, bf16[128,4096]{1,0:T(8,128)(2,1)}, u32[]{:S(2)}) copy-start(bf16[128,4096]{1,0:T(8,128)(2,1)} %get-tuple-element.43) | copy-start | bytes 3145732
  255.5 16.9 %collective-permute-start.29 = (bf16[128,4096]{1,0:T(8,128)(2,1)}, bf16[128,4096]{1,0:T(8,128)(2,1)S(1)}, u32[]{:S(2)}, u32[]{:S(2)}) collective-permute-start(bf16[128,4096]{1,0:T(8,128)(2,1)} %get-tuple-element.42), channel_id=1, source_target_pairs={{0,1},{1,0},{2,3},{3,2},{4,5},{5,4},{6,7},{7,6},{8,9},{9,8},{10,11... | collective-permute-start | bytes 3145736 | tf_op jit(solution)/shard_map/ppermute | solution.py:46
  256.0 15.3 %collective-permute-start.40 = (bf16[64,4096]{1,0:T(8,128)(2,1)}, bf16[64,4096]{1,0:T(8,128)(2,1)S(1)}, u32[]{:S(2)}, u32[]{:S(2)}) collective-permute-start(bf16[64,4096]{1,0:T(8,128)(2,1)} %get-tuple-element.57), channel_id=1, source_target_pairs={{0,4},{1,5},{2,6},{3,7},{4,8},{5,9},{6,10},{7,11},{8,12},{9,13},{1... | collective-permute-start | bytes 1572872 | tf_op jit(solution)/shard_map/ppermute | solution.py:46
  256.4 40.9 %copy-start.19 = (bf16[128,4096]{1,0:T(8,128)(2,1)S(1)}, bf16[128,4096]{1,0:T(8,128)(2,1)}, u32[]{:S(2)}) copy-start(bf16[128,4096]{1,0:T(8,128)(2,1)} %get-tuple-element.38) | copy-start | bytes 3145732
  256.4 40.9 %copy-start.21 = (bf16[128,4096]{1,0:T(8,128)(2,1)S(1)}, bf16[128,4096]{1,0:T(8,128)(2,1)}, u32[]{:S(2)}) copy-start(bf16[128,4096]{1,0:T(8,128)(2,1)} %get-tuple-element.41) | copy-start | bytes 3145732
  256.4 25.7 %collective-permute-start.44 = (bf16[128,4096]{1,0:T(8,128)(2,1)S(1)}, bf16[128,4096]{1,0:T(8,128)(2,1)S(1)}, u32[]{:S(2)}, u32[]{:S(2)}) collective-permute-start(bf16[128,4096]{1,0:T(8,128)(2,1)S(1)} %add_convert_fusion), channel_id=1, source_target_pairs={{0,12},{1,13},{2,14},{3,15},{4,0},{5,1},{6,2},{7,3},{8,4},{9,5},{1... | collective-permute-start | bytes 3145736 | tf_op jit(solution)/shard_map/ppermute | solution.py:46
  271.7 25.6 %collective-permute-start.41 = (bf16[128,4096]{1,0:T(8,128)(2,1)S(1)}, bf16[128,4096]{1,0:T(8,128)(2,1)S(1)}, u32[]{:S(2)}, u32[]{:S(2)}) collective-permute-start(bf16[128,4096]{1,0:T(8,128)(2,1)S(1)} %add_convert_fusion.1), channel_id=1, source_target_pairs={{0,4},{1,5},{2,6},{3,7},{4,8},{5,9},{6,10},{7,11},{8,12},{9,13},{1... | collective-permute-start | bytes 3145736 | tf_op jit(solution)/shard_map/ppermute | solution.py:46
  (13 other events, 23.2 us)
where the time goes:
time: 301 us; the launch traced here: 299 us
  waiting for transfers between devices  111 us (37%)
  Pallas kernels  96.3 us (32%)
  starting transfers between devices  62.9 us (21%)
  local copies, waits for them, and re-layouts  15.5 us (5%)
  other arithmetic  8.86 us (3%)
  between operations  5.01 us (2%)
    ppermute x45, waiting for transfers between devices, send(): return lax.ppermute(value, AXES, table)  111 us
    pallas_call x6, Pallas kernels, ffn(): pl.pallas_call(functools.partial(ffn_kernel, rows, len(arrays), ups, down...  68.2 us
    ppermute x45, starting transfers between devices, send(): return lax.ppermute(value, AXES, table)  62.9 us
    pallas_call x1, Pallas kernels, prefix_part(): pl.pallas_call(prefix_kernel, grid=(1,), out_shape=[jax.ShapeDtypeStruct(...  14.8 us
    pallas_call x1, Pallas kernels, suffix_part(): pl.pallas_call(suffix_kernel, grid=(steps,), out_shape=[jax.ShapeDtypeStr...  10.3 us
  transfers between devices with their start and end apart: 45, of which 18 were waited for; matrix products, arithmetic and copies ran while one was open for 6% of the time, Pallas kernels for 31%

commit v1 on v0

--- a/solution.py
+++ b/solution.py
@@ -66,130 +66,124 @@
     return pl.CostEstimate(flops=int(flops), bytes_accessed=int(nbytes), transcendentals=0)
 
 
-def cut_kernel(index_ref, cache_ref, *outs):
-    for place, out in enumerate(outs):
-        row = pl.multiple_of(index_ref[place] * 32, 32)
-        out[...] = cache_ref[pl.ds(row, 32), :]
-
-
-def cut_slices(index, cache):
+def cut_kernel(index_ref, cache_ref, up_ref, down_ref, *refs):
+    outs, share, sems = refs[:16], refs[16], refs[17]
+    first = pl.multiple_of(index_ref[8] * 64, 64)
+    moves = []
+    for i, (source, row) in enumerate(((up_ref, 0), (down_ref, 0), (up_ref, 32), (down_ref, 32))):
+        part = pl.ds(pl.multiple_of(first + row, 32), 32)
+        moves.append(pltpu.make_async_copy(source.at[part, :], share.at[pl.ds(i * 32, 32), :], sems.at[i]))
+    for move in moves:
+        move.start()
+    for place in range(8):
+        row = pl.multiple_of(index_ref[place] * 16, 16)
+        outs[place][...] = cache_ref[pl.ds(row, 16), :]
+        outs[8 + place][...] = cache_ref[pl.ds(pl.multiple_of(128 + row, 16), 16), :]
+    for move in moves:
+        move.wait()
+
+
+def cut_slices(index, cache, up, down):
     width = cache.shape[1]
     return pl.pallas_call(
         cut_kernel,
-        out_shape=[jax.ShapeDtypeStruct((32, width), BF16)] * 8,
-        in_specs=[smem(), vmem()],
-        out_specs=[vmem()] * 8,
+        out_shape=[jax.ShapeDtypeStruct((16, width), BF16)] * 16 + [jax.ShapeDtypeStruct((128, width), BF16)],
+        in_specs=[smem(), vmem(), hbm(), hbm()],
+        out_specs=[vmem()] * 17,
+        scratch_shapes=[pltpu.SemaphoreType.DMA((4,))],
         compiler_params=params(),
-        cost_estimate=cost(0, 4 * cache.size),
+        cost_estimate=cost(0, 6 * cache.size),
         name="cut_slices",
-    )(index, cache)
+    )(index, cache, up, down)
+
+
+def direct_kernel(up_ref, down_ref, out_ref, sems):
+    moves = [
+        pltpu.make_async_copy(up_ref.at[pl.ds(512, 256), :], out_ref.at[pl.ds(0, 256), :], sems.at[0]),
+        pltpu.make_async_copy(down_ref.at[pl.ds(512, 256), :], out_ref.at[pl.ds(256, 256), :], sems.at[1]),
+    ]
+    for move in moves:
+        move.start()
+    for move in moves:
+        move.wait()
+
+
+def direct_rows(up, down):
+    width = up.shape[1]
+    return pl.pallas_call(
+        direct_kernel,
+        out_shape=jax.ShapeDtypeStruct((512, width), BF16),
+        in_specs=[hbm(), hbm()],
+        out_specs=vmem(),
+        scratch_shapes=[pltpu.SemaphoreType.DMA((2,))],
+        compiler_params=params(),
+        cost_estimate=cost(0, 4 * 512 * width),
+        name="direct_rows",
+    )(up, down)
 
 
 GROUP = 8
 
 
-def suffix_kernel(slope_ref, proj_ref, context_ref, max_ref, total_ref):
-    step = pl.program_id(0)
-    row = lax.broadcasted_iota(jnp.int32, (128, 128), 0)
-    col = lax.broadcasted_iota(jnp.int32, (128, 128), 1)
-    offset = (col - row).astype(F32)
-    seen = col <= row
-    tops, totals = jnp.zeros((128, 128), F32), jnp.zeros((128, 128), F32)
-    for j in range(GROUP):
-        part = slice(j * 128, (j + 1) * 128)
-        scores = lax.dot_general(
-            proj_ref[0, :, part], proj_ref[1, :, part], (((1,), (1,)), ((), ())), preferred_element_type=F32
-        )
-        scores = scores * (1.0 / math.sqrt(128)) + slope_ref[step * GROUP + j] * offset
-        scores = jnp.where(seen, scores, -jnp.inf)
-        top = jnp.max(scores, axis=1, keepdims=True)
-        weights = jnp.exp(scores - top)
-        total = jnp.sum(weights, axis=1, keepdims=True)
-        context_ref[:, part] = jnp.dot(weights.astype(BF16), proj_ref[2, :, part], preferred_element_type=F32)
-        tops = jnp.where(col == j, top, tops)
-        totals = jnp.where(col == j, total, totals)
-    max_ref[0] = tops
-    total_ref[0] = totals
-
-
-def suffix_part(slopes, proj):
-    width = proj.shape[2]
-    steps = HEADS // GROUP
-    stats = jax.ShapeDtypeStruct((steps, 128, 128), F32)
-    stats_spec = pl.BlockSpec((1, 128, 128), lambda i: (i, 0, 0))
-    return pl.pallas_call(
-        suffix_kernel,
-        grid=(steps,),
-        out_shape=[jax.ShapeDtypeStruct((128, width), F32), stats, stats],
-        in_specs=[smem(), pl.BlockSpec((3, 128, width // steps), lambda i: (0, 0, i))],
-        out_specs=[pl.BlockSpec((128, width // steps), lambda i: (0, i)), stats_spec, stats_spec],
-        compiler_params=params(),
-        cost_estimate=cost(4 * 128 * 128 * width, 5 * 128 * width * 2),
-        name="suffix_part",
-    )(slopes, proj)
-
-
-def prefix_kernel(
-    slope_ref, place_ref, query_ref, context_ref, max_ref, total_ref, residual_ref, gain_ref,
-    s0, s1, s2, s3, s4, s5, s6, s7, state_ref, normed_ref, cached,
-):
-    for place, piece in enumerate((s0, s1, s2, s3, s4, s5, s6, s7)):
-        start = pl.multiple_of(place_ref[place] * 32, 32)
-        cached[pl.ds(start, 32), :] = piece[...]
-    row = lax.broadcasted_iota(jnp.int32, (128, 128), 0)
-    col = lax.broadcasted_iota(jnp.int32, (128, 128), 1)
-    offset = (col - row - 128).astype(F32)
-
-    def heads(i, running):
+def attention_kernel(slope_ref, place_ref, proj_ref, residual_ref, gain_ref, *refs):
+    pieces, (state_ref, normed_ref, keys, values, bias, sums) = refs[:16], refs[16:]
+    for place in range(8):
+        start = pl.multiple_of(place_ref[place] * 16, 16)
+        keys[pl.ds(start, 16), :] = pieces[place][...]
+        values[pl.ds(start, 16), :] = pieces[8 + place][...]
+    row = lax.broadcasted_iota(jnp.int32, (128, 256), 0)
+    col = lax.broadcasted_iota(jnp.int32, (128, 256), 1)
+    bias[...] = jnp.where(col - 128 <= row, (col - 128 - row).astype(F32), -1e30)
+    sums[...] = jnp.zeros((128, 128), F32)
+    ones = jnp.ones((256, 128), BF16)
+
+    @pl.loop(0, HEADS // GROUP)
+    def _(i):
         for j in range(GROUP):
             h = i * GROUP + j
             part = pl.ds(pl.multiple_of(h * 128, 128), 128)
+            key = jnp.concatenate([keys[:, part], proj_ref[1, :, part]], axis=0)
+            value = jnp.concatenate([values[:, part], proj_ref[2, :, part]], axis=0)
+            value = jnp.concatenate([value, ones], axis=1)
             scores = lax.dot_general(
-                query_ref[0, :, part], cached[0:128, part], (((1,), (1,)), ((), ())), preferred_element_type=F32
+                proj_ref[0, :, part], key, (((1,), (1,)), ((), ())), preferred_element_type=F32
             )
-            scores = scores * (1.0 / math.sqrt(128)) + slope_ref[h] * offset
-            top = jnp.max(scores, axis=1, keepdims=True)
-            weights = jnp.exp(scores - top)
-            total = jnp.sum(weights, axis=1, keepdims=True)
-            context = jnp.dot(weights.astype(BF16), cached[128:256, part], preferred_element_type=F32)
-            other, other_total = max_ref[i, :, j : j + 1], total_ref[i, :, j : j + 1]
-            joint = jnp.maximum(top, other)
-            first, second = jnp.exp(top - joint), jnp.exp(other - joint)
-            share = 1.0 / (first * total + second * other_total)
-            merged = (first * share) * context + (second * share) * context_ref[:, part]
-            state = (residual_ref[:, part].astype(F32) + merged).astype(BF16)
+            scores = scores * (1.0 / math.sqrt(128)) + slope_ref[h] * bias[...]
+            top = jnp.max(jnp.maximum(scores[:, :128], scores[:, 128:]), axis=1, keepdims=True)
+            weights = jnp.exp(scores - top).astype(BF16)
+            both = jnp.dot(weights, value, preferred_element_type=F32)
+            state = (residual_ref[:, part].astype(F32) + both[:, :128] / both[:, 128:]).astype(BF16)
             state_ref[:, part] = state
-            running = running + state.astype(F32)
-        return running
-
-    sums = lax.fori_loop(0, HEADS // GROUP, heads, jnp.zeros((128, 128), F32))
+            sums[...] += state.astype(F32)
+
     width = state_ref.shape[1]
-    mean = jnp.sum(sums, axis=1, keepdims=True) * (1.0 / width)
+    mean = jnp.broadcast_to(jnp.sum(sums[...], axis=1, keepdims=True) * (1.0 / width), (128, 128))
     squares = jnp.zeros((128, 128), F32)
     for h in range(HEADS):
         part = slice(h * 128, (h + 1) * 128)
         center = state_ref[:, part].astype(F32) - mean
         squares = squares + center * center
     spread = lax.rsqrt(jnp.sum(squares, axis=1, keepdims=True) * (1.0 / width) + NORM_EPS)
+    spread = jnp.broadcast_to(spread, (128, 128))
     for h in range(HEADS):
         part = slice(h * 128, (h + 1) * 128)
         center = state_ref[:, part].astype(F32) - mean
         normed_ref[:, part] = (center * spread * gain_ref[:, part]).astype(BF16)
 
 
-def prefix_part(slopes, places, query, suffix, residual, gain, pieces):
-    width = query.shape[2]
+def attention(slopes, places, proj, residual, gain, pieces):
+    width = proj.shape[2]
     return pl.pallas_call(
-        prefix_kernel,
-        grid=(1,),
+        attention_kernel,
         out_shape=[jax.ShapeDtypeStruct((128, width), BF16)] * 2,
-        in_specs=[smem(), smem(), pl.BlockSpec((1, 128, width), lambda i: (0, 0, 0))] + [vmem()] * 13,
+        in_specs=[smem(), smem()] + [vmem()] * 19,
         out_specs=[vmem()] * 2,
-        scratch_shapes=[pltpu.VMEM((256, width), BF16)],
+        scratch_shapes=[pltpu.VMEM((128, width), BF16)] * 2
+        + [pltpu.VMEM((128, 256), F32), pltpu.VMEM((128, 128), F32)],
         compiler_params=params(),
-        cost_estimate=cost(4 * 128 * 128 * width, 12 * 128 * width * 2),
-        name="prefix_part",
-    )(slopes, places, query, *suffix, residual, gain.reshape(1, width), *pieces)
+        cost_estimate=cost(8 * 128 * 256 * width, 8 * 128 * width * 2),
+        name="attention",
+    )(slopes, places, proj, residual, gain.reshape(1, width), *pieces)
 
 
 UNIT_TILE = 256
@@ -306,10 +300,6 @@
     return result if len(split) > 1 else result[0]
 
 
-def rows_of(value, start, count):
-    return lax.dynamic_slice_in_dim(value, start, count, 0)
-
-
 def body(residual, suffix_proj, prefix_cache, owner_req, lengths, norm_gain, up, down):
     width = residual.shape[3]
     me = lax.axis_index("req")
@@ -318,28 +308,22 @@
     owner = lax.dynamic_index_in_dim(owner_req, group, 0, keepdims=False)
     slopes = jnp.exp2(-8.0 * jnp.arange(1, HEADS + 1, dtype=F32) / HEADS)
 
-    dests = jnp.stack([((xl + dx) % 2) * 4 + (y + dy) % 4 for dx, dy in OFFSETS]).astype(jnp.int32)
+    other = (1 - xl) * 4 + y
+    dests = [((xl + dx) % 2) * 4 + (y + dy) % 4 for dx, dy in OFFSETS]
     origins = jnp.stack([((xl + dx) % 2) * 4 + (y - dy) % 4 for dx, dy in OFFSETS]).astype(jnp.int32)
-    cuts = cut_slices(dests, prefix_cache.reshape(256, width))
-    kept = cuts[0]
-    for place in range(1, 8):
-        got = send(cuts[place], req_offset(*OFFSETS[place]))
-        kept = jnp.where(origins[place] == owner, got, kept)
-    pieces = [kept] + [send(kept, req_offset(*OFFSETS[place])) for place in range(1, 8)]
-
-    other = (1 - xl) * 4 + y
-    first = other * 64
-    shard_send = jnp.concatenate(
-        [rows_of(up, first, 32), rows_of(down, first, 32), rows_of(up, first + 32, 32), rows_of(down, first + 32, 32)]
-    )
-    shard = send(shard_send, X_CUT)
-    direct_a = send(jnp.concatenate([up[512:640], down[512:640]]), X_CUT)
-    direct_b = send(jnp.concatenate([up[640:768], down[640:768]]), X_CUT)
-
-    suffix = suffix_part(slopes, suffix_proj[0, 0])
-    states, normed = prefix_part(
-        slopes, origins, suffix_proj[0, 0], suffix, residual[0, 0], norm_gain, pieces
-    )
+    cuts = cut_slices(jnp.stack(dests + [other]).astype(jnp.int32), prefix_cache.reshape(256, width), up, down)
+    pieces = []
+    for part in (cuts[:8], cuts[8:16]):
+        kept = part[0]
+        for place in range(1, 8):
+            got = send(part[place], req_offset(*OFFSETS[place]))
+            kept = jnp.where(origins[place] == owner, got, kept)
+        pieces += [kept] + [send(kept, req_offset(*OFFSETS[place])) for place in range(1, 8)]
+
+    shard = send(cuts[16], X_CUT)
+    direct = send(direct_rows(up, down), X_CUT)
+
+    states, normed = attention(slopes, origins, suffix_proj[0, 0], residual[0, 0], norm_gain, pieces)
 
     shard, _ = lax.optimization_barrier((shard, pieces))
     a_own, b_own = shard[:64], shard[64:]
@@ -351,13 +335,13 @@
     b_x = send(jnp.concatenate([b_own, b_m, b_p]), X_LOW)
     a_2u, a_2d = send(a_m[:64], Y_UP), send(a_p[64:], Y_DOWN)
     b_x2 = send(jnp.concatenate([b_2u, b_2d]), X_LOW)
-    far = [shard, direct_a, direct_b, a_x, b_m, b_p, a_m, a_p, b_2u, b_2d, b_x, a_2u, a_2d, b_x2]
+    far = [shard, direct, a_x, b_m, b_p, a_m, a_p, b_2u, b_2d, b_x, a_2u, a_2d, b_x2]
     far_units = [
-        (0, 0, 0, 32, 32), (0, 64, 0, 96, 32), (1, 0, 1, 128, 128), (3, 0, 3, 32, 32),
-        (4, 0, 4, 32, 32), (5, 0, 5, 32, 32), (6, 0, 6, 32, 32), (6, 64, 6, 96, 32),
-        (7, 0, 7, 32, 32), (7, 64, 7, 96, 32), (8, 0, 9, 0, 32),
-        (10, 0, 10, 32, 32), (10, 64, 10, 96, 32), (10, 128, 10, 160, 32),
-        (11, 0, 11, 32, 32), (12, 0, 12, 32, 32), (13, 0, 13, 32, 32), (2, 0, 2, 128, 128),
+        (0, 0, 0, 32, 32), (0, 64, 0, 96, 32), (1, 0, 1, 256, 256), (2, 0, 2, 32, 32),
+        (3, 0, 3, 32, 32), (4, 0, 4, 32, 32), (5, 0, 5, 32, 32), (5, 64, 5, 96, 32),
+        (6, 0, 6, 32, 32), (6, 64, 6, 96, 32), (7, 0, 8, 0, 32),
+        (9, 0, 9, 32, 32), (9, 64, 9, 96, 32), (9, 128, 9, 160, 32),
+        (10, 0, 10, 32, 32), (11, 0, 11, 32, 32), (12, 0, 12, 32, 32),
     ]
     near, near_units = [up, down], [(0, 0, 1, 0, 768)]
 

time: 301 us -> 293 us (0.973)
  starting transfers between devices: 62.9 us -> 81 us
  Pallas kernels: 96.3 us -> 85.9 us
  local copies, waits for them, and re-layouts: 15.5 us -> 8.78 us
  waiting for transfers between devices: 111 us -> 105 us
    ppermute x45 -> x58, starting transfers between devices: 62.9 us -> 81 us  [send(): return lax.ppermute(value, AXES, table)]
    pallas_call x3, Pallas kernels: 28.1 us -> 16.7 us  [the longest x1 7.94 us: attention(): pl.pallas_call(attention_kernel, out_shape=[jax.ShapeDtypeStruct((128, wi...]
    ppermute x45 -> x58, waiting for transfers between devices: 111 us -> 105 us  [send(): return lax.ppermute(value, AXES, table)]
    slice x1 -> x0, local copies, waits for them, and re-layouts: 4.01 us -> none  [body(): direct_b = send(jnp.concatenate([up[640:768], down[640:768]]), X_CUT)]
  transfers between devices with their start and end apart: 45 -> 58, of which waited for: 18 -> 17; matrix products, arithmetic and copies ran while one was open for 6% -> 4% of each run, Pallas kernels for 31% -> 28%
where the time goes in v1:
time: 293 us
  waiting for transfers between devices  105 us (36%)
  Pallas kernels  85.9 us (29%)
  starting transfers between devices  81 us (28%)
  local copies, waits for them, and re-layouts  8.78 us (3%)
  other arithmetic  6.75 us (2%)
  between operations  5.74 us (2%)
    ppermute x58, waiting for transfers between devices, send(): return lax.ppermute(value, AXES, table)  105 us
    ppermute x58, starting transfers between devices, send(): return lax.ppermute(value, AXES, table)  81 us
    pallas_call x6, Pallas kernels, ffn(): pl.pallas_call(functools.partial(ffn_kernel, rows, len(arrays), ups, down...  69.2 us
    pallas_call x1, Pallas kernels, attention(): pl.pallas_call(attention_kernel, out_shape=[jax.ShapeDtypeStruct((128, wi...  7.94 us
  transfers between devices with their start and end apart: 58, of which 17 were waited for; matrix products, arithmetic and copies ran while one was open for 4% of the time, Pallas kernels for 28%

profile of v1, /device:TPU:0, one launch (start us, length us, event | category | flops | bytes accessed | tf_op | source)
XLA Modules:
  0.0 292.8 jit_solution(16479666873563553618)
XLA Ops:
  0.6 4.5 %cut_slices.1 = (bf16[16,4096]{1,0:T(8,128)(2,1)}, bf16[16,4096]{1,0:T(8,128)(2,1)}, bf16[16,4096]{1,0:T(8,128)(2,1)}, bf16[16,4096]{1,0:T(8,128)(2,1)}, bf16[16...) custom-call(s32[9]{0:T(128)} %stack.69.index_ref, ...), custom_call_target="tpu_custom_call" | custom-call | bytes 6291456 | tf_op jit(solution)/shard_map/cut_slices/pallas_call | solution.py:88
  5.1 4.3 %collective-permute-start = (bf16[16,4096]{1,0:T(8,128)(2,1)}, bf16[16,4096]{1,0:T(8,128)(2,1)S(1)}, u32[]{:S(2)}, u32[]{:S(2)}) collective-permute-start(bf16[16,4096]{1,0:T(8,128)(2,1)} %get-tuple-element.33), channel_id=1, source_target_pairs={{0,96},{1,97},{2,98},{3,99},{4,100},{5,101},{6,102},{7,103},{8,104... | collective-permute-start | bytes 393224 | tf_op jit(solution)/shard_map/ppermute | solution.py:46
  9.4 1.0 collective-permute-start.1
  10.4 1.9 collective-permute-start.2
  13.6 3.5 %collective-permute-start.5 = (bf16[16,4096]{1,0:T(8,128)(2,1)}, bf16[16,4096]{1,0:T(8,128)(2,1)S(1)}, u32[]{:S(2)}, u32[]{:S(2)}) collective-permute-start(bf16[16,4096]{1,0:T(8,128)(2,1)} %get-tuple-element.38), channel_id=1, source_target_pairs={{0,48},{1,49},{2,50},{3,51},{4,52},{5,53},{6,54},{7,55},{8,56},{9,... | collective-permute-start | bytes 393224 | tf_op jit(solution)/shard_map/ppermute | solution.py:46
  17.1 1.0 collective-permute-start.6
  23.3 4.3 %collective-permute-start.14 = (bf16[16,4096]{1,0:T(8,128)(2,1)}, bf16[16,4096]{1,0:T(8,128)(2,1)S(1)}, u32[]{:S(2)}, u32[]{:S(2)}) collective-permute-start(bf16[16,4096]{1,0:T(8,128)(2,1)} %get-tuple-element.41), channel_id=1, source_target_pairs={{0,96},{1,97},{2,98},{3,99},{4,100},{5,101},{6,102},{7,103},{8,104... | collective-permute-start | bytes 393224 | tf_op jit(solution)/shard_map/ppermute | solution.py:46
  28.0 2.6 collective-permute-start.16
  31.3 1.0 select_select_fusion.1.refs_0_
  32.5 2.5 collective-permute-start.19
  35.6 1.3 collective-permute-done.16
  36.9 1.0 collective-permute-start.7
  37.9 2.2 collective-permute-start.8
  40.1 2.8 collective-permute-start.29
  42.9 1.0 collective-permute-start.9
  44.4 1.2 collective-permute-start.11
  45.7 2.9 collective-permute-start.12
  48.6 1.0 select_select_fusion.refs_8_
  49.6 2.3 collective-permute-start.13
  52.6 2.5 collective-permute-start.22
  55.1 0.9 collective-permute-start.23
  56.0 1.2 collective-permute-done.13.refs_7_
  57.2 1.1 collective-permute-start.24
  58.3 1.7 collective-permute-done.21.refs_9_
  60.3 3.8 %collective-permute-start.26 = (bf16[16,4096]{1,0:T(8,128)(2,1)S(1)}, bf16[16,4096]{1,0:T(8,128)(2,1)S(1)}, u32[]{:S(2)}, u32[]{:S(2)}) collective-permute-start(bf16[16,4096]{1,0:T(8,128)(2,1)S(1)} %select_select_fusion.refs_8_), channel_id=1, source_target_pairs={{0,112},{1,113},{2,114},{3,115},{4,116},{5,117},{6,118},{7,119},{8... | collective-permute-start | bytes 393224 | tf_op jit(solution)/shard_map/ppermute | solution.py:46
  64.1 1.7 collective-permute-start.27
  65.8 4.3 %direct_rows.1 = bf16[512,4096]{1,0:T(8,128)(2,1)} custom-call(bf16[768,4096]{1,0:T(8,128)(2,1)} %refs_4_.3, bf16[768,4096]{1,0:T(8,128)(2,1)} %refs_5_.3), custom_call_target="tpu_custom_call" | custom-call | bytes 8388608 | tf_op jit(solution)/shard_map/direct_rows/pallas_call | solution.py:113
  71.4 4.1 %collective-permute-start.30 = (bf16[512,4096]{1,0:T(8,128)(2,1)}, bf16[512,4096]{1,0:T(8,128)(2,1)}, u32[]{:S(2)}, u32[]{:S(2)}) collective-permute-start(bf16[512,4096]{1,0:T(8,128)(2,1)} %direct_rows.1), channel_id=1, source_target_pairs={{0,66},{1,67},{2,64},{3,65},{4,70},{5,71},{6,68},{7,69},{8,74},{9,... | collective-permute-start | bytes 12582920 | tf_op jit(solution)/shard_map/ppermute | solution.py:46
  76.2 7.9 %attention.1 = (bf16[128,4096]{1,0:T(8,128)(2,1)}, bf16[128,4096]{1,0:T(8,128)(2,1)}) custom-call(f32[32]{0:T(128)} %multiply_exponential_fusion.slope_ref, s32[8]{0:T(128)} %stack.61.place_ref, bf16[3,128,4096]{2,1,0:T(8,128)(2,1)} %bitcast.24, bf16[128,4096]{1,0:T(8,128)(2,1)} %bitcast.26, f32[1,4096]{1,0:T(1,128)} %bitcast.27, ...), custom_call_target="tpu_custom_call" | custom-call | flops 1073741824 | bytes 8388608 | tf_op jit(solution)/shard_map/attention/pallas_call | solution.py:176
  84.1 1.9 collective-permute-start.43
  86.1 2.2 collective-permute-start.44
  88.4 3.2 %collective-permute-start.33 = (bf16[64,4096]{1,0:T(8,128)(2,1)S(1)}, bf16[64,4096]{1,0:T(8,128)(2,1)S(1)}, u32[]{:S(2)}, u32[]{:S(2)}) collective-permute-start(bf16[64,4096]{1,0:T(8,128)(2,1)S(1)} %get-tuple-element.63), channel_id=1, source_target_pairs={{0,48},{1,49},{2,50},{3,51},{4,52},{5,53},{6,54},{7,55},{8,56},{9,... | collective-permute-start | bytes 1572872 | tf_op jit(solution)/shard_map/ppermute | solution.py:46
  91.6 15.7 %collective-permute-done.43.refs_0_ = bf16[128,4096]{1,0:T(8,128)(2,1)} collective-permute-done((bf16[128,4096]{1,0:T(8,128)(2,1)}, bf16[128,4096]{1,0:T(8,128)(2,1)}, u32[]{:S(2)}, u32[]{:S(2)}) %collective-permute-start.43) | collective-permute-done | bytes 1048608 | tf_op jit(solution)/shard_map/ppermute | solution.py:46
  107.3 1.1 slice.44
  108.9 1.1 slice.45
  110.1 3.3 %collective-permute-start.37 = (bf16[32,4096]{1,0:T(8,128)(2,1)S(1)}, bf16[32,4096]{1,0:T(8,128)(2,1)S(1)}, u32[]{:S(2)}, u32[]{:S(2)}) collective-permute-start(bf16[32,4096]{1,0:T(8,128)(2,1)S(1)} %slice.41), channel_id=1, source_target_pairs={{0,48},{1,49},{2,50},{3,51},{4,52},{5,53},{6,54},{7,55},{8,56},{9,... | collective-permute-start | bytes 786440 | tf_op jit(solution)/shard_map/ppermute | solution.py:46
  113.6 4.1 %collective-permute-done.36.refs_9_.refs_11_ = bf16[32,4096]{1,0:T(8,128)(2,1)S(1)} collective-permute-done((bf16[32,4096]{1,0:T(8,128)(2,1)S(1)}, bf16[32,4096]{1,0:T(8,128)(2,1)S(1)}, u32[]{:S(2)}, u32[]{:S(2)}) %collective-permute-start.36) | collective-permute-done | bytes 262176 | tf_op jit(solution)/shard_map/ppermute | solution.py:46
  117.7 2.9 collective-permute-start.49
  120.5 2.0 collective-permute-start.38
  122.9 4.3 %collective-permute-done.49.refs_1_ = bf16[64,4096]{1,0:T(8,128)(2,1)S(1)} collective-permute-done((bf16[64,4096]{1,0:T(8,128)(2,1)S(1)}, bf16[64,4096]{1,0:T(8,128)(2,1)S(1)}, u32[]{:S(2)}, u32[]{:S(2)}) %collective-permute-start.49) | collective-permute-done | bytes 524320 | tf_op jit(solution)/shard_map/ppermute | solution.py:46
  127.2 1.6 collective-permute-start.35
  128.8 32.6 %collective-permute-done.41.refs_14_.refs_16_ = bf16[64,4096]{1,0:T(8,128)(2,1)S(1)} collective-permute-done((bf16[64,4096]{1,0:T(8,128)(2,1)S(1)}, bf16[64,4096]{1,0:T(8,128)(2,1)S(1)}, u32[]{:S(2)}, u32[]{:S(2)}) %collective-permute-start.41) | collective-permute-done | bytes 524320 | tf_op jit(solution)/shard_map/ppermute | solution.py:46
  161.4 1.9 collective-permute-done.50.refs_2_
  164.0 1.0 slice.42
  165.0 0.8 slice.43
  165.8 1.9 collective-permute-start.39
  167.8 2.1 collective-permute-start.40
  169.9 9.6 %shard_map.86.refs_17_ = f32[256,4096]{1,0:T(8,128)} custom-call(bf16[64,4096]{1,0:T(8,128)(2,1)} %copy-done.11, bf16[64,4096]{1,0:T(8,128)(2,1)} %copy-done.12, bf16[64,4096]{1,0:T(8,128)(2,1)} %copy-done.13, bf16[64,4096]{1,0:T(8,128)(2,1)} %copy-done.14, bf16[768,4096]{1,0:T(8,128)(2,1)} %refs_4_.3, bf16[768,4096]{1,0:T(8,128)(2,1)} %refs_5_.3), custom_call_target="tpu_custom_call" | custom-call | flops 3221225472 | bytes 18874368 | tf_op jit(solution)/shard_map/pallas_call | solution.py:279
  179.6 2.4 collective-permute-done.39.refs_12_.refs_14_
  182.0 1.5 collective-permute-done.40.refs_13_.refs_15_
  183.5 10.6 %shard_map.87 = (bf16[128,4096]{1,0:T(8,128)(2,1)}, bf16[128,4096]{1,0:T(8,128)(2,1)}) custom-call(bf16[64,4096]{1,0:T(8,128)(2,1)} %copy-done.11, bf16[64,4096]{1,0:T(8,128)(2,1)} %copy-done.12, bf16[64,4096]{1,0:T(8,128)(2,1)} %copy-done.13, bf16[64,4096]{1,0:T(8,128)(2,1)} %copy-done.14, bf16[128,4096]{1,0:T(8,128)(2,1)} %copy-done, ...), custom_call_target="tpu_custom_call" | custom-call | flops 3221225472 | bytes 18874368 | tf_op jit(solution)/shard_map/pallas_call | solution.py:279
  194.4 13.8 %shard_map.84.refs_17_ = f32[512,4096]{1,0:T(8,128)} custom-call(bf16[128,4096]{1,0:T(8,128)(2,1)} %collective-permute-done.43.refs_0_, bf16[128,4096]{1,0:T(8,128)(2,1)} %collective-permute-done.44.refs_1_, bf16[128,4096]{1,0:T(8,128)(2,1)} %collective-permute-done.45.refs_2_, bf16[128,4096]{1,0:T(8,128)(2,1)} %collective-permute-done.46.refs_3_, ...), custom_call_target="tpu_custom_call" | custom-call | flops 6442450944 | bytes 25165824 | tf_op jit(solution)/shard_map/pallas_call | solution.py:279
  208.2 14.8 %shard_map.85 = (bf16[128,4096]{1,0:T(8,128)(2,1)}, bf16[128,4096]{1,0:T(8,128)(2,1)}, bf16[128,4096]{1,0:T(8,128)(2,1)}, bf16[128,4096]{1,0:T(8,128)(2,1)}) custom-call(bf16[128,4096]{1,0:T(8,128)(2,1)} %collective-permute-done.43.refs_0_, bf16[128,4096]{1,0:T(8,128)(2,1)} %collective-permute-done.44.refs_1_, ...), custom_call_target="tpu_custom_call" | custom-call | flops 6442450944 | bytes 25165824 | tf_op jit(solution)/shard_map/pallas_call | solution.py:279
  223.6 1.5 add_convert_fusion.2
  225.1 1.0 fusion.1
  226.1 1.5 collective-permute-start.56
  227.6 1.0 copy-done.10
  228.6 9.7 %shard_map.82.refs_15_ = f32[256,4096]{1,0:T(8,128)} custom-call(bf16[128,4096]{1,0:T(8,128)(2,1)} %get-tuple-element.50.refs_0_, bf16[128,4096]{1,0:T(8,128)(2,1)} %copy-done.10, bf16[768,4096]{1,0:T(8,128)(2,1)} %refs_4_.3, bf16[768,4096]{1,0:T(8,128)(2,1)} %refs_5_.3), custom_call_target="tpu_custom_call" | custom-call | flops 3221225472 | bytes 18874368 | tf_op jit(solution)/shard_map/pallas_call | solution.py:279
  238.4 10.7 %shard_map.83 = (bf16[128,4096]{1,0:T(8,128)(2,1)}, bf16[128,4096]{1,0:T(8,128)(2,1)}) custom-call(bf16[128,4096]{1,0:T(8,128)(2,1)} %get-tuple-element.50.refs_0_, bf16[128,4096]{1,0:T(8,128)(2,1)} %copy-done.10, bf16[128,4096]{1,0:T(8,128)(2,1)} %copy-done, bf16[512,4096]{1,0:T(8,128)(2,1)} %collective-permute-done.30.refs_3_.refs_5_, ...), custom_call_target="tpu_custom_call" | custom-call | flops 3221225472 | bytes 18874368 | tf_op jit(solution)/shard_map/pallas_call | solution.py:279
  250.6 2.7 collective-permute-start.57
  253.4 11.7 %collective-permute-done.53 = bf16[64,4096]{1,0:T(8,128)(2,1)S(1)} collective-permute-done((bf16[64,4096]{1,0:T(8,128)(2,1)}, bf16[64,4096]{1,0:T(8,128)(2,1)S(1)}, u32[]{:S(2)}, u32[]{:S(2)}) %collective-permute-start.53) | collective-permute-done | bytes 524320 | tf_op jit(solution)/shard_map/ppermute | solution.py:46
  266.1 9.6 %collective-permute-done.57 = bf16[128,4096]{1,0:T(8,128)(2,1)S(1)} collective-permute-done((bf16[128,4096]{1,0:T(8,128)(2,1)S(1)}, bf16[128,4096]{1,0:T(8,128)(2,1)S(1)}, u32[]{:S(2)}, u32[]{:S(2)}) %collective-permute-start.57) | collective-permute-done | bytes 1048608 | tf_op jit(solution)/shard_map/ppermute | solution.py:46
  275.7 15.2 %collective-permute-done.54 = bf16[128,4096]{1,0:T(8,128)(2,1)S(1)} collective-permute-done((bf16[128,4096]{1,0:T(8,128)(2,1)S(1)}, bf16[128,4096]{1,0:T(8,128)(2,1)S(1)}, u32[]{:S(2)}, u32[]{:S(2)}) %collective-permute-start.54) | collective-permute-done | bytes 1048608 | tf_op jit(solution)/shard_map/ppermute | solution.py:46
  290.9 1.9 fusion
  (157 shorter events, 12.9 us)
Async XLA Ops:
  5.1 8.5 %collective-permute-start = (bf16[16,4096]{1,0:T(8,128)(2,1)}, bf16[16,4096]{1,0:T(8,128)(2,1)S(1)}, u32[]{:S(2)}, u32[]{:S(2)}) collective-permute-start(bf16[16,4096]{1,0:T(8,128)(2,1)} %get-tuple-element.33), channel_id=1, source_target_pairs={{0,96},{1,97},{2,98},{3,99},{4,100},{5,101},{6,102},{7,103},{8,104... | collective-permute-start | bytes 393224 | tf_op jit(solution)/shard_map/ppermute | solution.py:46
  9.4 7.8 %collective-permute-start.1 = (bf16[16,4096]{1,0:T(8,128)(2,1)}, bf16[16,4096]{1,0:T(8,128)(2,1)S(1)}, u32[]{:S(2)}, u32[]{:S(2)}) collective-permute-start(bf16[16,4096]{1,0:T(8,128)(2,1)} %get-tuple-element.34), channel_id=1, source_target_pairs={{0,112},{1,113},{2,114},{3,115},{4,116},{5,117},{6,118},{7,119},{8... | collective-permute-start | bytes 393224 | tf_op jit(solution)/shard_map/ppermute | solution.py:46
  10.4 12.9 %collective-permute-start.2 = (bf16[16,4096]{1,0:T(8,128)(2,1)}, bf16[16,4096]{1,0:T(8,128)(2,1)S(1)}, u32[]{:S(2)}, u32[]{:S(2)}) collective-permute-start(bf16[16,4096]{1,0:T(8,128)(2,1)} %get-tuple-element.35), channel_id=1, source_target_pairs={{0,80},{1,81},{2,82},{3,83},{4,84},{5,85},{6,86},{7,87},{8,88},{9,... | collective-permute-start | bytes 393224 | tf_op jit(solution)/shard_map/ppermute | solution.py:46
  12.3 15.3 %collective-permute-start.3 = (bf16[16,4096]{1,0:T(8,128)(2,1)}, bf16[16,4096]{1,0:T(8,128)(2,1)S(1)}, u32[]{:S(2)}, u32[]{:S(2)}) collective-permute-start(bf16[16,4096]{1,0:T(8,128)(2,1)} %get-tuple-element.36), channel_id=1, source_target_pairs={{0,64},{1,65},{2,66},{3,67},{4,68},{5,69},{6,70},{7,71},{8,72},{9,... | collective-permute-start | bytes 393224 | tf_op jit(solution)/shard_map/ppermute | solution.py:46
  12.8 15.1 %collective-permute-start.4 = (bf16[16,4096]{1,0:T(8,128)(2,1)}, bf16[16,4096]{1,0:T(8,128)(2,1)S(1)}, u32[]{:S(2)}, u32[]{:S(2)}) collective-permute-start(bf16[16,4096]{1,0:T(8,128)(2,1)} %get-tuple-element.37), channel_id=1, source_target_pairs={{0,32},{1,33},{2,34},{3,35},{4,36},{5,37},{6,38},{7,39},{8,40},{9,... | collective-permute-start | bytes 393224 | tf_op jit(solution)/shard_map/ppermute | solution.py:46
  13.6 17.0 %collective-permute-start.5 = (bf16[16,4096]{1,0:T(8,128)(2,1)}, bf16[16,4096]{1,0:T(8,128)(2,1)S(1)}, u32[]{:S(2)}, u32[]{:S(2)}) collective-permute-start(bf16[16,4096]{1,0:T(8,128)(2,1)} %get-tuple-element.38), channel_id=1, source_target_pairs={{0,48},{1,49},{2,50},{3,51},{4,52},{5,53},{6,54},{7,55},{8,56},{9,... | collective-permute-start | bytes 393224 | tf_op jit(solution)/shard_map/ppermute | solution.py:46
  17.1 14.0 %collective-permute-start.6 = (bf16[16,4096]{1,0:T(8,128)(2,1)}, bf16[16,4096]{1,0:T(8,128)(2,1)S(1)}, u32[]{:S(2)}, u32[]{:S(2)}) collective-permute-start(bf16[16,4096]{1,0:T(8,128)(2,1)} %get-tuple-element.39), channel_id=1, source_target_pairs={{0,16},{1,17},{2,18},{3,19},{4,20},{5,21},{6,22},{7,23},{8,24},{9,... | collective-permute-start | bytes 393224 | tf_op jit(solution)/shard_map/ppermute | solution.py:46
  23.3 9.2 %collective-permute-start.14 = (bf16[16,4096]{1,0:T(8,128)(2,1)}, bf16[16,4096]{1,0:T(8,128)(2,1)S(1)}, u32[]{:S(2)}, u32[]{:S(2)}) collective-permute-start(bf16[16,4096]{1,0:T(8,128)(2,1)} %get-tuple-element.41), channel_id=1, source_target_pairs={{0,96},{1,97},{2,98},{3,99},{4,100},{5,101},{6,102},{7,103},{8,104... | collective-permute-start | bytes 393224 | tf_op jit(solution)/shard_map/ppermute | solution.py:46
  27.6 7.5 %collective-permute-start.15 = (bf16[16,4096]{1,0:T(8,128)(2,1)}, bf16[16,4096]{1,0:T(8,128)(2,1)S(1)}, u32[]{:S(2)}, u32[]{:S(2)}) collective-permute-start(bf16[16,4096]{1,0:T(8,128)(2,1)} %get-tuple-element.42), channel_id=1, source_target_pairs={{0,112},{1,113},{2,114},{3,115},{4,116},{5,117},{6,118},{7,119},{8... | collective-permute-start | bytes 393224 | tf_op jit(solution)/shard_map/ppermute | solution.py:46
  28.0 8.9 %collective-permute-start.16 = (bf16[16,4096]{1,0:T(8,128)(2,1)}, bf16[16,4096]{1,0:T(8,128)(2,1)S(1)}, u32[]{:S(2)}, u32[]{:S(2)}) collective-permute-start(bf16[16,4096]{1,0:T(8,128)(2,1)} %get-tuple-element.43), channel_id=1, source_target_pairs={{0,80},{1,81},{2,82},{3,83},{4,84},{5,85},{6,86},{7,87},{8,88},{9,... | collective-permute-start | bytes 393224 | tf_op jit(solution)/shard_map/ppermute | solution.py:46
  30.6 7.3 %collective-permute-start.17 = (bf16[16,4096]{1,0:T(8,128)(2,1)}, bf16[16,4096]{1,0:T(8,128)(2,1)S(1)}, u32[]{:S(2)}, u32[]{:S(2)}) collective-permute-start(bf16[16,4096]{1,0:T(8,128)(2,1)} %get-tuple-element.44), channel_id=1, source_target_pairs={{0,64},{1,65},{2,66},{3,67},{4,68},{5,69},{6,70},{7,71},{8,72},{9,... | collective-permute-start | bytes 393224 | tf_op jit(solution)/shard_map/ppermute | solution.py:46
  31.2 8.9 %collective-permute-start.18 = (bf16[16,4096]{1,0:T(8,128)(2,1)}, bf16[16,4096]{1,0:T(8,128)(2,1)S(1)}, u32[]{:S(2)}, u32[]{:S(2)}) collective-permute-start(bf16[16,4096]{1,0:T(8,128)(2,1)} %get-tuple-element.45), channel_id=1, source_target_pairs={{0,32},{1,33},{2,34},{3,35},{4,36},{5,37},{6,38},{7,39},{8,40},{9,... | collective-permute-start | bytes 393224 | tf_op jit(solution)/shard_map/ppermute | solution.py:46
  32.5 10.4 %collective-permute-start.19 = (bf16[16,4096]{1,0:T(8,128)(2,1)}, bf16[16,4096]{1,0:T(8,128)(2,1)S(1)}, u32[]{:S(2)}, u32[]{:S(2)}) collective-permute-start(bf16[16,4096]{1,0:T(8,128)(2,1)} %get-tuple-element.46), channel_id=1, source_target_pairs={{0,48},{1,49},{2,50},{3,51},{4,52},{5,53},{6,54},{7,55},{8,56},{9,... | collective-permute-start | bytes 393224 | tf_op jit(solution)/shard_map/ppermute | solution.py:46
  35.1 8.7 %collective-permute-start.20 = (bf16[16,4096]{1,0:T(8,128)(2,1)}, bf16[16,4096]{1,0:T(8,128)(2,1)S(1)}, u32[]{:S(2)}, u32[]{:S(2)}) collective-permute-start(bf16[16,4096]{1,0:T(8,128)(2,1)} %get-tuple-element.47), channel_id=1, source_target_pairs={{0,16},{1,17},{2,18},{3,19},{4,20},{5,21},{6,22},{7,23},{8,24},{9,... | collective-permute-start | bytes 393224 | tf_op jit(solution)/shard_map/ppermute | solution.py:46
  36.9 7.6 %collective-permute-start.7 = (bf16[16,4096]{1,0:T(8,128)(2,1)S(1)}, bf16[16,4096]{1,0:T(8,128)(2,1)S(1)}, u32[]{:S(2)}, u32[]{:S(2)}) collective-permute-start(bf16[16,4096]{1,0:T(8,128)(2,1)S(1)} %select_select_fusion.1.refs_0_), channel_id=1, source_target_pairs={{0,16},{1,17},{2,18},{3,19},{4,20},{5,21},{6,22},{7,23},{8,24},{9,... | collective-permute-start | bytes 393224 | tf_op jit(solution)/shard_map/ppermute | solution.py:46
  37.9 7.8 %collective-permute-start.8 = (bf16[16,4096]{1,0:T(8,128)(2,1)S(1)}, bf16[16,4096]{1,0:T(8,128)(2,1)S(1)}, u32[]{:S(2)}, u32[]{:S(2)}) collective-permute-start(bf16[16,4096]{1,0:T(8,128)(2,1)S(1)} %select_select_fusion.1.refs_0_), channel_id=1, source_target_pairs={{0,48},{1,49},{2,50},{3,51},{4,52},{5,53},{6,54},{7,55},{8,56},{9,... | collective-permute-start | bytes 393224 | tf_op jit(solution)/shard_map/ppermute | solution.py:46
  40.1 48.1 %collective-permute-start.29 = (bf16[128,4096]{1,0:T(8,128)(2,1)}, bf16[128,4096]{1,0:T(8,128)(2,1)S(1)}, u32[]{:S(2)}, u32[]{:S(2)}) collective-permute-start(bf16[128,4096]{1,0:T(8,128)(2,1)} %get-tuple-element.51), channel_id=1, source_target_pairs={{0,66},{1,67},{2,64},{3,65},{4,70},{5,71},{6,68},{7,69},{8,74},{9,... | collective-permute-start | bytes 3145736 | tf_op jit(solution)/shard_map/ppermute | solution.py:46
  42.9 6.7 %collective-permute-start.9 = (bf16[16,4096]{1,0:T(8,128)(2,1)S(1)}, bf16[16,4096]{1,0:T(8,128)(2,1)S(1)}, u32[]{:S(2)}, u32[]{:S(2)}) collective-permute-start(bf16[16,4096]{1,0:T(8,128)(2,1)S(1)} %select_select_fusion.1.refs_0_), channel_id=1, source_target_pairs={{0,32},{1,33},{2,34},{3,35},{4,36},{5,37},{6,38},{7,39},{8,40},{9,... | collective-permute-start | bytes 393224 | tf_op jit(solution)/shard_map/ppermute | solution.py:46
  43.8 8.0 %collective-permute-start.10 = (bf16[16,4096]{1,0:T(8,128)(2,1)S(1)}, bf16[16,4096]{1,0:T(8,128)(2,1)S(1)}, u32[]{:S(2)}, u32[]{:S(2)}) collective-permute-start(bf16[16,4096]{1,0:T(8,128)(2,1)S(1)} %select_select_fusion.1.refs_0_), channel_id=1, source_target_pairs={{0,64},{1,65},{2,66},{3,67},{4,68},{5,69},{6,70},{7,71},{8,72},{9,... | collective-permute-start | bytes 393224 | tf_op jit(solution)/shard_map/ppermute | solution.py:46
  44.4 8.2 %collective-permute-start.11 = (bf16[16,4096]{1,0:T(8,128)(2,1)S(1)}, bf16[16,4096]{1,0:T(8,128)(2,1)S(1)}, u32[]{:S(2)}, u32[]{:S(2)}) collective-permute-start(bf16[16,4096]{1,0:T(8,128)(2,1)S(1)} %select_select_fusion.1.refs_0_), channel_id=1, source_target_pairs={{0,80},{1,81},{2,82},{3,83},{4,84},{5,85},{6,86},{7,87},{8,88},{9,... | collective-permute-start | bytes 393224 | tf_op jit(solution)/shard_map/ppermute | solution.py:46
  45.7 9.5 %collective-permute-start.12 = (bf16[16,4096]{1,0:T(8,128)(2,1)S(1)}, bf16[16,4096]{1,0:T(8,128)(2,1)S(1)}, u32[]{:S(2)}, u32[]{:S(2)}) collective-permute-start(bf16[16,4096]{1,0:T(8,128)(2,1)S(1)} %select_select_fusion.1.refs_0_), channel_id=1, source_target_pairs={{0,112},{1,113},{2,114},{3,115},{4,116},{5,117},{6,118},{7,119},{8... | collective-permute-start | bytes 393224 | tf_op jit(solution)/shard_map/ppermute | solution.py:46
  49.6 7.6 %collective-permute-start.13 = (bf16[16,4096]{1,0:T(8,128)(2,1)S(1)}, bf16[16,4096]{1,0:T(8,128)(2,1)S(1)}, u32[]{:S(2)}, u32[]{:S(2)}) collective-permute-start(bf16[16,4096]{1,0:T(8,128)(2,1)S(1)} %select_select_fusion.1.refs_0_), channel_id=1, source_target_pairs={{0,96},{1,97},{2,98},{3,99},{4,100},{5,101},{6,102},{7,103},{8,104... | collective-permute-start | bytes 393224 | tf_op jit(solution)/shard_map/ppermute | solution.py:46
  51.9 8.1 %collective-permute-start.21 = (bf16[16,4096]{1,0:T(8,128)(2,1)S(1)}, bf16[16,4096]{1,0:T(8,128)(2,1)S(1)}, u32[]{:S(2)}, u32[]{:S(2)}) collective-permute-start(bf16[16,4096]{1,0:T(8,128)(2,1)S(1)} %select_select_fusion.refs_8_), channel_id=1, source_target_pairs={{0,16},{1,17},{2,18},{3,19},{4,20},{5,21},{6,22},{7,23},{8,24},{9,... | collective-permute-start | bytes 393224 | tf_op jit(solution)/shard_map/ppermute | solution.py:46
  52.6 7.7 %collective-permute-start.22 = (bf16[16,4096]{1,0:T(8,128)(2,1)S(1)}, bf16[16,4096]{1,0:T(8,128)(2,1)S(1)}, u32[]{:S(2)}, u32[]{:S(2)}) collective-permute-start(bf16[16,4096]{1,0:T(8,128)(2,1)S(1)} %select_select_fusion.refs_8_), channel_id=1, source_target_pairs={{0,48},{1,49},{2,50},{3,51},{4,52},{5,53},{6,54},{7,55},{8,56},{9,... | collective-permute-start | bytes 393224 | tf_op jit(solution)/shard_map/ppermute | solution.py:46
  55.1 9.0 %collective-permute-start.23 = (bf16[16,4096]{1,0:T(8,128)(2,1)S(1)}, bf16[16,4096]{1,0:T(8,128)(2,1)S(1)}, u32[]{:S(2)}, u32[]{:S(2)}) collective-permute-start(bf16[16,4096]{1,0:T(8,128)(2,1)S(1)} %select_select_fusion.refs_8_), channel_id=1, source_target_pairs={{0,32},{1,33},{2,34},{3,35},{4,36},{5,37},{6,38},{7,39},{8,40},{9,... | collective-permute-start | bytes 393224 | tf_op jit(solution)/shard_map/ppermute | solution.py:46
  57.2 14.2 %collective-permute-start.24 = (bf16[16,4096]{1,0:T(8,128)(2,1)S(1)}, bf16[16,4096]{1,0:T(8,128)(2,1)S(1)}, u32[]{:S(2)}, u32[]{:S(2)}) collective-permute-start(bf16[16,4096]{1,0:T(8,128)(2,1)S(1)} %select_select_fusion.refs_8_), channel_id=1, source_target_pairs={{0,64},{1,65},{2,66},{3,67},{4,68},{5,69},{6,70},{7,71},{8,72},{9,... | collective-permute-start | bytes 393224 | tf_op jit(solution)/shard_map/ppermute | solution.py:46
  59.9 15.5 %collective-permute-start.25 = (bf16[16,4096]{1,0:T(8,128)(2,1)S(1)}, bf16[16,4096]{1,0:T(8,128)(2,1)S(1)}, u32[]{:S(2)}, u32[]{:S(2)}) collective-permute-start(bf16[16,4096]{1,0:T(8,128)(2,1)S(1)} %select_select_fusion.refs_8_), channel_id=1, source_target_pairs={{0,80},{1,81},{2,82},{3,83},{4,84},{5,85},{6,86},{7,87},{8,88},{9,... | collective-permute-start | bytes 393224 | tf_op jit(solution)/shard_map/ppermute | solution.py:46
  60.3 15.1 %collective-permute-start.26 = (bf16[16,4096]{1,0:T(8,128)(2,1)S(1)}, bf16[16,4096]{1,0:T(8,128)(2,1)S(1)}, u32[]{:S(2)}, u32[]{:S(2)}) collective-permute-start(bf16[16,4096]{1,0:T(8,128)(2,1)S(1)} %select_select_fusion.refs_8_), channel_id=1, source_target_pairs={{0,112},{1,113},{2,114},{3,115},{4,116},{5,117},{6,118},{7,119},{8... | collective-permute-start | bytes 393224 | tf_op jit(solution)/shard_map/ppermute | solution.py:46
  64.1 11.4 %collective-permute-start.27 = (bf16[16,4096]{1,0:T(8,128)(2,1)S(1)}, bf16[16,4096]{1,0:T(8,128)(2,1)S(1)}, u32[]{:S(2)}, u32[]{:S(2)}) collective-permute-start(bf16[16,4096]{1,0:T(8,128)(2,1)S(1)} %select_select_fusion.refs_8_), channel_id=1, source_target_pairs={{0,96},{1,97},{2,98},{3,99},{4,100},{5,101},{6,102},{7,103},{8,104... | collective-permute-start | bytes 393224 | tf_op jit(solution)/shard_map/ppermute | solution.py:46
  71.4 112.1 %collective-permute-start.30 = (bf16[512,4096]{1,0:T(8,128)(2,1)}, bf16[512,4096]{1,0:T(8,128)(2,1)}, u32[]{:S(2)}, u32[]{:S(2)}) collective-permute-start(bf16[512,4096]{1,0:T(8,128)(2,1)} %direct_rows.1), channel_id=1, source_target_pairs={{0,66},{1,67},{2,64},{3,65},{4,70},{5,71},{6,68},{7,69},{8,74},{9,... | collective-permute-start | bytes 12582920 | tf_op jit(solution)/shard_map/ppermute | solution.py:46
  84.1 23.2 %collective-permute-start.43 = (bf16[128,4096]{1,0:T(8,128)(2,1)}, bf16[128,4096]{1,0:T(8,128)(2,1)}, u32[]{:S(2)}, u32[]{:S(2)}) collective-permute-start(bf16[128,4096]{1,0:T(8,128)(2,1)} %get-tuple-element.50.refs_0_), channel_id=1, source_target_pairs={{0,4},{1,5},{2,6},{3,7},{4,8},{5,9},{6,10},{7,11},{8,12},{9,13},{1... | collective-permute-start | bytes 3145736 | tf_op jit(solution)/shard_map/ppermute | solution.py:46
  86.1 22.3 %collective-permute-start.44 = (bf16[128,4096]{1,0:T(8,128)(2,1)}, bf16[128,4096]{1,0:T(8,128)(2,1)}, u32[]{:S(2)}, u32[]{:S(2)}) collective-permute-start(bf16[128,4096]{1,0:T(8,128)(2,1)} %get-tuple-element.50.refs_0_), channel_id=1, source_target_pairs={{0,12},{1,13},{2,14},{3,15},{4,0},{5,1},{6,2},{7,3},{8,4},{9,5},{1... | collective-permute-start | bytes 3145736 | tf_op jit(solution)/shard_map/ppermute | solution.py:46
  88.3 21.6 %collective-permute-start.32 = (bf16[64,4096]{1,0:T(8,128)(2,1)S(1)}, bf16[64,4096]{1,0:T(8,128)(2,1)S(1)}, u32[]{:S(2)}, u32[]{:S(2)}) collective-permute-start(bf16[64,4096]{1,0:T(8,128)(2,1)S(1)} %get-tuple-element.63), channel_id=1, source_target_pairs={{0,16},{1,17},{2,18},{3,19},{4,20},{5,21},{6,22},{7,23},{8,24},{9,... | collective-permute-start | bytes 1572872 | tf_op jit(solution)/shard_map/ppermute | solution.py:46
  88.4 21.7 %collective-permute-start.33 = (bf16[64,4096]{1,0:T(8,128)(2,1)S(1)}, bf16[64,4096]{1,0:T(8,128)(2,1)S(1)}, u32[]{:S(2)}, u32[]{:S(2)}) collective-permute-start(bf16[64,4096]{1,0:T(8,128)(2,1)S(1)} %get-tuple-element.63), channel_id=1, source_target_pairs={{0,48},{1,49},{2,50},{3,51},{4,52},{5,53},{6,54},{7,55},{8,56},{9,... | collective-permute-start | bytes 1572872 | tf_op jit(solution)/shard_map/ppermute | solution.py:46
  107.3 15.3 %collective-permute-start.31 = (bf16[64,4096]{1,0:T(8,128)(2,1)S(1)}, bf16[64,4096]{1,0:T(8,128)(2,1)S(1)}, u32[]{:S(2)}, u32[]{:S(2)}) collective-permute-start(bf16[64,4096]{1,0:T(8,128)(2,1)S(1)} %get-tuple-element.64), channel_id=1, source_target_pairs={{0,64},{1,65},{2,66},{3,67},{4,68},{5,69},{6,70},{7,71},{8,72},{9,... | collective-permute-start | bytes 1572872 | tf_op jit(solution)/shard_map/ppermute | solution.py:46
  108.4 14.4 %collective-permute-start.48 = (bf16[64,4096]{1,0:T(8,128)(2,1)S(1)}, bf16[64,4096]{1,0:T(8,128)(2,1)S(1)}, u32[]{:S(2)}, u32[]{:S(2)}) collective-permute-start(bf16[64,4096]{1,0:T(8,128)(2,1)S(1)} %slice.44), channel_id=1, source_target_pairs={{0,4},{1,5},{2,6},{3,7},{4,8},{5,9},{6,10},{7,11},{8,12},{9,13},{1... | collective-permute-start | bytes 1572872 | tf_op jit(solution)/shard_map/ppermute | solution.py:46
  110.0 7.7 %collective-permute-start.36 = (bf16[32,4096]{1,0:T(8,128)(2,1)S(1)}, bf16[32,4096]{1,0:T(8,128)(2,1)S(1)}, u32[]{:S(2)}, u32[]{:S(2)}) collective-permute-start(bf16[32,4096]{1,0:T(8,128)(2,1)S(1)} %slice.40), channel_id=1, source_target_pairs={{0,16},{1,17},{2,18},{3,19},{4,20},{5,21},{6,22},{7,23},{8,24},{9,... | collective-permute-start | bytes 786440 | tf_op jit(solution)/shard_map/ppermute | solution.py:46
  110.1 10.4 %collective-permute-start.37 = (bf16[32,4096]{1,0:T(8,128)(2,1)S(1)}, bf16[32,4096]{1,0:T(8,128)(2,1)S(1)}, u32[]{:S(2)}, u32[]{:S(2)}) collective-permute-start(bf16[32,4096]{1,0:T(8,128)(2,1)S(1)} %slice.41), channel_id=1, source_target_pairs={{0,48},{1,49},{2,50},{3,51},{4,52},{5,53},{6,54},{7,55},{8,56},{9,... | collective-permute-start | bytes 786440 | tf_op jit(solution)/shard_map/ppermute | solution.py:46
  117.7 47.3 %copy-start.8 = (bf16[32,4096]{1,0:T(8,128)(2,1)}, bf16[32,4096]{1,0:T(8,128)(2,1)S(1)}, u32[]{:S(2)}) copy-start(bf16[32,4096]{1,0:T(8,128)(2,1)S(1)} %collective-permute-done.36.refs_9_.refs_11_) | copy-start | bytes 786436
  117.7 9.6 %collective-permute-start.49 = (bf16[64,4096]{1,0:T(8,128)(2,1)S(1)}, bf16[64,4096]{1,0:T(8,128)(2,1)S(1)}, u32[]{:S(2)}, u32[]{:S(2)}) collective-permute-start(bf16[64,4096]{1,0:T(8,128)(2,1)S(1)} %slice.45), channel_id=1, source_target_pairs={{0,12},{1,13},{2,14},{3,15},{4,0},{5,1},{6,2},{7,3},{8,4},{9,5},{1... | collective-permute-start | bytes 1572872 | tf_op jit(solution)/shard_map/ppermute | solution.py:46
  120.5 47.2 %collective-permute-start.38 = (bf16[192,4096]{1,0:T(8,128)(2,1)S(1)}, bf16[192,4096]{1,0:T(8,128)(2,1)S(1)}, u32[]{:S(2)}, u32[]{:S(2)}) collective-permute-start(bf16[192,4096]{1,0:T(8,128)(2,1)S(1)} %pad_maximum_fusion), channel_id=1, source_target_pairs={{0,64},{1,65},{2,66},{3,67},{4,68},{5,69},{6,70},{7,71},{8,72},{9,... | collective-permute-start | bytes 4718600 | tf_op jit(solution)/shard_map/ppermute | solution.py:46
  122.6 43.2 %copy-start.6 = (bf16[64,4096]{1,0:T(8,128)(2,1)}, bf16[64,4096]{1,0:T(8,128)(2,1)S(1)}, u32[]{:S(2)}) copy-start(bf16[64,4096]{1,0:T(8,128)(2,1)S(1)} %collective-permute-done.31.refs_4_.refs_6_) | copy-start | bytes 1572868
  122.6 38.8 %collective-permute-start.41 = (bf16[64,4096]{1,0:T(8,128)(2,1)S(1)}, bf16[64,4096]{1,0:T(8,128)(2,1)S(1)}, u32[]{:S(2)}, u32[]{:S(2)}) collective-permute-start(bf16[64,4096]{1,0:T(8,128)(2,1)S(1)} %pad_maximum_fusion.2), channel_id=1, source_target_pairs={{0,64},{1,65},{2,66},{3,67},{4,68},{5,69},{6,70},{7,71},{8,72},{9,... | collective-permute-start | bytes 1572872 | tf_op jit(solution)/shard_map/ppermute | solution.py:46
  122.8 44.9 %copy-start.11 = (bf16[64,4096]{1,0:T(8,128)(2,1)}, bf16[64,4096]{1,0:T(8,128)(2,1)S(1)}, u32[]{:S(2)}) copy-start(bf16[64,4096]{1,0:T(8,128)(2,1)S(1)} %collective-permute-done.48.refs_0_) | copy-start | bytes 1572868
  122.8 40.7 %collective-permute-start.34 = (bf16[128,4096]{1,0:T(8,128)(2,1)S(1)}, bf16[128,4096]{1,0:T(8,128)(2,1)S(1)}, u32[]{:S(2)}, u32[]{:S(2)}) collective-permute-start(bf16[128,4096]{1,0:T(8,128)(2,1)S(1)} %pad_maximum_fusion.1), channel_id=1, source_target_pairs={{0,16},{1,17},{2,18},{3,19},{4,20},{5,21},{6,22},{7,23},{8,24},{9,... | collective-permute-start | bytes 3145736 | tf_op jit(solution)/shard_map/ppermute | solution.py:46
  127.2 40.5 %copy-start.12 = (bf16[64,4096]{1,0:T(8,128)(2,1)}, bf16[64,4096]{1,0:T(8,128)(2,1)S(1)}, u32[]{:S(2)}) copy-start(bf16[64,4096]{1,0:T(8,128)(2,1)S(1)} %collective-permute-done.49.refs_1_) | copy-start | bytes 1572868
  127.2 36.7 %collective-permute-start.35 = (bf16[128,4096]{1,0:T(8,128)(2,1)S(1)}, bf16[128,4096]{1,0:T(8,128)(2,1)S(1)}, u32[]{:S(2)}, u32[]{:S(2)}) collective-permute-start(bf16[128,4096]{1,0:T(8,128)(2,1)S(1)} %pad_maximum_fusion.1), channel_id=1, source_target_pairs={{0,48},{1,49},{2,50},{3,51},{4,52},{5,53},{6,54},{7,55},{8,56},{9,... | collective-permute-start | bytes 3145736 | tf_op jit(solution)/shard_map/ppermute | solution.py:46
  161.4 1.9 collective-permute-start.50
  163.4 2.5 collective-permute-start.51
  163.5 30.9 %collective-permute-start.45 = (bf16[128,4096]{1,0:T(8,128)(2,1)}, bf16[128,4096]{1,0:T(8,128)(2,1)}, u32[]{:S(2)}, u32[]{:S(2)}) collective-permute-start(bf16[128,4096]{1,0:T(8,128)(2,1)} %collective-permute-done.43.refs_0_), channel_id=1, source_target_pairs={{0,1},{1,0},{2,3},{3,2},{4,5},{5,4},{6,7},{7,6},{8,9},{9,8},{10,11... | collective-permute-start | bytes 3145736 | tf_op jit(solution)/shard_map/ppermute | solution.py:46
  163.9 30.5 %collective-permute-start.46 = (bf16[128,4096]{1,0:T(8,128)(2,1)}, bf16[128,4096]{1,0:T(8,128)(2,1)}, u32[]{:S(2)}, u32[]{:S(2)}) collective-permute-start(bf16[128,4096]{1,0:T(8,128)(2,1)} %collective-permute-done.44.refs_1_), channel_id=1, source_target_pairs={{0,1},{1,0},{2,3},{3,2},{4,5},{5,4},{6,7},{7,6},{8,9},{9,8},{10,11... | collective-permute-start | bytes 3145736 | tf_op jit(solution)/shard_map/ppermute | solution.py:46
  165.8 16.1 %collective-permute-start.39 = (bf16[64,4096]{1,0:T(8,128)(2,1)}, bf16[64,4096]{1,0:T(8,128)(2,1)}, u32[]{:S(2)}, u32[]{:S(2)}) collective-permute-start(bf16[64,4096]{1,0:T(8,128)(2,1)} %slice.42), channel_id=1, source_target_pairs={{0,16},{1,17},{2,18},{3,19},{4,20},{5,21},{6,22},{7,23},{8,24},{9,... | collective-permute-start | bytes 1572872 | tf_op jit(solution)/shard_map/ppermute | solution.py:46
  167.8 15.7 %collective-permute-start.40 = (bf16[64,4096]{1,0:T(8,128)(2,1)}, bf16[64,4096]{1,0:T(8,128)(2,1)}, u32[]{:S(2)}, u32[]{:S(2)}) collective-permute-start(bf16[64,4096]{1,0:T(8,128)(2,1)} %slice.43), channel_id=1, source_target_pairs={{0,48},{1,49},{2,50},{3,51},{4,52},{5,53},{6,54},{7,55},{8,56},{9,... | collective-permute-start | bytes 1572872 | tf_op jit(solution)/shard_map/ppermute | solution.py:46
  181.9 45.7 %collective-permute-start.28 = (bf16[128,4096]{1,0:T(8,128)(2,1)}, bf16[128,4096]{1,0:T(8,128)(2,1)S(1)}, u32[]{:S(2)}, u32[]{:S(2)}) collective-permute-start(bf16[128,4096]{1,0:T(8,128)(2,1)} %get-tuple-element.50.refs_0_), channel_id=1, source_target_pairs={{0,1},{1,0},{2,3},{3,2},{4,5},{5,4},{6,7},{7,6},{8,9},{9,8},{10,11... | collective-permute-start | bytes 3145736 | tf_op jit(solution)/shard_map/ppermute | solution.py:46
  194.0 29.6 %collective-permute-start.52 = (bf16[128,4096]{1,0:T(8,128)(2,1)}, bf16[128,4096]{1,0:T(8,128)(2,1)}, u32[]{:S(2)}, u32[]{:S(2)}) collective-permute-start(bf16[128,4096]{1,0:T(8,128)(2,1)} %get-tuple-element.58), channel_id=1, source_target_pairs={{0,1},{1,0},{2,3},{3,2},{4,5},{5,4},{6,7},{7,6},{8,9},{9,8},{10,11... | collective-permute-start | bytes 3145736 | tf_op jit(solution)/shard_map/ppermute | solution.py:46
  223.1 27.2 %collective-permute-start.55 = (bf16[128,4096]{1,0:T(8,128)(2,1)}, bf16[128,4096]{1,0:T(8,128)(2,1)S(1)}, u32[]{:S(2)}, u32[]{:S(2)}) collective-permute-start(bf16[128,4096]{1,0:T(8,128)(2,1)} %get-tuple-element.60), channel_id=1, source_target_pairs={{0,1},{1,0},{2,3},{3,2},{4,5},{5,4},{6,7},{7,6},{8,9},{9,8},{10,11... | collective-permute-start | bytes 3145736 | tf_op jit(solution)/shard_map/ppermute | solution.py:46
  226.1 24.1 %collective-permute-start.56 = (bf16[64,4096]{1,0:T(8,128)(2,1)}, bf16[64,4096]{1,0:T(8,128)(2,1)S(1)}, u32[]{:S(2)}, u32[]{:S(2)}) collective-permute-start(bf16[64,4096]{1,0:T(8,128)(2,1)} %get-tuple-element.62), channel_id=1, source_target_pairs={{0,12},{1,13},{2,14},{3,15},{4,0},{5,1},{6,2},{7,3},{8,4},{9,5},{1... | collective-permute-start | bytes 1572872 | tf_op jit(solution)/shard_map/ppermute | solution.py:46
  238.3 15.0 %collective-permute-start.47 = (bf16[128,4096]{1,0:T(8,128)(2,1)}, bf16[128,4096]{1,0:T(8,128)(2,1)S(1)}, u32[]{:S(2)}, u32[]{:S(2)}) collective-permute-start(bf16[128,4096]{1,0:T(8,128)(2,1)} %get-tuple-element.56), channel_id=1, source_target_pairs={{0,1},{1,0},{2,3},{3,2},{4,5},{5,4},{6,7},{7,6},{8,9},{9,8},{10,11... | collective-permute-start | bytes 3145736 | tf_op jit(solution)/shard_map/ppermute | solution.py:46
  249.1 17.0 %collective-permute-start.42 = (bf16[128,4096]{1,0:T(8,128)(2,1)}, bf16[128,4096]{1,0:T(8,128)(2,1)S(1)}, u32[]{:S(2)}, u32[]{:S(2)}) collective-permute-start(bf16[128,4096]{1,0:T(8,128)(2,1)} %get-tuple-element.54), channel_id=1, source_target_pairs={{0,1},{1,0},{2,3},{3,2},{4,5},{5,4},{6,7},{7,6},{8,9},{9,8},{10,11... | collective-permute-start | bytes 3145736 | tf_op jit(solution)/shard_map/ppermute | solution.py:46
  249.7 15.3 %collective-permute-start.53 = (bf16[64,4096]{1,0:T(8,128)(2,1)}, bf16[64,4096]{1,0:T(8,128)(2,1)S(1)}, u32[]{:S(2)}, u32[]{:S(2)}) collective-permute-start(bf16[64,4096]{1,0:T(8,128)(2,1)} %get-tuple-element.61), channel_id=1, source_target_pairs={{0,4},{1,5},{2,6},{3,7},{4,8},{5,9},{6,10},{7,11},{8,12},{9,13},{1... | collective-permute-start | bytes 1572872 | tf_op jit(solution)/shard_map/ppermute | solution.py:46
  250.6 40.3 %copy-start.15 = (bf16[128,4096]{1,0:T(8,128)(2,1)S(1)}, bf16[128,4096]{1,0:T(8,128)(2,1)}, u32[]{:S(2)}) copy-start(bf16[128,4096]{1,0:T(8,128)(2,1)} %get-tuple-element.49) | copy-start | bytes 3145732
  250.6 40.3 %copy-start.17 = (bf16[128,4096]{1,0:T(8,128)(2,1)S(1)}, bf16[128,4096]{1,0:T(8,128)(2,1)}, u32[]{:S(2)}) copy-start(bf16[128,4096]{1,0:T(8,128)(2,1)} %get-tuple-element.53) | copy-start | bytes 3145732
  250.6 25.1 %collective-permute-start.57 = (bf16[128,4096]{1,0:T(8,128)(2,1)S(1)}, bf16[128,4096]{1,0:T(8,128)(2,1)S(1)}, u32[]{:S(2)}, u32[]{:S(2)}) collective-permute-start(bf16[128,4096]{1,0:T(8,128)(2,1)S(1)} %add_convert_fusion), channel_id=1, source_target_pairs={{0,12},{1,13},{2,14},{3,15},{4,0},{5,1},{6,2},{7,3},{8,4},{9,5},{1... | collective-permute-start | bytes 3145736 | tf_op jit(solution)/shard_map/ppermute | solution.py:46
  265.4 25.6 %collective-permute-start.54 = (bf16[128,4096]{1,0:T(8,128)(2,1)S(1)}, bf16[128,4096]{1,0:T(8,128)(2,1)S(1)}, u32[]{:S(2)}, u32[]{:S(2)}) collective-permute-start(bf16[128,4096]{1,0:T(8,128)(2,1)S(1)} %add_convert_fusion.1), channel_id=1, source_target_pairs={{0,4},{1,5},{2,6},{3,7},{4,8},{5,9},{6,10},{7,11},{8,12},{9,13},{1... | collective-permute-start | bytes 3145736 | tf_op jit(solution)/shard_map/ppermute | solution.py:46
  (31 other events, 382.4 us)

commit v2 on v1

--- a/solution.py
+++ b/solution.py
@@ -39,7 +39,7 @@
     return pairs(lambda xl, y, z, xh, c: ((xl + dx) % 2, y + dy, z, xh, c))
 
 
-OFFSETS = tuple((dx, dy) for dx in range(2) for dy in (0, 1, 3, 2))
+OFFSETS = ((0, 0), (1, 2), (0, 2), (1, 1), (1, 3), (0, 1), (0, 3), (1, 0))
 
 
 def send(value, table):
@@ -67,7 +67,7 @@
 
 
 def cut_kernel(index_ref, cache_ref, up_ref, down_ref, *refs):
-    outs, share, sems = refs[:16], refs[16], refs[17]
+    outs, share, sems = refs[:8], refs[8], refs[9]
     first = pl.multiple_of(index_ref[8] * 64, 64)
     moves = []
     for i, (source, row) in enumerate(((up_ref, 0), (down_ref, 0), (up_ref, 32), (down_ref, 32))):
@@ -76,9 +76,8 @@
     for move in moves:
         move.start()
     for place in range(8):
-        row = pl.multiple_of(index_ref[place] * 16, 16)
-        outs[place][...] = cache_ref[pl.ds(row, 16), :]
-        outs[8 + place][...] = cache_ref[pl.ds(pl.multiple_of(128 + row, 16), 16), :]
+        row = pl.multiple_of(index_ref[place] * 32, 32)
+        outs[place][...] = cache_ref[pl.ds(row, 32), :]
     for move in moves:
         move.wait()
 
@@ -87,9 +86,9 @@
     width = cache.shape[1]
     return pl.pallas_call(
         cut_kernel,
-        out_shape=[jax.ShapeDtypeStruct((16, width), BF16)] * 16 + [jax.ShapeDtypeStruct((128, width), BF16)],
+        out_shape=[jax.ShapeDtypeStruct((32, width), BF16)] * 8 + [jax.ShapeDtypeStruct((128, width), BF16)],
         in_specs=[smem(), vmem(), hbm(), hbm()],
-        out_specs=[vmem()] * 17,
+        out_specs=[vmem()] * 9,
         scratch_shapes=[pltpu.SemaphoreType.DMA((4,))],
         compiler_params=params(),
         cost_estimate=cost(0, 6 * cache.size),
@@ -126,11 +125,9 @@
 
 
 def attention_kernel(slope_ref, place_ref, proj_ref, residual_ref, gain_ref, *refs):
-    pieces, (state_ref, normed_ref, keys, values, bias, sums) = refs[:16], refs[16:]
+    pieces, (state_ref, low_ref, high_ref, cached, bias, sums) = refs[:8], refs[8:]
     for place in range(8):
-        start = pl.multiple_of(place_ref[place] * 16, 16)
-        keys[pl.ds(start, 16), :] = pieces[place][...]
-        values[pl.ds(start, 16), :] = pieces[8 + place][...]
+        cached[pl.ds(pl.multiple_of(place_ref[place] * 32, 32), 32), :] = pieces[place][...]
     row = lax.broadcasted_iota(jnp.int32, (128, 256), 0)
     col = lax.broadcasted_iota(jnp.int32, (128, 256), 1)
     bias[...] = jnp.where(col - 128 <= row, (col - 128 - row).astype(F32), -1e30)
@@ -142,8 +139,8 @@
         for j in range(GROUP):
             h = i * GROUP + j
             part = pl.ds(pl.multiple_of(h * 128, 128), 128)
-            key = jnp.concatenate([keys[:, part], proj_ref[1, :, part]], axis=0)
-            value = jnp.concatenate([values[:, part], proj_ref[2, :, part]], axis=0)
+            key = jnp.concatenate([cached[0:128, part], proj_ref[1, :, part]], axis=0)
+            value = jnp.concatenate([cached[128:256, part], proj_ref[2, :, part]], axis=0)
             value = jnp.concatenate([value, ones], axis=1)
             scores = lax.dot_general(
                 proj_ref[0, :, part], key, (((1,), (1,)), ((), ())), preferred_element_type=F32
@@ -168,17 +165,19 @@
     for h in range(HEADS):
         part = slice(h * 128, (h + 1) * 128)
         center = state_ref[:, part].astype(F32) - mean
-        normed_ref[:, part] = (center * spread * gain_ref[:, part]).astype(BF16)
+        normed = (center * spread * gain_ref[:, part]).astype(BF16)
+        low_ref[:, part] = normed[:64]
+        high_ref[:, part] = normed[64:]
 
 
 def attention(slopes, places, proj, residual, gain, pieces):
     width = proj.shape[2]
     return pl.pallas_call(
         attention_kernel,
-        out_shape=[jax.ShapeDtypeStruct((128, width), BF16)] * 2,
-        in_specs=[smem(), smem()] + [vmem()] * 19,
-        out_specs=[vmem()] * 2,
-        scratch_shapes=[pltpu.VMEM((128, width), BF16)] * 2
+        out_shape=[jax.ShapeDtypeStruct((128, width), BF16)] + [jax.ShapeDtypeStruct((64, width), BF16)] * 2,
+        in_specs=[smem(), smem()] + [vmem()] * 11,
+        out_specs=[vmem()] * 3,
+        scratch_shapes=[pltpu.VMEM((256, width), BF16)]
         + [pltpu.VMEM((128, 256), F32), pltpu.VMEM((128, 128), F32)],
         compiler_params=params(),
         cost_estimate=cost(8 * 128 * 256 * width, 8 * 128 * width * 2),
@@ -312,47 +311,44 @@
     dests = [((xl + dx) % 2) * 4 + (y + dy) % 4 for dx, dy in OFFSETS]
     origins = jnp.stack([((xl + dx) % 2) * 4 + (y - dy) % 4 for dx, dy in OFFSETS]).astype(jnp.int32)
     cuts = cut_slices(jnp.stack(dests + [other]).astype(jnp.int32), prefix_cache.reshape(256, width), up, down)
-    pieces = []
-    for part in (cuts[:8], cuts[8:16]):
-        kept = part[0]
-        for place in range(1, 8):
-            got = send(part[place], req_offset(*OFFSETS[place]))
-            kept = jnp.where(origins[place] == owner, got, kept)
-        pieces += [kept] + [send(kept, req_offset(*OFFSETS[place])) for place in range(1, 8)]
-
-    shard = send(cuts[16], X_CUT)
+    kept = cuts[0]
+    for place in range(1, 8):
+        got = send(cuts[place], req_offset(*OFFSETS[place]))
+        kept = jnp.where(origins[place] == owner, got, kept)
+    pieces = [kept] + [send(kept, req_offset(*OFFSETS[place])) for place in range(1, 8)]
+
+    shard = send(cuts[8], X_CUT)
     direct = send(direct_rows(up, down), X_CUT)
 
-    states, normed = attention(slopes, origins, suffix_proj[0, 0], residual[0, 0], norm_gain, pieces)
-
-    shard, _ = lax.optimization_barrier((shard, pieces))
+    states, low, high = attention(slopes, origins, suffix_proj[0, 0], residual[0, 0], norm_gain, pieces)
+
+    shard, _ = lax.optimization_barrier((shard, (pieces[5], pieces[6], pieces[7])))
     a_own, b_own = shard[:64], shard[64:]
     a_x = send(a_own, X_LOW)
     b_m, b_p = send(b_own, Y_UP), send(b_own, Y_DOWN)
+    b_2 = send(b_own, req_offset(0, 2))
+    b_x = send(jnp.concatenate([b_own, b_m, b_p, b_2]), X_LOW)
     a_pair = jnp.concatenate([a_own, a_x])
     a_m, a_p = send(a_pair, Y_UP), send(a_pair, Y_DOWN)
-    b_2u, b_2d = send(b_m[:32], Y_UP), send(b_p[32:], Y_DOWN)
-    b_x = send(jnp.concatenate([b_own, b_m, b_p]), X_LOW)
-    a_2u, a_2d = send(a_m[:64], Y_UP), send(a_p[64:], Y_DOWN)
-    b_x2 = send(jnp.concatenate([b_2u, b_2d]), X_LOW)
-    far = [shard, direct, a_x, b_m, b_p, a_m, a_p, b_2u, b_2d, b_x, a_2u, a_2d, b_x2]
+    a_2 = send(a_pair, req_offset(0, 2))
+    far = [shard, direct, a_x, b_m, b_p, b_2, b_x, a_m, a_p, a_2]
+    pieces_of = lambda index, count: [(index, 64 * i, index, 64 * i + 32, 32) for i in range(count)]
     far_units = [
-        (0, 0, 0, 32, 32), (0, 64, 0, 96, 32), (1, 0, 1, 256, 256), (2, 0, 2, 32, 32),
-        (3, 0, 3, 32, 32), (4, 0, 4, 32, 32), (5, 0, 5, 32, 32), (5, 64, 5, 96, 32),
-        (6, 0, 6, 32, 32), (6, 64, 6, 96, 32), (7, 0, 8, 0, 32),
-        (9, 0, 9, 32, 32), (9, 64, 9, 96, 32), (9, 128, 9, 160, 32),
-        (10, 0, 10, 32, 32), (11, 0, 11, 32, 32), (12, 0, 12, 32, 32),
+        *pieces_of(0, 2), (1, 0, 1, 256, 256), *pieces_of(2, 1), *pieces_of(3, 1), *pieces_of(4, 1), *pieces_of(5, 1),
+        *pieces_of(7, 2), *pieces_of(8, 2), *pieces_of(9, 2), *pieces_of(6, 4),
     ]
     near, near_units = [up, down], [(0, 0, 1, 0, 768)]
 
-    t_m, t_p = send(normed, Z_UP), send(normed, Z_DOWN)
-    t_0c = send(normed, CORE)
-    t_2u, t_2d = send(t_m[:64], Z_UP), send(t_p[64:], Z_DOWN)
-    t_mc, t_pc = send(t_m, CORE), send(t_p, CORE)
-    t_2uc, t_2dc = send(t_2u, CORE), send(t_2d, CORE)
-    own = [normed, t_0c]
-    side = [t_m, t_p, t_mc, t_pc]
-    far_z = [t_2u, t_2d, t_2uc, t_2dc]
+    low_m, high_p = send(low, Z_UP), send(high, Z_DOWN)
+    high_m, low_p = send(high, Z_UP), send(low, Z_DOWN)
+    t_2u, t_2d = send(low_m, Z_UP), send(high_p, Z_DOWN)
+
+    def both_cores(*values):
+        return list(values) + [send(value, CORE) for value in values]
+
+    own = both_cores(low, high)
+    side = both_cores(low_m, high_m, low_p, high_p)
+    far_z = both_cores(t_2u, t_2d)
     y_own = ffn(own, near, near_units)
     y_side = ffn(side, near, near_units)
     y_far = ffn(far_z, near, near_units)

time: 293 us -> 291 us (level)
  starting transfers between devices: 81 us -> 53.5 us
  waiting for transfers between devices: 105 us -> 129 us
    ppermute x58 -> x46, starting transfers between devices: 81 us -> 53.5 us  [send(): return lax.ppermute(value, AXES, table)]
    ppermute x58 -> x46, waiting for transfers between devices: 105 us -> 129 us  [send(): return lax.ppermute(value, AXES, table)]
    slice x6 -> x0, local copies, waits for them, and re-layouts: 3.98 us -> none  [the longest x2 2.15 us: body(): t_2u, t_2d = (send(t_m[:64], Z_UP), send(t_p[64:], Z_DOWN))]
  transfers between devices with their start and end apart: 58 -> 46, of which waited for: 17 -> 18; matrix products, arithmetic and copies ran while one was open for 4% -> 3% of each run, Pallas kernels for 28% -> 29%
where the time goes in v2:
time: 291 us; the launch traced here: 289 us
  waiting for transfers between devices  129 us (44%)
  Pallas kernels  87.6 us (30%)
  starting transfers between devices  53.5 us (18%)
  other arithmetic  6.98 us (2%)
  local copies, waits for them, and re-layouts  6.48 us (2%)
  between operations  5.01 us (2%)
    ppermute x46, waiting for transfers between devices, send(): return lax.ppermute(value, AXES, table)  129 us
    pallas_call x6, Pallas kernels, ffn(): pl.pallas_call(functools.partial(ffn_kernel, rows, len(arrays), ups, down...  71 us
    ppermute x46, starting transfers between devices, send(): return lax.ppermute(value, AXES, table)  53.5 us
    pallas_call x1, Pallas kernels, attention(): pl.pallas_call(attention_kernel, out_shape=[jax.ShapeDtypeStruct((128, wi...  7.95 us
  transfers between devices with their start and end apart: 46, of which 18 were waited for; matrix products, arithmetic and copies ran while one was open for 3% of the time, Pallas kernels for 29%

profile of v2, /device:TPU:0, one launch (start us, length us, event | category | flops | bytes accessed | tf_op | source)
XLA Modules:
  0.0 288.7 jit_solution(4603005921307677096)
XLA Ops:
  0.0 0.7 stack.69.index_ref
  0.7 4.5 %cut_slices.1 = (bf16[32,4096]{1,0:T(8,128)(2,1)}, bf16[32,4096]{1,0:T(8,128)(2,1)}, bf16[32,4096]{1,0:T(8,128)(2,1)}, bf16[32,4096]{1,0:T(8,128)(2,1)}, bf16[32...) custom-call(s32[9]{0:T(128)} %stack.69.index_ref, ...), custom_call_target="tpu_custom_call" | custom-call | bytes 6291456 | tf_op jit(solution)/shard_map/cut_slices/pallas_call | solution.py:87
  5.2 1.7 collective-permute-start
  6.9 3.0 %collective-permute-start.1 = (bf16[32,4096]{1,0:T(8,128)(2,1)}, bf16[32,4096]{1,0:T(8,128)(2,1)S(1)}, u32[]{:S(2)}, u32[]{:S(2)}) collective-permute-start(bf16[32,4096]{1,0:T(8,128)(2,1)} %get-tuple-element.27), channel_id=1, source_target_pairs={{0,48},{1,49},{2,50},{3,51},{4,52},{5,53},{6,54},{7,55},{8,56},{9,... | collective-permute-start | bytes 786440 | tf_op jit(solution)/shard_map/ppermute | solution.py:46
  9.9 3.2 %collective-permute-start.3 = (bf16[32,4096]{1,0:T(8,128)(2,1)}, bf16[32,4096]{1,0:T(8,128)(2,1)S(1)}, u32[]{:S(2)}, u32[]{:S(2)}) collective-permute-start(bf16[32,4096]{1,0:T(8,128)(2,1)} %get-tuple-element.29), channel_id=1, source_target_pairs={{0,112},{1,113},{2,114},{3,115},{4,116},{5,117},{6,118},{7,119},{8... | collective-permute-start | bytes 786440 | tf_op jit(solution)/shard_map/ppermute | solution.py:46
  13.4 4.6 %collective-permute-start.5 = (bf16[32,4096]{1,0:T(8,128)(2,1)}, bf16[32,4096]{1,0:T(8,128)(2,1)S(1)}, u32[]{:S(2)}, u32[]{:S(2)}) collective-permute-start(bf16[32,4096]{1,0:T(8,128)(2,1)} %get-tuple-element.31), channel_id=1, source_target_pairs={{0,32},{1,33},{2,34},{3,35},{4,36},{5,37},{6,38},{7,39},{8,40},{9,... | collective-permute-start | bytes 786440 | tf_op jit(solution)/shard_map/ppermute | solution.py:46
  17.9 11.6 %collective-permute-done.1 = bf16[32,4096]{1,0:T(8,128)(2,1)S(1)} collective-permute-done((bf16[32,4096]{1,0:T(8,128)(2,1)}, bf16[32,4096]{1,0:T(8,128)(2,1)S(1)}, u32[]{:S(2)}, u32[]{:S(2)}) %collective-permute-start.1) | collective-permute-done | bytes 262176 | tf_op jit(solution)/shard_map/ppermute | solution.py:46
  29.6 0.6 dynamic_slice.4
  34.0 2.2 collective-permute-start.16
  36.1 4.8 %collective-permute-done.6 = bf16[32,4096]{1,0:T(8,128)(2,1)S(1)} collective-permute-done((bf16[32,4096]{1,0:T(8,128)(2,1)}, bf16[32,4096]{1,0:T(8,128)(2,1)S(1)}, u32[]{:S(2)}, u32[]{:S(2)}) %collective-permute-start.6) | collective-permute-done | bytes 262176 | tf_op jit(solution)/shard_map/ppermute | solution.py:46
  40.9 1.0 select_select_fusion.refs_0_
  42.1 2.3 collective-permute-start.8
  44.4 2.6 collective-permute-start.9
  47.0 2.3 collective-permute-start.10
  49.3 1.7 collective-permute-done.7.refs_1_
  51.0 1.0 collective-permute-start.11
  52.0 6.2 %collective-permute-done.8.refs_2_ = bf16[32,4096]{1,0:T(8,128)(2,1)S(1)} collective-permute-done((bf16[32,4096]{1,0:T(8,128)(2,1)S(1)}, bf16[32,4096]{1,0:T(8,128)(2,1)S(1)}, u32[]{:S(2)}, u32[]{:S(2)}) %collective-permute-start.8) | collective-permute-done | bytes 262176 | tf_op jit(solution)/shard_map/ppermute | solution.py:46
  58.2 1.0 collective-permute-start.12
  59.3 4.2 %direct_rows.1 = bf16[512,4096]{1,0:T(8,128)(2,1)} custom-call(bf16[768,4096]{1,0:T(8,128)(2,1)} %refs_4_.3, bf16[768,4096]{1,0:T(8,128)(2,1)} %refs_5_.3), custom_call_target="tpu_custom_call" | custom-call | bytes 8388608 | tf_op jit(solution)/shard_map/direct_rows/pallas_call | solution.py:112
  63.6 0.6 stack.61.place_ref
  64.2 0.6 multiply_exponential_fusion.slope_ref
  64.8 3.4 %collective-permute-start.17 = (bf16[512,4096]{1,0:T(8,128)(2,1)}, bf16[512,4096]{1,0:T(8,128)(2,1)}, u32[]{:S(2)}, u32[]{:S(2)}) collective-permute-start(bf16[512,4096]{1,0:T(8,128)(2,1)} %direct_rows.1), channel_id=1, source_target_pairs={{0,66},{1,67},{2,64},{3,65},{4,70},{5,71},{6,68},{7,69},{8,74},{9,... | collective-permute-start | bytes 12582920 | tf_op jit(solution)/shard_map/ppermute | solution.py:46
  68.2 0.7 copy-done.29
  69.1 8.0 %attention.1 = (bf16[128,4096]{1,0:T(8,128)(2,1)}, bf16[64,4096]{1,0:T(8,128)(2,1)}, bf16[64,4096]{1,0:T(8,128)(2,1)}) custom-call(f32[32]{0:T(128)} %multiply_exponential_fusion.slope_ref, s32[8]{0:T(128)} %stack.61.place_ref, bf16[3,128,4096]{2,1,0:T(8,128)(2,1)} %bitcast.24, bf16[128,4096]{1,0:T(8,128)(2,1)} %bitcast.26, f32[1,4096]{1,0:T(1,128)} %bitcast.27, ...), custom_call_target="tpu_custom_call" | custom-call | flops 1073741824 | bytes 8388608 | tf_op jit(solution)/shard_map/attention/pallas_call | solution.py:175
  77.0 1.6 collective-permute-start.27
  78.7 2.9 %collective-permute-start.30 = (bf16[64,4096]{1,0:T(8,128)(2,1)}, bf16[64,4096]{1,0:T(8,128)(2,1)}, u32[]{:S(2)}, u32[]{:S(2)}) collective-permute-start(bf16[64,4096]{1,0:T(8,128)(2,1)} %get-tuple-element.36.refs_1_), channel_id=1, source_target_pairs={{0,12},{1,13},{2,14},{3,15},{4,0},{5,1},{6,2},{7,3},{8,4},{9,5},{1... | collective-permute-start | bytes 1572872 | tf_op jit(solution)/shard_map/ppermute | solution.py:46
  81.7 3.2 %collective-permute-start.20 = (bf16[64,4096]{1,0:T(8,128)(2,1)S(1)}, bf16[64,4096]{1,0:T(8,128)(2,1)S(1)}, u32[]{:S(2)}, u32[]{:S(2)}) collective-permute-start(bf16[64,4096]{1,0:T(8,128)(2,1)S(1)} %get-tuple-element.49), channel_id=1, source_target_pairs={{0,48},{1,49},{2,50},{3,51},{4,52},{5,53},{6,54},{7,55},{8,56},{9,... | collective-permute-start | bytes 1572872 | tf_op jit(solution)/shard_map/ppermute | solution.py:46
  84.9 9.2 %collective-permute-done.27.refs_0_ = bf16[64,4096]{1,0:T(8,128)(2,1)} collective-permute-done((bf16[64,4096]{1,0:T(8,128)(2,1)}, bf16[64,4096]{1,0:T(8,128)(2,1)}, u32[]{:S(2)}, u32[]{:S(2)}) %collective-permute-start.27) | collective-permute-done | bytes 524320 | tf_op jit(solution)/shard_map/ppermute | solution.py:46
  94.2 1.6 collective-permute-done.19.refs_7_.refs_11_
  96.0 5.2 %collective-permute-done.20.refs_8_.refs_12_ = bf16[64,4096]{1,0:T(8,128)(2,1)S(1)} collective-permute-done((bf16[64,4096]{1,0:T(8,128)(2,1)S(1)}, bf16[64,4096]{1,0:T(8,128)(2,1)S(1)}, u32[]{:S(2)}, u32[]{:S(2)}) %collective-permute-start.20) | collective-permute-done | bytes 524320 | tf_op jit(solution)/shard_map/ppermute | solution.py:46
  101.1 3.7 %collective-permute-done.21.refs_9_.refs_13_ = bf16[64,4096]{1,0:T(8,128)(2,1)S(1)} collective-permute-done((bf16[64,4096]{1,0:T(8,128)(2,1)S(1)}, bf16[64,4096]{1,0:T(8,128)(2,1)S(1)}, u32[]{:S(2)}, u32[]{:S(2)}) %collective-permute-start.21) | collective-permute-done | bytes 524320 | tf_op jit(solution)/shard_map/ppermute | solution.py:46
  104.8 2.5 collective-permute-start.37
  107.5 0.9 collective-permute-start.22
  108.4 2.1 collective-permute-done.18.refs_6_.refs_10_
  110.6 1.7 collective-permute-start.29
  112.3 2.0 collective-permute-done.37.refs_1_
  114.4 5.5 %collective-permute-done.29.refs_2_ = bf16[64,4096]{1,0:T(8,128)(2,1)} collective-permute-done((bf16[64,4096]{1,0:T(8,128)(2,1)S(1)}, bf16[64,4096]{1,0:T(8,128)(2,1)}, u32[]{:S(2)}, u32[]{:S(2)}) %collective-permute-start.29) | collective-permute-done | bytes 524320 | tf_op jit(solution)/shard_map/ppermute | solution.py:46
  119.9 3.2 %collective-permute-start.24 = (bf16[128,4096]{1,0:T(8,128)(2,1)S(1)}, bf16[128,4096]{1,0:T(8,128)(2,1)S(1)}, u32[]{:S(2)}, u32[]{:S(2)}) collective-permute-start(bf16[128,4096]{1,0:T(8,128)(2,1)S(1)} %pad_maximum_fusion.1), channel_id=1, source_target_pairs={{0,48},{1,49},{2,50},{3,51},{4,52},{5,53},{6,54},{7,55},{8,56},{9,... | collective-permute-start | bytes 3145736 | tf_op jit(solution)/shard_map/ppermute | solution.py:46
  123.2 1.3 collective-permute-start.25
  124.4 22.0 %collective-permute-done.23.refs_11_.refs_15_ = bf16[128,4096]{1,0:T(8,128)(2,1)S(1)} collective-permute-done((bf16[128,4096]{1,0:T(8,128)(2,1)S(1)}, bf16[128,4096]{1,0:T(8,128)(2,1)S(1)}, u32[]{:S(2)}, u32[]{:S(2)}) %collective-permute-start.23) | collective-permute-done | bytes 1048608 | tf_op jit(solution)/shard_map/ppermute | solution.py:46
  146.4 16.5 %collective-permute-done.24.refs_12_.refs_16_ = bf16[128,4096]{1,0:T(8,128)(2,1)S(1)} collective-permute-done((bf16[128,4096]{1,0:T(8,128)(2,1)S(1)}, bf16[128,4096]{1,0:T(8,128)(2,1)S(1)}, u32[]{:S(2)}, u32[]{:S(2)}) %collective-permute-start.24) | collective-permute-done | bytes 1048608 | tf_op jit(solution)/shard_map/ppermute | solution.py:46
  163.0 1.5 collective-permute-done.25.refs_13_.refs_17_
  164.6 0.9 copy-done.4
  165.5 10.4 %shard_map.86.refs_14_ = f32[256,4096]{1,0:T(8,128)} custom-call(bf16[64,4096]{1,0:T(8,128)(2,1)} %copy-done.12, bf16[64,4096]{1,0:T(8,128)(2,1)} %copy-done.13, bf16[64,4096]{1,0:T(8,128)(2,1)} %copy-done.16, bf16[64,4096]{1,0:T(8,128)(2,1)} %copy-done.17, bf16[768,4096]{1,0:T(8,128)(2,1)} %refs_4_.3, bf16[768,4096]{1,0:T(8,128)(2,1)} %refs_5_.3), custom_call_target="tpu_custom_call" | custom-call | flops 3221225472 | bytes 18874368 | tf_op jit(solution)/shard_map/pallas_call | solution.py:278
  176.0 10.9 %shard_map.87 = (bf16[128,4096]{1,0:T(8,128)(2,1)}, bf16[128,4096]{1,0:T(8,128)(2,1)}) custom-call(bf16[64,4096]{1,0:T(8,128)(2,1)} %copy-done.12, bf16[64,4096]{1,0:T(8,128)(2,1)} %copy-done.13, bf16[64,4096]{1,0:T(8,128)(2,1)} %copy-done.16, bf16[64,4096]{1,0:T(8,128)(2,1)} %copy-done.17, bf16[128,4096]{1,0:T(8,128)(2,1)} %copy-done.1, ...), custom_call_target="tpu_custom_call" | custom-call | flops 3221225472 | bytes 18874368 | tf_op jit(solution)/shard_map/pallas_call | solution.py:278
  186.9 0.6 collective-permute-start.15
  187.6 13.8 %shard_map.84.refs_18_ = f32[512,4096]{1,0:T(8,128)} custom-call(bf16[64,4096]{1,0:T(8,128)(2,1)} %collective-permute-done.27.refs_0_, bf16[64,4096]{1,0:T(8,128)(2,1)} %collective-permute-done.28.refs_1_, bf16[64,4096]{1,0:T(8,128)(2,1)} %collective-permute-done.29.refs_2_, bf16[64,4096]{1,0:T(8,128)(2,1)} %collective-permute-done.30.refs_3_, ...), custom_call_target="tpu_custom_call" | custom-call | flops 6442450944 | bytes 25165824 | tf_op jit(solution)/shard_map/pallas_call | solution.py:278
  201.5 15.1 %shard_map.85 = (bf16[128,4096]{1,0:T(8,128)(2,1)}, bf16[128,4096]{1,0:T(8,128)(2,1)}, bf16[128,4096]{1,0:T(8,128)(2,1)}, bf16[128,4096]{1,0:T(8,128)(2,1)}) custom-call(bf16[64,4096]{1,0:T(8,128)(2,1)} %collective-permute-done.27.refs_0_, bf16[64,4096]{1,0:T(8,128)(2,1)} %collective-permute-done.28.refs_1_, ...), custom_call_target="tpu_custom_call" | custom-call | flops 6442450944 | bytes 25165824 | tf_op jit(solution)/shard_map/pallas_call | solution.py:278
  216.6 0.5 collective-permute-start.43
  217.1 1.5 add_convert_fusion.2
  218.6 1.1 fusion.1
  219.7 2.8 collective-permute-start.44
  222.4 0.8 copy-done.14
  223.2 0.8 copy-done.15
  224.0 9.7 %shard_map.82.refs_14_ = f32[256,4096]{1,0:T(8,128)} custom-call(bf16[64,4096]{1,0:T(8,128)(2,1)} %get-tuple-element.35.refs_0_, bf16[64,4096]{1,0:T(8,128)(2,1)} %get-tuple-element.36.refs_1_, bf16[64,4096]{1,0:T(8,128)(2,1)} %copy-done.14, bf16[64,4096]{1,0:T(8,128)(2,1)} %copy-done.15, bf16[768,4096]{1,0:T(8,128)(2,1)} %refs_4_.3, bf16[768,4096]{1,0:T(8,128)(2,1)} %refs_5_.3), custom_call_target="tpu_custom_call" | custom-call | flops 3221225472 | bytes 18874368 | tf_op jit(solution)/shard_map/pallas_call | solution.py:278
  234.1 11.1 %shard_map.83 = (bf16[128,4096]{1,0:T(8,128)(2,1)}, bf16[128,4096]{1,0:T(8,128)(2,1)}) custom-call(bf16[64,4096]{1,0:T(8,128)(2,1)} %get-tuple-element.35.refs_0_, bf16[64,4096]{1,0:T(8,128)(2,1)} %get-tuple-element.36.refs_1_, bf16[64,4096]{1,0:T(8,128)(2,1)} %copy-done.14, bf16[64,4096]{1,0:T(8,128)(2,1)} %copy-done.15, bf16[128,4096]{1,0:T(8,128)(2,1)} %copy-done.1, ...), custom_call_target="tpu_custom_call" | custom-call | flops 3221225472 | bytes 18874368 | tf_op jit(solution)/shard_map/pallas_call | solution.py:278
  245.2 0.6 collective-permute-start.26
  245.8 1.4 add_convert_fusion
  247.2 3.3 %collective-permute-start.45 = (bf16[128,4096]{1,0:T(8,128)(2,1)S(1)}, bf16[128,4096]{1,0:T(8,128)(2,1)S(1)}, u32[]{:S(2)}, u32[]{:S(2)}) collective-permute-start(bf16[128,4096]{1,0:T(8,128)(2,1)S(1)} %add_convert_fusion), channel_id=1, source_target_pairs={{0,12},{1,13},{2,14},{3,15},{4,0},{5,1},{6,2},{7,3},{8,4},{9,5},{1... | collective-permute-start | bytes 3145736 | tf_op jit(solution)/shard_map/ppermute | solution.py:46
  250.5 10.4 %collective-permute-done.41 = bf16[64,4096]{1,0:T(8,128)(2,1)S(1)} collective-permute-done((bf16[64,4096]{1,0:T(8,128)(2,1)S(1)}, bf16[64,4096]{1,0:T(8,128)(2,1)S(1)}, u32[]{:S(2)}, u32[]{:S(2)}) %collective-permute-start.41) | collective-permute-done | bytes 524320 | tf_op jit(solution)/shard_map/ppermute | solution.py:46
  260.9 0.3 add_convert_fusion.1
  262.0 10.9 %collective-permute-done.45 = bf16[128,4096]{1,0:T(8,128)(2,1)S(1)} collective-permute-done((bf16[128,4096]{1,0:T(8,128)(2,1)S(1)}, bf16[128,4096]{1,0:T(8,128)(2,1)S(1)}, u32[]{:S(2)}, u32[]{:S(2)}) %collective-permute-start.45) | collective-permute-done | bytes 1048608 | tf_op jit(solution)/shard_map/ppermute | solution.py:46
  272.8 13.9 %collective-permute-done.42 = bf16[128,4096]{1,0:T(8,128)(2,1)S(1)} collective-permute-done((bf16[128,4096]{1,0:T(8,128)(2,1)S(1)}, bf16[128,4096]{1,0:T(8,128)(2,1)S(1)}, u32[]{:S(2)}, u32[]{:S(2)}) %collective-permute-start.42) | collective-permute-done | bytes 1048608 | tf_op jit(solution)/shard_map/ppermute | solution.py:46
  286.8 1.9 fusion
  (117 shorter events, 2.2 us)
Async XLA Ops:
  0.7 28.9 %copy-start.32 = (s32[16]{0:T(128)S(1)}, s32[16]{0:T(128)}, u32[]{:S(2)}) copy-start(s32[16]{0:T(128)} %param.11) | copy-start | bytes 196
  5.2 8.2 %collective-permute-start = (bf16[32,4096]{1,0:T(8,128)(2,1)}, bf16[32,4096]{1,0:T(8,128)(2,1)S(1)}, u32[]{:S(2)}, u32[]{:S(2)}) collective-permute-start(bf16[32,4096]{1,0:T(8,128)(2,1)} %get-tuple-element.26), channel_id=1, source_target_pairs={{0,64},{1,65},{2,66},{3,67},{4,68},{5,69},{6,70},{7,71},{8,72},{9,... | collective-permute-start | bytes 786440 | tf_op jit(solution)/shard_map/ppermute | solution.py:46
  6.9 22.7 %collective-permute-start.1 = (bf16[32,4096]{1,0:T(8,128)(2,1)}, bf16[32,4096]{1,0:T(8,128)(2,1)S(1)}, u32[]{:S(2)}, u32[]{:S(2)}) collective-permute-start(bf16[32,4096]{1,0:T(8,128)(2,1)} %get-tuple-element.27), channel_id=1, source_target_pairs={{0,48},{1,49},{2,50},{3,51},{4,52},{5,53},{6,54},{7,55},{8,56},{9,... | collective-permute-start | bytes 786440 | tf_op jit(solution)/shard_map/ppermute | solution.py:46
  9.9 24.1 %collective-permute-start.2 = (bf16[32,4096]{1,0:T(8,128)(2,1)}, bf16[32,4096]{1,0:T(8,128)(2,1)S(1)}, u32[]{:S(2)}, u32[]{:S(2)}) collective-permute-start(bf16[32,4096]{1,0:T(8,128)(2,1)} %get-tuple-element.28), channel_id=1, source_target_pairs={{0,16},{1,17},{2,18},{3,19},{4,20},{5,21},{6,22},{7,23},{8,24},{9,... | collective-permute-start | bytes 786440 | tf_op jit(solution)/shard_map/ppermute | solution.py:46
  9.9 26.3 %collective-permute-start.3 = (bf16[32,4096]{1,0:T(8,128)(2,1)}, bf16[32,4096]{1,0:T(8,128)(2,1)S(1)}, u32[]{:S(2)}, u32[]{:S(2)}) collective-permute-start(bf16[32,4096]{1,0:T(8,128)(2,1)} %get-tuple-element.29), channel_id=1, source_target_pairs={{0,112},{1,113},{2,114},{3,115},{4,116},{5,117},{6,118},{7,119},{8... | collective-permute-start | bytes 786440 | tf_op jit(solution)/shard_map/ppermute | solution.py:46
  13.1 23.1 %collective-permute-start.4 = (bf16[32,4096]{1,0:T(8,128)(2,1)}, bf16[32,4096]{1,0:T(8,128)(2,1)S(1)}, u32[]{:S(2)}, u32[]{:S(2)}) collective-permute-start(bf16[32,4096]{1,0:T(8,128)(2,1)} %get-tuple-element.30), channel_id=1, source_target_pairs={{0,80},{1,81},{2,82},{3,83},{4,84},{5,85},{6,86},{7,87},{8,88},{9,... | collective-permute-start | bytes 786440 | tf_op jit(solution)/shard_map/ppermute | solution.py:46
  13.4 22.8 %collective-permute-start.5 = (bf16[32,4096]{1,0:T(8,128)(2,1)}, bf16[32,4096]{1,0:T(8,128)(2,1)S(1)}, u32[]{:S(2)}, u32[]{:S(2)}) collective-permute-start(bf16[32,4096]{1,0:T(8,128)(2,1)} %get-tuple-element.31), channel_id=1, source_target_pairs={{0,32},{1,33},{2,34},{3,35},{4,36},{5,37},{6,38},{7,39},{8,40},{9,... | collective-permute-start | bytes 786440 | tf_op jit(solution)/shard_map/ppermute | solution.py:46
  29.5 11.4 %collective-permute-start.6 = (bf16[32,4096]{1,0:T(8,128)(2,1)}, bf16[32,4096]{1,0:T(8,128)(2,1)S(1)}, u32[]{:S(2)}, u32[]{:S(2)}) collective-permute-start(bf16[32,4096]{1,0:T(8,128)(2,1)} %get-tuple-element.32), channel_id=1, source_target_pairs={{0,96},{1,97},{2,98},{3,99},{4,100},{5,101},{6,102},{7,103},{8,104... | collective-permute-start | bytes 786440 | tf_op jit(solution)/shard_map/ppermute | solution.py:46
  34.0 47.6 %collective-permute-start.16 = (bf16[128,4096]{1,0:T(8,128)(2,1)}, bf16[128,4096]{1,0:T(8,128)(2,1)S(1)}, u32[]{:S(2)}, u32[]{:S(2)}) collective-permute-start(bf16[128,4096]{1,0:T(8,128)(2,1)} %get-tuple-element.37), channel_id=1, source_target_pairs={{0,66},{1,67},{2,64},{3,65},{4,70},{5,71},{6,68},{7,69},{8,74},{9,... | collective-permute-start | bytes 3145736 | tf_op jit(solution)/shard_map/ppermute | solution.py:46
  42.0 21.6 %copy-start.23 = (bf16[32,4096]{1,0:T(8,128)(2,1)}, bf16[32,4096]{1,0:T(8,128)(2,1)S(1)}, u32[]{:S(2)}) copy-start(bf16[32,4096]{1,0:T(8,128)(2,1)S(1)} %select_select_fusion.refs_0_) | copy-start | bytes 786436
  42.0 9.0 %collective-permute-start.7 = (bf16[32,4096]{1,0:T(8,128)(2,1)S(1)}, bf16[32,4096]{1,0:T(8,128)(2,1)S(1)}, u32[]{:S(2)}, u32[]{:S(2)}) collective-permute-start(bf16[32,4096]{1,0:T(8,128)(2,1)S(1)} %select_select_fusion.refs_0_), channel_id=1, source_target_pairs={{0,96},{1,97},{2,98},{3,99},{4,100},{5,101},{6,102},{7,103},{8,104... | collective-permute-start | bytes 786440 | tf_op jit(solution)/shard_map/ppermute | solution.py:46
  42.1 16.1 %collective-permute-start.8 = (bf16[32,4096]{1,0:T(8,128)(2,1)S(1)}, bf16[32,4096]{1,0:T(8,128)(2,1)S(1)}, u32[]{:S(2)}, u32[]{:S(2)}) collective-permute-start(bf16[32,4096]{1,0:T(8,128)(2,1)S(1)} %select_select_fusion.refs_0_), channel_id=1, source_target_pairs={{0,32},{1,33},{2,34},{3,35},{4,36},{5,37},{6,38},{7,39},{8,40},{9,... | collective-permute-start | bytes 786440 | tf_op jit(solution)/shard_map/ppermute | solution.py:46
  44.4 14.8 %collective-permute-start.9 = (bf16[32,4096]{1,0:T(8,128)(2,1)S(1)}, bf16[32,4096]{1,0:T(8,128)(2,1)S(1)}, u32[]{:S(2)}, u32[]{:S(2)}) collective-permute-start(bf16[32,4096]{1,0:T(8,128)(2,1)S(1)} %select_select_fusion.refs_0_), channel_id=1, source_target_pairs={{0,80},{1,81},{2,82},{3,83},{4,84},{5,85},{6,86},{7,87},{8,88},{9,... | collective-permute-start | bytes 786440 | tf_op jit(solution)/shard_map/ppermute | solution.py:46
  47.0 17.8 %collective-permute-start.10 = (bf16[32,4096]{1,0:T(8,128)(2,1)S(1)}, bf16[32,4096]{1,0:T(8,128)(2,1)S(1)}, u32[]{:S(2)}, u32[]{:S(2)}) collective-permute-start(bf16[32,4096]{1,0:T(8,128)(2,1)S(1)} %select_select_fusion.refs_0_), channel_id=1, source_target_pairs={{0,112},{1,113},{2,114},{3,115},{4,116},{5,117},{6,118},{7,119},{8... | collective-permute-start | bytes 786440 | tf_op jit(solution)/shard_map/ppermute | solution.py:46
  51.0 12.6 %copy-start.25 = (bf16[32,4096]{1,0:T(8,128)(2,1)}, bf16[32,4096]{1,0:T(8,128)(2,1)S(1)}, u32[]{:S(2)}) copy-start(bf16[32,4096]{1,0:T(8,128)(2,1)S(1)} %collective-permute-done.7.refs_1_) | copy-start | bytes 786436
  51.0 17.2 %collective-permute-start.11 = (bf16[32,4096]{1,0:T(8,128)(2,1)S(1)}, bf16[32,4096]{1,0:T(8,128)(2,1)S(1)}, u32[]{:S(2)}, u32[]{:S(2)}) collective-permute-start(bf16[32,4096]{1,0:T(8,128)(2,1)S(1)} %select_select_fusion.refs_0_), channel_id=1, source_target_pairs={{0,16},{1,17},{2,18},{3,19},{4,20},{5,21},{6,22},{7,23},{8,24},{9,... | collective-permute-start | bytes 786440 | tf_op jit(solution)/shard_map/ppermute | solution.py:46
  58.2 10.0 %collective-permute-start.12 = (bf16[32,4096]{1,0:T(8,128)(2,1)S(1)}, bf16[32,4096]{1,0:T(8,128)(2,1)S(1)}, u32[]{:S(2)}, u32[]{:S(2)}) collective-permute-start(bf16[32,4096]{1,0:T(8,128)(2,1)S(1)} %select_select_fusion.refs_0_), channel_id=1, source_target_pairs={{0,48},{1,49},{2,50},{3,51},{4,52},{5,53},{6,54},{7,55},{8,56},{9,... | collective-permute-start | bytes 786440 | tf_op jit(solution)/shard_map/ppermute | solution.py:46
  59.2 9.0 %collective-permute-start.13 = (bf16[32,4096]{1,0:T(8,128)(2,1)S(1)}, bf16[32,4096]{1,0:T(8,128)(2,1)S(1)}, u32[]{:S(2)}, u32[]{:S(2)}) collective-permute-start(bf16[32,4096]{1,0:T(8,128)(2,1)S(1)} %select_select_fusion.refs_0_), channel_id=1, source_target_pairs={{0,64},{1,65},{2,66},{3,67},{4,68},{5,69},{6,70},{7,71},{8,72},{9,... | collective-permute-start | bytes 786440 | tf_op jit(solution)/shard_map/ppermute | solution.py:46
  64.8 111.1 %collective-permute-start.17 = (bf16[512,4096]{1,0:T(8,128)(2,1)}, bf16[512,4096]{1,0:T(8,128)(2,1)}, u32[]{:S(2)}, u32[]{:S(2)}) collective-permute-start(bf16[512,4096]{1,0:T(8,128)(2,1)} %direct_rows.1), channel_id=1, source_target_pairs={{0,66},{1,67},{2,64},{3,65},{4,70},{5,71},{6,68},{7,69},{8,74},{9,... | collective-permute-start | bytes 12582920 | tf_op jit(solution)/shard_map/ppermute | solution.py:46
  77.0 17.1 %copy-start.10 = (bf16[64,4096]{1,0:T(8,128)(2,1)S(1)}, bf16[64,4096]{1,0:T(8,128)(2,1)}, u32[]{:S(2)}) copy-start(bf16[64,4096]{1,0:T(8,128)(2,1)} %get-tuple-element.36.refs_1_) | copy-start | bytes 1572868
  77.0 17.1 %collective-permute-start.27 = (bf16[64,4096]{1,0:T(8,128)(2,1)}, bf16[64,4096]{1,0:T(8,128)(2,1)}, u32[]{:S(2)}, u32[]{:S(2)}) collective-permute-start(bf16[64,4096]{1,0:T(8,128)(2,1)} %get-tuple-element.35.refs_0_), channel_id=1, source_target_pairs={{0,4},{1,5},{2,6},{3,7},{4,8},{5,9},{6,10},{7,11},{8,12},{9,13},{1... | collective-permute-start | bytes 1572872 | tf_op jit(solution)/shard_map/ppermute | solution.py:46
  78.7 15.5 %collective-permute-start.30 = (bf16[64,4096]{1,0:T(8,128)(2,1)}, bf16[64,4096]{1,0:T(8,128)(2,1)}, u32[]{:S(2)}, u32[]{:S(2)}) collective-permute-start(bf16[64,4096]{1,0:T(8,128)(2,1)} %get-tuple-element.36.refs_1_), channel_id=1, source_target_pairs={{0,12},{1,13},{2,14},{3,15},{4,0},{5,1},{6,2},{7,3},{8,4},{9,5},{1... | collective-permute-start | bytes 1572872 | tf_op jit(solution)/shard_map/ppermute | solution.py:46
  81.6 25.9 %copy-start.1 = (bf16[128,4096]{1,0:T(8,128)(2,1)}, bf16[128,4096]{1,0:T(8,128)(2,1)S(1)}, u32[]{:S(2)}) copy-start(bf16[128,4096]{1,0:T(8,128)(2,1)S(1)} %collective-permute-done.16.refs_4_.refs_8_) | copy-start | bytes 3145732
  81.6 14.1 %collective-permute-start.19 = (bf16[64,4096]{1,0:T(8,128)(2,1)S(1)}, bf16[64,4096]{1,0:T(8,128)(2,1)S(1)}, u32[]{:S(2)}, u32[]{:S(2)}) collective-permute-start(bf16[64,4096]{1,0:T(8,128)(2,1)S(1)} %get-tuple-element.49), channel_id=1, source_target_pairs={{0,16},{1,17},{2,18},{3,19},{4,20},{5,21},{6,22},{7,23},{8,24},{9,... | collective-permute-start | bytes 1572872 | tf_op jit(solution)/shard_map/ppermute | solution.py:46
  81.7 19.4 %collective-permute-start.20 = (bf16[64,4096]{1,0:T(8,128)(2,1)S(1)}, bf16[64,4096]{1,0:T(8,128)(2,1)S(1)}, u32[]{:S(2)}, u32[]{:S(2)}) collective-permute-start(bf16[64,4096]{1,0:T(8,128)(2,1)S(1)} %get-tuple-element.49), channel_id=1, source_target_pairs={{0,48},{1,49},{2,50},{3,51},{4,52},{5,53},{6,54},{7,55},{8,56},{9,... | collective-permute-start | bytes 1572872 | tf_op jit(solution)/shard_map/ppermute | solution.py:46
  94.1 10.7 %collective-permute-start.21 = (bf16[64,4096]{1,0:T(8,128)(2,1)S(1)}, bf16[64,4096]{1,0:T(8,128)(2,1)S(1)}, u32[]{:S(2)}, u32[]{:S(2)}) collective-permute-start(bf16[64,4096]{1,0:T(8,128)(2,1)S(1)} %get-tuple-element.49), channel_id=1, source_target_pairs={{0,32},{1,33},{2,34},{3,35},{4,36},{5,37},{6,38},{7,39},{8,40},{9,... | collective-permute-start | bytes 1572872 | tf_op jit(solution)/shard_map/ppermute | solution.py:46
  94.1 13.4 %collective-permute-start.28 = (bf16[64,4096]{1,0:T(8,128)(2,1)S(1)}, bf16[64,4096]{1,0:T(8,128)(2,1)}, u32[]{:S(2)}, u32[]{:S(2)}) collective-permute-start(bf16[64,4096]{1,0:T(8,128)(2,1)S(1)} %copy-done.10), channel_id=1, source_target_pairs={{0,4},{1,5},{2,6},{3,7},{4,8},{5,9},{6,10},{7,11},{8,12},{9,13},{1... | collective-permute-start | bytes 1572872 | tf_op jit(solution)/shard_map/ppermute | solution.py:46
  95.8 14.8 %copy-start.9 = (bf16[64,4096]{1,0:T(8,128)(2,1)S(1)}, bf16[64,4096]{1,0:T(8,128)(2,1)}, u32[]{:S(2)}) copy-start(bf16[64,4096]{1,0:T(8,128)(2,1)} %get-tuple-element.35.refs_0_) | copy-start | bytes 1572868
  95.8 14.8 %collective-permute-start.18 = (bf16[64,4096]{1,0:T(8,128)(2,1)S(1)}, bf16[64,4096]{1,0:T(8,128)(2,1)S(1)}, u32[]{:S(2)}, u32[]{:S(2)}) collective-permute-start(bf16[64,4096]{1,0:T(8,128)(2,1)S(1)} %get-tuple-element.50), channel_id=1, source_target_pairs={{0,64},{1,65},{2,66},{3,67},{4,68},{5,69},{6,70},{7,71},{8,72},{9,... | collective-permute-start | bytes 1572872 | tf_op jit(solution)/shard_map/ppermute | solution.py:46
  101.1 11.2 %collective-permute-start.36 = (bf16[64,4096]{1,0:T(8,128)(2,1)}, bf16[64,4096]{1,0:T(8,128)(2,1)S(1)}, u32[]{:S(2)}, u32[]{:S(2)}) collective-permute-start(bf16[64,4096]{1,0:T(8,128)(2,1)} %collective-permute-done.27.refs_0_), channel_id=1, source_target_pairs={{0,4},{1,5},{2,6},{3,7},{4,8},{5,9},{6,10},{7,11},{8,12},{9,13},{1... | collective-permute-start | bytes 1572872 | tf_op jit(solution)/shard_map/ppermute | solution.py:46
  104.8 9.5 %collective-permute-start.37 = (bf16[64,4096]{1,0:T(8,128)(2,1)}, bf16[64,4096]{1,0:T(8,128)(2,1)S(1)}, u32[]{:S(2)}, u32[]{:S(2)}) collective-permute-start(bf16[64,4096]{1,0:T(8,128)(2,1)} %collective-permute-done.30.refs_3_), channel_id=1, source_target_pairs={{0,12},{1,13},{2,14},{3,15},{4,0},{5,1},{6,2},{7,3},{8,4},{9,5},{1... | collective-permute-start | bytes 1572872 | tf_op jit(solution)/shard_map/ppermute | solution.py:46
  107.5 57.0 %collective-permute-start.22 = (bf16[256,4096]{1,0:T(8,128)(2,1)S(1)}, bf16[256,4096]{1,0:T(8,128)(2,1)S(1)}, u32[]{:S(2)}, u32[]{:S(2)}) collective-permute-start(bf16[256,4096]{1,0:T(8,128)(2,1)S(1)} %pad_maximum_fusion), channel_id=1, source_target_pairs={{0,64},{1,65},{2,66},{3,67},{4,68},{5,69},{6,70},{7,71},{8,72},{9,... | collective-permute-start | bytes 6291464 | tf_op jit(solution)/shard_map/ppermute | solution.py:46
  110.6 65.3 %copy-start.5 = (bf16[64,4096]{1,0:T(8,128)(2,1)}, bf16[64,4096]{1,0:T(8,128)(2,1)S(1)}, u32[]{:S(2)}) copy-start(bf16[64,4096]{1,0:T(8,128)(2,1)S(1)} %collective-permute-done.18.refs_6_.refs_10_) | copy-start | bytes 1572868
  110.6 9.3 %collective-permute-start.29 = (bf16[64,4096]{1,0:T(8,128)(2,1)S(1)}, bf16[64,4096]{1,0:T(8,128)(2,1)}, u32[]{:S(2)}, u32[]{:S(2)}) collective-permute-start(bf16[64,4096]{1,0:T(8,128)(2,1)S(1)} %copy-done.9), channel_id=1, source_target_pairs={{0,12},{1,13},{2,14},{3,15},{4,0},{5,1},{6,2},{7,3},{8,4},{9,5},{1... | collective-permute-start | bytes 1572872 | tf_op jit(solution)/shard_map/ppermute | solution.py:46
  112.3 52.2 %copy-start.12 = (bf16[64,4096]{1,0:T(8,128)(2,1)}, bf16[64,4096]{1,0:T(8,128)(2,1)S(1)}, u32[]{:S(2)}) copy-start(bf16[64,4096]{1,0:T(8,128)(2,1)S(1)} %collective-permute-done.36.refs_0_) | copy-start | bytes 1572868
  112.3 7.6 %collective-permute-start.38 = (bf16[64,4096]{1,0:T(8,128)(2,1)S(1)}, bf16[64,4096]{1,0:T(8,128)(2,1)S(1)}, u32[]{:S(2)}, u32[]{:S(2)}) collective-permute-start(bf16[64,4096]{1,0:T(8,128)(2,1)S(1)} %collective-permute-done.36.refs_0_), channel_id=1, source_target_pairs={{0,1},{1,0},{2,3},{3,2},{4,5},{5,4},{6,7},{7,6},{8,9},{9,8},{10,11... | collective-permute-start | bytes 1572872 | tf_op jit(solution)/shard_map/ppermute | solution.py:46
  114.3 50.3 %copy-start.13 = (bf16[64,4096]{1,0:T(8,128)(2,1)}, bf16[64,4096]{1,0:T(8,128)(2,1)S(1)}, u32[]{:S(2)}) copy-start(bf16[64,4096]{1,0:T(8,128)(2,1)S(1)} %collective-permute-done.37.refs_1_) | copy-start | bytes 1572868
  114.3 8.9 %collective-permute-start.39 = (bf16[64,4096]{1,0:T(8,128)(2,1)S(1)}, bf16[64,4096]{1,0:T(8,128)(2,1)S(1)}, u32[]{:S(2)}, u32[]{:S(2)}) collective-permute-start(bf16[64,4096]{1,0:T(8,128)(2,1)S(1)} %collective-permute-done.37.refs_1_), channel_id=1, source_target_pairs={{0,1},{1,0},{2,3},{3,2},{4,5},{5,4},{6,7},{7,6},{8,9},{9,8},{10,11... | collective-permute-start | bytes 1572872 | tf_op jit(solution)/shard_map/ppermute | solution.py:46
  119.9 26.5 %collective-permute-start.23 = (bf16[128,4096]{1,0:T(8,128)(2,1)S(1)}, bf16[128,4096]{1,0:T(8,128)(2,1)S(1)}, u32[]{:S(2)}, u32[]{:S(2)}) collective-permute-start(bf16[128,4096]{1,0:T(8,128)(2,1)S(1)} %pad_maximum_fusion.1), channel_id=1, source_target_pairs={{0,16},{1,17},{2,18},{3,19},{4,20},{5,21},{6,22},{7,23},{8,24},{9,... | collective-permute-start | bytes 3145736 | tf_op jit(solution)/shard_map/ppermute | solution.py:46
  119.9 44.6 %copy-start.16 = (bf16[64,4096]{1,0:T(8,128)(2,1)}, bf16[64,4096]{1,0:T(8,128)(2,1)S(1)}, u32[]{:S(2)}) copy-start(bf16[64,4096]{1,0:T(8,128)(2,1)S(1)} %collective-permute-done.38.refs_2_) | copy-start | bytes 1572868
  119.9 43.1 %collective-permute-start.24 = (bf16[128,4096]{1,0:T(8,128)(2,1)S(1)}, bf16[128,4096]{1,0:T(8,128)(2,1)S(1)}, u32[]{:S(2)}, u32[]{:S(2)}) collective-permute-start(bf16[128,4096]{1,0:T(8,128)(2,1)S(1)} %pad_maximum_fusion.1), channel_id=1, source_target_pairs={{0,48},{1,49},{2,50},{3,51},{4,52},{5,53},{6,54},{7,55},{8,56},{9,... | collective-permute-start | bytes 3145736 | tf_op jit(solution)/shard_map/ppermute | solution.py:46
  123.2 41.4 %copy-start.17 = (bf16[64,4096]{1,0:T(8,128)(2,1)}, bf16[64,4096]{1,0:T(8,128)(2,1)S(1)}, u32[]{:S(2)}) copy-start(bf16[64,4096]{1,0:T(8,128)(2,1)S(1)} %collective-permute-done.39.refs_3_) | copy-start | bytes 1572868
  123.2 41.4 %collective-permute-start.25 = (bf16[128,4096]{1,0:T(8,128)(2,1)S(1)}, bf16[128,4096]{1,0:T(8,128)(2,1)S(1)}, u32[]{:S(2)}, u32[]{:S(2)}) collective-permute-start(bf16[128,4096]{1,0:T(8,128)(2,1)S(1)} %pad_maximum_fusion.1), channel_id=1, source_target_pairs={{0,32},{1,33},{2,34},{3,35},{4,36},{5,37},{6,38},{7,39},{8,40},{9,... | collective-permute-start | bytes 3145736 | tf_op jit(solution)/shard_map/ppermute | solution.py:46
  146.4 29.5 %copy-start.2 = (bf16[128,4096]{1,0:T(8,128)(2,1)}, bf16[128,4096]{1,0:T(8,128)(2,1)S(1)}, u32[]{:S(2)}) copy-start(bf16[128,4096]{1,0:T(8,128)(2,1)S(1)} %collective-permute-done.23.refs_11_.refs_15_) | copy-start | bytes 3145732
  146.4 40.5 %collective-permute-start.31 = (bf16[64,4096]{1,0:T(8,128)(2,1)}, bf16[64,4096]{1,0:T(8,128)(2,1)}, u32[]{:S(2)}, u32[]{:S(2)}) collective-permute-start(bf16[64,4096]{1,0:T(8,128)(2,1)} %collective-permute-done.27.refs_0_), channel_id=1, source_target_pairs={{0,1},{1,0},{2,3},{3,2},{4,5},{5,4},{6,7},{7,6},{8,9},{9,8},{10,11... | collective-permute-start | bytes 1572872 | tf_op jit(solution)/shard_map/ppermute | solution.py:46
  163.0 24.6 %collective-permute-start.34 = (bf16[64,4096]{1,0:T(8,128)(2,1)}, bf16[64,4096]{1,0:T(8,128)(2,1)}, u32[]{:S(2)}, u32[]{:S(2)}) collective-permute-start(bf16[64,4096]{1,0:T(8,128)(2,1)} %collective-permute-done.30.refs_3_), channel_id=1, source_target_pairs={{0,1},{1,0},{2,3},{3,2},{4,5},{5,4},{6,7},{7,6},{8,9},{9,8},{10,11... | collective-permute-start | bytes 1572872 | tf_op jit(solution)/shard_map/ppermute | solution.py:46
  164.5 23.0 %collective-permute-start.32 = (bf16[64,4096]{1,0:T(8,128)(2,1)}, bf16[64,4096]{1,0:T(8,128)(2,1)}, u32[]{:S(2)}, u32[]{:S(2)}) collective-permute-start(bf16[64,4096]{1,0:T(8,128)(2,1)} %collective-permute-done.28.refs_1_), channel_id=1, source_target_pairs={{0,1},{1,0},{2,3},{3,2},{4,5},{5,4},{6,7},{7,6},{8,9},{9,8},{10,11... | collective-permute-start | bytes 1572872 | tf_op jit(solution)/shard_map/ppermute | solution.py:46
  165.5 22.1 %collective-permute-start.33 = (bf16[64,4096]{1,0:T(8,128)(2,1)}, bf16[64,4096]{1,0:T(8,128)(2,1)}, u32[]{:S(2)}, u32[]{:S(2)}) collective-permute-start(bf16[64,4096]{1,0:T(8,128)(2,1)} %collective-permute-done.29.refs_2_), channel_id=1, source_target_pairs={{0,1},{1,0},{2,3},{3,2},{4,5},{5,4},{6,7},{7,6},{8,9},{9,8},{10,11... | collective-permute-start | bytes 1572872 | tf_op jit(solution)/shard_map/ppermute | solution.py:46
  175.9 46.5 %collective-permute-start.14 = (bf16[64,4096]{1,0:T(8,128)(2,1)}, bf16[64,4096]{1,0:T(8,128)(2,1)S(1)}, u32[]{:S(2)}, u32[]{:S(2)}) collective-permute-start(bf16[64,4096]{1,0:T(8,128)(2,1)} %get-tuple-element.35.refs_0_), channel_id=1, source_target_pairs={{0,1},{1,0},{2,3},{3,2},{4,5},{5,4},{6,7},{7,6},{8,9},{9,8},{10,11... | collective-permute-start | bytes 1572872 | tf_op jit(solution)/shard_map/ppermute | solution.py:46
  186.9 35.5 %collective-permute-start.15 = (bf16[64,4096]{1,0:T(8,128)(2,1)S(1)}, bf16[64,4096]{1,0:T(8,128)(2,1)S(1)}, u32[]{:S(2)}, u32[]{:S(2)}) collective-permute-start(bf16[64,4096]{1,0:T(8,128)(2,1)S(1)} %copy-done.11), channel_id=1, source_target_pairs={{0,1},{1,0},{2,3},{3,2},{4,5},{5,4},{6,7},{7,6},{8,9},{9,8},{10,11... | collective-permute-start | bytes 1572872 | tf_op jit(solution)/shard_map/ppermute | solution.py:46
  187.5 29.6 %collective-permute-start.40 = (bf16[128,4096]{1,0:T(8,128)(2,1)}, bf16[128,4096]{1,0:T(8,128)(2,1)}, u32[]{:S(2)}, u32[]{:S(2)}) collective-permute-start(bf16[128,4096]{1,0:T(8,128)(2,1)} %get-tuple-element.44), channel_id=1, source_target_pairs={{0,1},{1,0},{2,3},{3,2},{4,5},{5,4},{6,7},{7,6},{8,9},{9,8},{10,11... | collective-permute-start | bytes 3145736 | tf_op jit(solution)/shard_map/ppermute | solution.py:46
  201.4 15.6 %copy-start.22 = (bf16[128,4096]{1,0:T(8,128)(2,1)S(1)}, bf16[128,4096]{1,0:T(8,128)(2,1)}, u32[]{:S(2)}) copy-start(bf16[128,4096]{1,0:T(8,128)(2,1)} %get-tuple-element.43) | copy-start | bytes 3145732
  216.6 29.1 %collective-permute-start.43 = (bf16[128,4096]{1,0:T(8,128)(2,1)}, bf16[128,4096]{1,0:T(8,128)(2,1)S(1)}, u32[]{:S(2)}, u32[]{:S(2)}) collective-permute-start(bf16[128,4096]{1,0:T(8,128)(2,1)} %get-tuple-element.46), channel_id=1, source_target_pairs={{0,1},{1,0},{2,3},{3,2},{4,5},{5,4},{6,7},{7,6},{8,9},{9,8},{10,11... | collective-permute-start | bytes 3145736 | tf_op jit(solution)/shard_map/ppermute | solution.py:46
  219.7 26.1 %collective-permute-start.44 = (bf16[64,4096]{1,0:T(8,128)(2,1)}, bf16[64,4096]{1,0:T(8,128)(2,1)}, u32[]{:S(2)}, u32[]{:S(2)}) collective-permute-start(bf16[64,4096]{1,0:T(8,128)(2,1)} %get-tuple-element.48), channel_id=1, source_target_pairs={{0,12},{1,13},{2,14},{3,15},{4,0},{5,1},{6,2},{7,3},{8,4},{9,5},{1... | collective-permute-start | bytes 1572872 | tf_op jit(solution)/shard_map/ppermute | solution.py:46
  233.8 12.0 %copy-start.24 = (bf16[64,4096]{1,0:T(8,128)(2,1)S(1)}, bf16[64,4096]{1,0:T(8,128)(2,1)}, u32[]{:S(2)}) copy-start(bf16[64,4096]{1,0:T(8,128)(2,1)} %get-tuple-element.47) | copy-start | bytes 1572868
  233.8 12.0 %copy-start.20 = (bf16[128,4096]{1,0:T(8,128)(2,1)S(1)}, bf16[128,4096]{1,0:T(8,128)(2,1)}, u32[]{:S(2)}) copy-start(bf16[128,4096]{1,0:T(8,128)(2,1)} %get-tuple-element.45) | copy-start | bytes 3145732
  233.8 16.7 %collective-permute-start.35 = (bf16[128,4096]{1,0:T(8,128)(2,1)}, bf16[128,4096]{1,0:T(8,128)(2,1)S(1)}, u32[]{:S(2)}, u32[]{:S(2)}) collective-permute-start(bf16[128,4096]{1,0:T(8,128)(2,1)} %get-tuple-element.42), channel_id=1, source_target_pairs={{0,1},{1,0},{2,3},{3,2},{4,5},{5,4},{6,7},{7,6},{8,9},{9,8},{10,11... | collective-permute-start | bytes 3145736 | tf_op jit(solution)/shard_map/ppermute | solution.py:46
  245.2 15.7 %copy-start.19 = (bf16[128,4096]{1,0:T(8,128)(2,1)S(1)}, bf16[128,4096]{1,0:T(8,128)(2,1)}, u32[]{:S(2)}) copy-start(bf16[128,4096]{1,0:T(8,128)(2,1)} %get-tuple-element.41) | copy-start | bytes 3145732
  245.2 16.8 %collective-permute-start.26 = (bf16[128,4096]{1,0:T(8,128)(2,1)}, bf16[128,4096]{1,0:T(8,128)(2,1)S(1)}, u32[]{:S(2)}, u32[]{:S(2)}) collective-permute-start(bf16[128,4096]{1,0:T(8,128)(2,1)} %get-tuple-element.40), channel_id=1, source_target_pairs={{0,1},{1,0},{2,3},{3,2},{4,5},{5,4},{6,7},{7,6},{8,9},{9,8},{10,11... | collective-permute-start | bytes 3145736 | tf_op jit(solution)/shard_map/ppermute | solution.py:46
  245.7 15.1 %collective-permute-start.41 = (bf16[64,4096]{1,0:T(8,128)(2,1)S(1)}, bf16[64,4096]{1,0:T(8,128)(2,1)S(1)}, u32[]{:S(2)}, u32[]{:S(2)}) collective-permute-start(bf16[64,4096]{1,0:T(8,128)(2,1)S(1)} %copy-done.24), channel_id=1, source_target_pairs={{0,4},{1,5},{2,6},{3,7},{4,8},{5,9},{6,10},{7,11},{8,12},{9,13},{1... | collective-permute-start | bytes 1572872 | tf_op jit(solution)/shard_map/ppermute | solution.py:46
  247.1 39.6 %copy-start.18 = (bf16[128,4096]{1,0:T(8,128)(2,1)S(1)}, bf16[128,4096]{1,0:T(8,128)(2,1)}, u32[]{:S(2)}) copy-start(bf16[128,4096]{1,0:T(8,128)(2,1)} %get-tuple-element.34) | copy-start | bytes 3145732
  247.2 39.6 %copy-start.21 = (bf16[128,4096]{1,0:T(8,128)(2,1)S(1)}, bf16[128,4096]{1,0:T(8,128)(2,1)}, u32[]{:S(2)}) copy-start(bf16[128,4096]{1,0:T(8,128)(2,1)} %get-tuple-element.39) | copy-start | bytes 3145732
  247.2 25.7 %collective-permute-start.45 = (bf16[128,4096]{1,0:T(8,128)(2,1)S(1)}, bf16[128,4096]{1,0:T(8,128)(2,1)S(1)}, u32[]{:S(2)}, u32[]{:S(2)}) collective-permute-start(bf16[128,4096]{1,0:T(8,128)(2,1)S(1)} %add_convert_fusion), channel_id=1, source_target_pairs={{0,12},{1,13},{2,14},{3,15},{4,0},{5,1},{6,2},{7,3},{8,4},{9,5},{1... | collective-permute-start | bytes 3145736 | tf_op jit(solution)/shard_map/ppermute | solution.py:46
  261.2 25.6 %collective-permute-start.42 = (bf16[128,4096]{1,0:T(8,128)(2,1)S(1)}, bf16[128,4096]{1,0:T(8,128)(2,1)S(1)}, u32[]{:S(2)}, u32[]{:S(2)}) collective-permute-start(bf16[128,4096]{1,0:T(8,128)(2,1)S(1)} %add_convert_fusion.1), channel_id=1, source_target_pairs={{0,4},{1,5},{2,6},{3,7},{4,8},{5,9},{6,10},{7,11},{8,12},{9,13},{1... | collective-permute-start | bytes 3145736 | tf_op jit(solution)/shard_map/ppermute | solution.py:46
  (15 other events, 62.0 us)

commit v3 on v2

--- a/solution.py
+++ b/solution.py
@@ -3,6 +3,7 @@
 
 import jax
 import jax.numpy as jnp
+import numpy as np
 from jax import lax
 from jax.experimental import pallas as pl
 from jax.experimental.pallas import tpu as pltpu
@@ -13,7 +14,7 @@
 NORM_EPS = 1e-05
 AXES = ("req", "grp")
 F32, BF16 = jnp.float32, jnp.bfloat16
-VMEM_LIMIT = 60 * 1024 * 1024
+MIB = 1024 * 1024
 
 
 def pairs(move):
@@ -58,67 +59,65 @@
     return pl.BlockSpec(memory_space=pl.ANY)
 
 
-def params():
-    return pltpu.CompilerParams(vmem_limit_bytes=VMEM_LIMIT)
+def params(mib):
+    return pltpu.CompilerParams(vmem_limit_bytes=mib * MIB)
 
 
 def cost(flops, nbytes):
     return pl.CostEstimate(flops=int(flops), bytes_accessed=int(nbytes), transcendentals=0)
 
 
-def cut_kernel(index_ref, cache_ref, up_ref, down_ref, *refs):
-    outs, share, sems = refs[:8], refs[8], refs[9]
-    first = pl.multiple_of(index_ref[8] * 64, 64)
-    moves = []
-    for i, (source, row) in enumerate(((up_ref, 0), (down_ref, 0), (up_ref, 32), (down_ref, 32))):
-        part = pl.ds(pl.multiple_of(first + row, 32), 32)
-        moves.append(pltpu.make_async_copy(source.at[part, :], share.at[pl.ds(i * 32, 32), :], sems.at[i]))
-    for move in moves:
-        move.start()
-    for place in range(8):
-        row = pl.multiple_of(index_ref[place] * 32, 32)
-        outs[place][...] = cache_ref[pl.ds(row, 32), :]
-    for move in moves:
-        move.wait()
-
-
-def cut_slices(index, cache, up, down):
+def cut_kernel(index_ref, cache_ref, *outs):
+    for place, out in enumerate(outs):
+        out[...] = cache_ref[pl.ds(pl.multiple_of(index_ref[place] * 32, 32), 32), :]
+
+
+def cut_slices(index, cache):
     width = cache.shape[1]
     return pl.pallas_call(
         cut_kernel,
-        out_shape=[jax.ShapeDtypeStruct((32, width), BF16)] * 8 + [jax.ShapeDtypeStruct((128, width), BF16)],
-        in_specs=[smem(), vmem(), hbm(), hbm()],
-        out_specs=[vmem()] * 9,
-        scratch_shapes=[pltpu.SemaphoreType.DMA((4,))],
-        compiler_params=params(),
-        cost_estimate=cost(0, 6 * cache.size),
+        out_shape=[jax.ShapeDtypeStruct((32, width), BF16)] * 8,
+        in_specs=[smem(), vmem()],
+        out_specs=[vmem()] * 8,
+        compiler_params=params(8),
+        cost_estimate=cost(0, 4 * cache.size),
         name="cut_slices",
-    )(index, cache, up, down)
-
-
-def direct_kernel(up_ref, down_ref, out_ref, sems):
-    moves = [
-        pltpu.make_async_copy(up_ref.at[pl.ds(512, 256), :], out_ref.at[pl.ds(0, 256), :], sems.at[0]),
-        pltpu.make_async_copy(down_ref.at[pl.ds(512, 256), :], out_ref.at[pl.ds(256, 256), :], sems.at[1]),
-    ]
-    for move in moves:
-        move.start()
-    for move in moves:
-        move.wait()
-
-
-def direct_rows(up, down):
+    )(index, cache)
+
+
+def share_kernel(index_ref, up_ref, down_ref, first_ref, second_ref, direct_ref, sems):
+    start = index_ref[8] * 64
+    moves = []
+
+    def move(source, row, target, place, count):
+        copy = pltpu.make_async_copy(
+            source.at[pl.ds(row, count), :], target.at[pl.ds(place, count), :], sems.at[len(moves)]
+        )
+        copy.start()
+        moves.append(copy)
+
+    for i, target in enumerate((first_ref, second_ref)):
+        row = pl.multiple_of(start + 32 * i, 32)
+        move(up_ref, row, target, 0, 32)
+        move(down_ref, row, target, 32, 32)
+    move(up_ref, 512, direct_ref, 0, 256)
+    move(down_ref, 512, direct_ref, 256, 256)
+    for copy in moves:
+        copy.wait()
+
+
+def weight_shares(index, up, down):
     width = up.shape[1]
     return pl.pallas_call(
-        direct_kernel,
-        out_shape=jax.ShapeDtypeStruct((512, width), BF16),
-        in_specs=[hbm(), hbm()],
-        out_specs=vmem(),
-        scratch_shapes=[pltpu.SemaphoreType.DMA((2,))],
-        compiler_params=params(),
-        cost_estimate=cost(0, 4 * 512 * width),
-        name="direct_rows",
-    )(up, down)
+        share_kernel,
+        out_shape=[jax.ShapeDtypeStruct((count, width), BF16) for count in (64, 64, 512)],
+        in_specs=[smem(), hbm(), hbm()],
+        out_specs=[vmem()] * 3,
+        scratch_shapes=[pltpu.SemaphoreType.DMA((6,))],
+        compiler_params=params(10),
+        cost_estimate=cost(0, 4 * 640 * width),
+        name="weight_shares",
+    )(index, up, down)
 
 
 GROUP = 8
@@ -127,7 +126,7 @@
 def attention_kernel(slope_ref, place_ref, proj_ref, residual_ref, gain_ref, *refs):
     pieces, (state_ref, low_ref, high_ref, cached, bias, sums) = refs[:8], refs[8:]
     for place in range(8):
-        cached[pl.ds(pl.multiple_of(place_ref[place] * 32, 32), 32), :] = pieces[place][...]
+        cached[pl.ds(pl.multiple_of(place_ref[9 + place] * 32, 32), 32), :] = pieces[place][...]
     row = lax.broadcasted_iota(jnp.int32, (128, 256), 0)
     col = lax.broadcasted_iota(jnp.int32, (128, 256), 1)
     bias[...] = jnp.where(col - 128 <= row, (col - 128 - row).astype(F32), -1e30)
@@ -179,7 +178,7 @@
         out_specs=[vmem()] * 3,
         scratch_shapes=[pltpu.VMEM((256, width), BF16)]
         + [pltpu.VMEM((128, 256), F32), pltpu.VMEM((128, 128), F32)],
-        compiler_params=params(),
+        compiler_params=params(20),
         cost_estimate=cost(8 * 128 * 256 * width, 8 * 128 * width * 2),
         name="attention",
     )(slopes, places, proj, residual, gain.reshape(1, width), *pieces)
@@ -293,7 +292,7 @@
             pltpu.SemaphoreType.DMA,
             pltpu.SemaphoreType.DMA((width // COLUMN_TILE, len(split))),
         ],
-        compiler_params=params(),
+        compiler_params=params(14 + total // 256 * 10),
         cost_estimate=cost(4 * total * filled * width, 2 * total * width * 3 + 4 * filled * width),
     )(*tokens, *arrays, *(() if start is None else (start,)))
     return result if len(split) > 1 else result[0]
@@ -305,25 +304,26 @@
     group = lax.axis_index("grp")
     xl, y = me // 4, me % 4
     owner = lax.dynamic_index_in_dim(owner_req, group, 0, keepdims=False)
-    slopes = jnp.exp2(-8.0 * jnp.arange(1, HEADS + 1, dtype=F32) / HEADS)
+    slopes = jnp.asarray(np.exp2(-8.0 * np.arange(1, HEADS + 1) / HEADS), F32)
 
     other = (1 - xl) * 4 + y
     dests = [((xl + dx) % 2) * 4 + (y + dy) % 4 for dx, dy in OFFSETS]
-    origins = jnp.stack([((xl + dx) % 2) * 4 + (y - dy) % 4 for dx, dy in OFFSETS]).astype(jnp.int32)
-    cuts = cut_slices(jnp.stack(dests + [other]).astype(jnp.int32), prefix_cache.reshape(256, width), up, down)
+    origins = [((xl + dx) % 2) * 4 + (y - dy) % 4 for dx, dy in OFFSETS]
+    index = jnp.stack(dests + [other] + origins).astype(jnp.int32)
+    cuts = cut_slices(index, prefix_cache.reshape(256, width))
     kept = cuts[0]
     for place in range(1, 8):
         got = send(cuts[place], req_offset(*OFFSETS[place]))
         kept = jnp.where(origins[place] == owner, got, kept)
     pieces = [kept] + [send(kept, req_offset(*OFFSETS[place])) for place in range(1, 8)]
 
-    shard = send(cuts[8], X_CUT)
-    direct = send(direct_rows(up, down), X_CUT)
-
-    states, low, high = attention(slopes, origins, suffix_proj[0, 0], residual[0, 0], norm_gain, pieces)
-
-    shard, _ = lax.optimization_barrier((shard, (pieces[5], pieces[6], pieces[7])))
-    a_own, b_own = shard[:64], shard[64:]
+    first, second, direct = weight_shares(index, up, down)
+    first, second = send(first, X_CUT), send(second, X_CUT)
+    direct = send(direct, X_CUT)
+
+    states, low, high = attention(slopes, index, suffix_proj[0, 0], residual[0, 0], norm_gain, pieces)
+
+    a_own, b_own, _ = lax.optimization_barrier((first, second, tuple(pieces)))
     a_x = send(a_own, X_LOW)
     b_m, b_p = send(b_own, Y_UP), send(b_own, Y_DOWN)
     b_2 = send(b_own, req_offset(0, 2))
@@ -331,11 +331,11 @@
     a_pair = jnp.concatenate([a_own, a_x])
     a_m, a_p = send(a_pair, Y_UP), send(a_pair, Y_DOWN)
     a_2 = send(a_pair, req_offset(0, 2))
-    far = [shard, direct, a_x, b_m, b_p, b_2, b_x, a_m, a_p, a_2]
+    far = [a_own, b_own, direct, a_x, b_m, b_p, b_2, b_x, a_m, a_p, a_2]
     pieces_of = lambda index, count: [(index, 64 * i, index, 64 * i + 32, 32) for i in range(count)]
     far_units = [
-        *pieces_of(0, 2), (1, 0, 1, 256, 256), *pieces_of(2, 1), *pieces_of(3, 1), *pieces_of(4, 1), *pieces_of(5, 1),
-        *pieces_of(7, 2), *pieces_of(8, 2), *pieces_of(9, 2), *pieces_of(6, 4),
+        *pieces_of(0, 1), *pieces_of(1, 1), (2, 0, 2, 256, 256), *pieces_of(3, 1), *pieces_of(4, 1), *pieces_of(5, 1),
+        *pieces_of(6, 1), *pieces_of(8, 2), *pieces_of(9, 2), *pieces_of(10, 2), *pieces_of(7, 4),
     ]
     near, near_units = [up, down], [(0, 0, 1, 0, 768)]
 

time: 291 us -> 258 us (0.89)
  Pallas kernels: 87.6 us -> 55.8 us
  waiting for transfers between devices: 129 us -> 107 us
  starting transfers between devices: 53.5 us -> 66.3 us
  local copies, waits for them, and re-layouts: 6.48 us -> 15.8 us
    pallas_call x6, Pallas kernels: 71 us -> 46.4 us  [ffn(): pl.pallas_call(functools.partial(ffn_kernel, rows, len(arrays), ups, down...]
    ppermute x46 -> x47, waiting for transfers between devices: 129 us -> 107 us  [send(): return lax.ppermute(value, AXES, table)]
    ppermute x46 -> x47, starting transfers between devices: 53.5 us -> 66.3 us  [send(): return lax.ppermute(value, AXES, table)]
    unnamed x66 -> x79, local copies, waits for them, and re-layouts: 3.49 us -> 14.2 us
    pallas_call x1, Pallas kernels: 4.49 us -> 0.68 us  [cut_slices(): pl.pallas_call(cut_kernel, out_shape=[jax.ShapeDtypeStruct((32, width), B...]
  transfers between devices with their start and end apart: 46 -> 47, of which waited for: 18 -> 19; matrix products, arithmetic and copies ran while one was open for 3% -> 2% of each run, Pallas kernels for 29% -> 22%
where the time goes in v3:
time: 258 us; the launch traced here: 255 us
  waiting for transfers between devices  107 us (41%)
  starting transfers between devices  66.3 us (26%)
  Pallas kernels  55.8 us (22%)
  local copies, waits for them, and re-layouts  15.8 us (6%)
  between operations  5.67 us (2%)
  other arithmetic  4.66 us (2%)
    ppermute x47, waiting for transfers between devices, send(): return lax.ppermute(value, AXES, table)  107 us
    ppermute x47, starting transfers between devices, send(): return lax.ppermute(value, AXES, table)  66.3 us
    pallas_call x6, Pallas kernels, ffn(): pl.pallas_call(functools.partial(ffn_kernel, rows, len(arrays), ups, down...  46.4 us
    unnamed x79, local copies, waits for them, and re-layouts  14.2 us
    pallas_call x1, Pallas kernels, attention(): pl.pallas_call(attention_kernel, out_shape=[jax.ShapeDtypeStruct((128, wi...  5.71 us
  transfers between devices with their start and end apart: 47, of which 19 were waited for; matrix products, arithmetic and copies ran while one was open for 2% of the time, Pallas kernels for 22%

profile of v3, /device:TPU:0, one launch (start us, length us, event | category | flops | bytes accessed | tf_op | source)
XLA Modules:
  0.0 255.1 jit_solution(4339834708979098078)
XLA Ops:
  0.1 1.6 copy-done.29
  1.7 0.7 cut_slices.1
  2.4 1.7 collective-permute-start
  4.1 3.0 %collective-permute-start.1 = (bf16[32,4096]{1,0:T(8,128)(2,1)S(1)}, bf16[32,4096]{1,0:T(8,128)(2,1)S(1)}, u32[]{:S(2)}, u32[]{:S(2)}) collective-permute-start(bf16[32,4096]{1,0:T(8,128)(2,1)S(1)} %get-tuple-element.30), channel_id=1, source_target_pairs={{0,48},{1,49},{2,50},{3,51},{4,52},{5,53},{6,54},{7,55},{8,56},{9,... | collective-permute-start | bytes 786440 | tf_op jit(solution)/shard_map/ppermute | solution.py:47
  7.1 3.2 %collective-permute-start.3 = (bf16[32,4096]{1,0:T(8,128)(2,1)S(1)}, bf16[32,4096]{1,0:T(8,128)(2,1)S(1)}, u32[]{:S(2)}, u32[]{:S(2)}) collective-permute-start(bf16[32,4096]{1,0:T(8,128)(2,1)S(1)} %get-tuple-element.32), channel_id=1, source_target_pairs={{0,112},{1,113},{2,114},{3,115},{4,116},{5,117},{6,118},{7,119},{8... | collective-permute-start | bytes 786440 | tf_op jit(solution)/shard_map/ppermute | solution.py:47
  10.4 4.6 %collective-permute-start.5 = (bf16[32,4096]{1,0:T(8,128)(2,1)S(1)}, bf16[32,4096]{1,0:T(8,128)(2,1)S(1)}, u32[]{:S(2)}, u32[]{:S(2)}) collective-permute-start(bf16[32,4096]{1,0:T(8,128)(2,1)S(1)} %get-tuple-element.34), channel_id=1, source_target_pairs={{0,32},{1,33},{2,34},{3,35},{4,36},{5,37},{6,38},{7,39},{8,40},{9,... | collective-permute-start | bytes 786440 | tf_op jit(solution)/shard_map/ppermute | solution.py:47
  14.9 11.5 %collective-permute-done.1 = bf16[32,4096]{1,0:T(8,128)(2,1)S(1)} collective-permute-done((bf16[32,4096]{1,0:T(8,128)(2,1)S(1)}, bf16[32,4096]{1,0:T(8,128)(2,1)S(1)}, u32[]{:S(2)}, u32[]{:S(2)}) %collective-permute-start.1) | collective-permute-done | bytes 262176 | tf_op jit(solution)/shard_map/ppermute | solution.py:47
  26.4 0.6 dynamic_slice.4
  31.6 7.1 %collective-permute-done.6 = bf16[32,4096]{1,0:T(8,128)(2,1)S(1)} collective-permute-done((bf16[32,4096]{1,0:T(8,128)(2,1)S(1)}, bf16[32,4096]{1,0:T(8,128)(2,1)S(1)}, u32[]{:S(2)}, u32[]{:S(2)}) %collective-permute-start.6) | collective-permute-done | bytes 262176 | tf_op jit(solution)/shard_map/ppermute | solution.py:47
  38.9 1.8 collective-permute-start.8
  40.8 2.9 %collective-permute-start.9 = (bf16[32,4096]{1,0:T(8,128)(2,1)S(1)}, bf16[32,4096]{1,0:T(8,128)(2,1)S(1)}, u32[]{:S(2)}, u32[]{:S(2)}) collective-permute-start(bf16[32,4096]{1,0:T(8,128)(2,1)S(1)} %select_select_fusion.refs_0_), channel_id=1, source_target_pairs={{0,80},{1,81},{2,82},{3,83},{4,84},{5,85},{6,86},{7,87},{8,88},{9,... | collective-permute-start | bytes 786440 | tf_op jit(solution)/shard_map/ppermute | solution.py:47
  43.7 2.8 %copy-done = bf16[768,4096]{1,0:T(8,128)(2,1)S(1)} copy-done((bf16[768,4096]{1,0:T(8,128)(2,1)S(1)}, bf16[768,4096]{1,0:T(8,128)(2,1)}, u32[]{:S(2)}) %copy-start) | copy-done | bytes 6291480
  46.5 2.8 %copy-done.1 = bf16[768,4096]{1,0:T(8,128)(2,1)S(1)} copy-done((bf16[768,4096]{1,0:T(8,128)(2,1)S(1)}, bf16[768,4096]{1,0:T(8,128)(2,1)}, u32[]{:S(2)}) %copy-start.1) | copy-done | bytes 6291480
  49.3 3.0 %weight_shares.1 = (bf16[64,4096]{1,0:T(8,128)(2,1)S(1)}, bf16[64,4096]{1,0:T(8,128)(2,1)S(1)}, bf16[512,4096]{1,0:T(8,128)(2,1)}) custom-call(s32[17]{0:T(128)S(1)} %stack.65.index_ref.place_ref, bf16[768,4096]{1,0:T(8,128)(2,1)S(1)} %copy-done, bf16[768,4096]{1,0:T(8,128)(2,1)S(1)} %copy-done.1), custom_call_target="tpu_custom_call" | custom-call | bytes 10485760 | tf_op jit(solution)/shard_map/weight_shares/pallas_call | solution.py:111
  52.3 2.2 collective-permute-start.16
  54.4 2.1 collective-permute-start.10
  56.6 1.2 collective-permute-start.17
  57.7 2.1 collective-permute-start.18
  59.9 1.8 collective-permute-done.10.refs_4_
  61.7 4.4 %collective-permute-start.12 = (bf16[32,4096]{1,0:T(8,128)(2,1)S(1)}, bf16[32,4096]{1,0:T(8,128)(2,1)S(1)}, u32[]{:S(2)}, u32[]{:S(2)}) collective-permute-start(bf16[32,4096]{1,0:T(8,128)(2,1)S(1)} %select_select_fusion.refs_0_), channel_id=1, source_target_pairs={{0,48},{1,49},{2,50},{3,51},{4,52},{5,53},{6,54},{7,55},{8,56},{9,... | collective-permute-start | bytes 786440 | tf_op jit(solution)/shard_map/ppermute | solution.py:47
  66.5 11.7 %collective-permute-done.12.refs_6_ = bf16[32,4096]{1,0:T(8,128)(2,1)S(1)} collective-permute-done((bf16[32,4096]{1,0:T(8,128)(2,1)S(1)}, bf16[32,4096]{1,0:T(8,128)(2,1)S(1)}, u32[]{:S(2)}, u32[]{:S(2)}) %collective-permute-start.12) | collective-permute-done | bytes 262176 | tf_op jit(solution)/shard_map/ppermute | solution.py:47
  78.3 1.3 collective-permute-done.17.refs_5_.refs_9_
  79.6 3.2 %collective-permute-start.21 = (bf16[64,4096]{1,0:T(8,128)(2,1)S(1)}, bf16[64,4096]{1,0:T(8,128)(2,1)S(1)}, u32[]{:S(2)}, u32[]{:S(2)}) collective-permute-start(bf16[64,4096]{1,0:T(8,128)(2,1)S(1)} %collective-permute-done.17.refs_5_.refs_9_), channel_id=1, source_target_pairs={{0,48},{1,49},{2,50},{3,51},{4,52},{5,53},{6,54},{7,55},{8,56},{9,... | collective-permute-start | bytes 1572872 | tf_op jit(solution)/shard_map/ppermute | solution.py:47
  82.8 2.9 %collective-permute-start.22 = (bf16[64,4096]{1,0:T(8,128)(2,1)S(1)}, bf16[64,4096]{1,0:T(8,128)(2,1)S(1)}, u32[]{:S(2)}, u32[]{:S(2)}) collective-permute-start(bf16[64,4096]{1,0:T(8,128)(2,1)S(1)} %collective-permute-done.17.refs_5_.refs_9_), channel_id=1, source_target_pairs={{0,32},{1,33},{2,34},{3,35},{4,36},{5,37},{6,38},{7,39},{8,40},{9,... | collective-permute-start | bytes 1572872 | tf_op jit(solution)/shard_map/ppermute | solution.py:47
  85.8 5.7 %attention.1 = (bf16[128,4096]{1,0:T(8,128)(2,1)S(1)}, bf16[64,4096]{1,0:T(8,128)(2,1)}, bf16[64,4096]{1,0:T(8,128)(2,1)}) custom-call(f32[32]{0:T(128)S(1)} %copy-done.35, s32[17]{0:T(128)S(1)} %stack.65.index_ref.place_ref, bf16[3,128,4096]{2,1,0:T(8,128)(2,1)S(1)} %bitcast.26, bf16[128,4096]{1,0:T(8,128)(2,1)S(1)} %bitcast.28, f32[1,4096]{1,0:T(1,128)S(1)} %bitcast.29, ...), custom_call_target="tpu_custom_call" | custom-call | flops 1073741824 | bytes 8388608 | tf_op jit(solution)/shard_map/attention/pallas_call | solution.py:174
  91.5 1.0 copy-done.30
  92.5 1.9 collective-permute-start.28
  94.4 1.9 collective-permute-start.29
  96.7 4.0 %collective-permute-start.30 = (bf16[64,4096]{1,0:T(8,128)(2,1)}, bf16[64,4096]{1,0:T(8,128)(2,1)S(1)}, u32[]{:S(2)}, u32[]{:S(2)}) collective-permute-start(bf16[64,4096]{1,0:T(8,128)(2,1)} %get-tuple-element.38.refs_0_), channel_id=1, source_target_pairs={{0,12},{1,13},{2,14},{3,15},{4,0},{5,1},{6,2},{7,3},{8,4},{9,5},{1... | collective-permute-start | bytes 1572872 | tf_op jit(solution)/shard_map/ppermute | solution.py:47
  101.0 2.9 %collective-permute-done.28.refs_0_ = bf16[64,4096]{1,0:T(8,128)(2,1)S(1)} collective-permute-done((bf16[64,4096]{1,0:T(8,128)(2,1)}, bf16[64,4096]{1,0:T(8,128)(2,1)S(1)}, u32[]{:S(2)}, u32[]{:S(2)}) %collective-permute-start.28) | collective-permute-done | bytes 524320 | tf_op jit(solution)/shard_map/ppermute | solution.py:47
  103.9 2.0 collective-permute-start.31
  105.9 3.6 %collective-permute-done.29.refs_1_ = bf16[64,4096]{1,0:T(8,128)(2,1)S(1)} collective-permute-done((bf16[64,4096]{1,0:T(8,128)(2,1)}, bf16[64,4096]{1,0:T(8,128)(2,1)S(1)}, u32[]{:S(2)}, u32[]{:S(2)}) %collective-permute-start.29) | collective-permute-done | bytes 524320 | tf_op jit(solution)/shard_map/ppermute | solution.py:47
  110.0 1.2 collective-permute-done.19.refs_7_.refs_11_
  111.1 1.6 collective-permute-start.37
  112.8 2.7 %collective-permute-done.31.refs_3_ = bf16[64,4096]{1,0:T(8,128)(2,1)S(1)} collective-permute-done((bf16[64,4096]{1,0:T(8,128)(2,1)}, bf16[64,4096]{1,0:T(8,128)(2,1)S(1)}, u32[]{:S(2)}, u32[]{:S(2)}) %collective-permute-start.31) | collective-permute-done | bytes 524320 | tf_op jit(solution)/shard_map/ppermute | solution.py:47
  115.6 3.6 %collective-permute-start.38 = (bf16[64,4096]{1,0:T(8,128)(2,1)S(1)}, bf16[64,4096]{1,0:T(8,128)(2,1)S(1)}, u32[]{:S(2)}, u32[]{:S(2)}) collective-permute-start(bf16[64,4096]{1,0:T(8,128)(2,1)S(1)} %collective-permute-done.31.refs_3_), channel_id=1, source_target_pairs={{0,12},{1,13},{2,14},{3,15},{4,0},{5,1},{6,2},{7,3},{8,4},{9,5},{1... | collective-permute-start | bytes 1572872 | tf_op jit(solution)/shard_map/ppermute | solution.py:47
  119.1 1.3 collective-permute-start.24
  120.4 1.1 collective-permute-done.37.refs_0_
  121.5 1.7 collective-permute-start.25
  123.2 2.6 %collective-permute-done.38.refs_1_ = bf16[64,4096]{1,0:T(8,128)(2,1)S(1)} collective-permute-done((bf16[64,4096]{1,0:T(8,128)(2,1)S(1)}, bf16[64,4096]{1,0:T(8,128)(2,1)S(1)}, u32[]{:S(2)}, u32[]{:S(2)}) %collective-permute-start.38) | collective-permute-done | bytes 524320 | tf_op jit(solution)/shard_map/ppermute | solution.py:47
  125.8 1.9 collective-permute-start.26
  127.7 9.7 %collective-permute-done.24.refs_12_.refs_16_ = bf16[128,4096]{1,0:T(8,128)(2,1)S(1)} collective-permute-done((bf16[128,4096]{1,0:T(8,128)(2,1)S(1)}, bf16[128,4096]{1,0:T(8,128)(2,1)S(1)}, u32[]{:S(2)}, u32[]{:S(2)}) %collective-permute-start.24) | collective-permute-done | bytes 1048608 | tf_op jit(solution)/shard_map/ppermute | solution.py:47
  137.4 11.5 %collective-permute-done.25.refs_13_.refs_17_ = bf16[128,4096]{1,0:T(8,128)(2,1)S(1)} collective-permute-done((bf16[128,4096]{1,0:T(8,128)(2,1)S(1)}, bf16[128,4096]{1,0:T(8,128)(2,1)S(1)}, u32[]{:S(2)}, u32[]{:S(2)}) %collective-permute-start.25) | collective-permute-done | bytes 1048608 | tf_op jit(solution)/shard_map/ppermute | solution.py:47
  149.5 1.3 collective-permute-done.40.refs_3_
  151.4 6.1 %shard_map.95.refs_15_ = f32[256,4096]{1,0:T(8,128)S(1)} custom-call(bf16[64,4096]{1,0:T(8,128)(2,1)S(1)} %collective-permute-done.37.refs_0_, bf16[64,4096]{1,0:T(8,128)(2,1)S(1)} %collective-permute-done.38.refs_1_, bf16[64,4096]{1,0:T(8,128)(2,1)S(1)} %collective-permute-done.39.refs_2_, bf16[64,4096]{1,0:T(8,128)(2,1)S(1)} %collective-permute-done.40.refs_3_, ...), custom_call_target="tpu_custom_call" | custom-call | flops 3221225472 | bytes 18874368 | tf_op jit(solution)/shard_map/pallas_call | solution.py:277
  157.7 6.9 %shard_map.96 = (bf16[128,4096]{1,0:T(8,128)(2,1)S(1)}, bf16[128,4096]{1,0:T(8,128)(2,1)}) custom-call(bf16[64,4096]{1,0:T(8,128)(2,1)S(1)} %collective-permute-done.37.refs_0_, bf16[64,4096]{1,0:T(8,128)(2,1)S(1)} %collective-permute-done.38.refs_1_, bf16[64,4096]{1,0:T(8,128)(2,1)S(1)} %collective-permute-done.39.refs_2_, ...), custom_call_target="tpu_custom_call" | custom-call | flops 3221225472 | bytes 18874368 | tf_op jit(solution)/shard_map/pallas_call | solution.py:277
  164.6 1.0 copy-done.32
  166.0 0.8 copy-done.27
  167.0 1.2 copy-done.28
  168.1 10.5 %shard_map.93.refs_19_ = f32[512,4096]{1,0:T(8,128)} custom-call(bf16[64,4096]{1,0:T(8,128)(2,1)S(1)} %collective-permute-done.28.refs_0_, bf16[64,4096]{1,0:T(8,128)(2,1)S(1)} %collective-permute-done.29.refs_1_, bf16[64,4096]{1,0:T(8,128)(2,1)S(1)} %collective-permute-done.30.refs_2_, bf16[64,4096]{1,0:T(8,128)(2,1)S(1)} %collective-permute-done.31.refs_3_, ...), custom_call_target="tpu_custom_call" | custom-call | flops 6442450944 | bytes 25165824 | tf_op jit(solution)/shard_map/pallas_call | solution.py:277
  178.7 0.8 copy-done.25
  179.6 1.0 copy-done.26
  180.6 10.2 %shard_map.94 = (bf16[128,4096]{1,0:T(8,128)(2,1)S(1)}, bf16[128,4096]{1,0:T(8,128)(2,1)S(1)}, bf16[128,4096]{1,0:T(8,128)(2,1)S(1)}, bf16[128,4096]{1,0:T(8,128)(2,1)S(1)}) custom-call(bf16[64,4096]{1,0:T(8,128)(2,1)S(1)} %collective-permute-done.28.refs_0_, bf16[64,4096]{1,0:T(8,128)(2,1)S(1)} %collective-permute-done.29.refs_1_, ...), custom_call_target="tpu_custom_call" | custom-call | flops 6442450944 | bytes 25165824 | tf_op jit(solution)/shard_map/pallas_call | solution.py:277
  191.3 1.8 add_convert_fusion.2
  193.1 0.9 fusion.1
  194.0 3.6 %collective-permute-start.45 = (bf16[64,4096]{1,0:T(8,128)(2,1)}, bf16[64,4096]{1,0:T(8,128)(2,1)S(1)}, u32[]{:S(2)}, u32[]{:S(2)}) collective-permute-start(bf16[64,4096]{1,0:T(8,128)(2,1)} %get-tuple-element.54), channel_id=1, source_target_pairs={{0,12},{1,13},{2,14},{3,15},{4,0},{5,1},{6,2},{7,3},{8,4},{9,5},{1... | collective-permute-start | bytes 1572872 | tf_op jit(solution)/shard_map/ppermute | solution.py:47
  197.6 6.6 %shard_map.91.refs_15_ = f32[256,4096]{1,0:T(8,128)S(1)} custom-call(bf16[64,4096]{1,0:T(8,128)(2,1)} %get-tuple-element.38.refs_0_, bf16[64,4096]{1,0:T(8,128)(2,1)} %get-tuple-element.39.refs_1_, bf16[64,4096]{1,0:T(8,128)(2,1)S(1)} %collective-permute-done.14.refs_2_, bf16[64,4096]{1,0:T(8,128)(2,1)S(1)} %collective-permute-done.15.refs_3_, ...), custom_call_target="tpu_custom_call" | custom-call | flops 3221225472 | bytes 18874368 | tf_op jit(solution)/shard_map/pallas_call | solution.py:277
  204.4 1.0 copy-done.24
  205.4 6.2 %shard_map.92 = (bf16[128,4096]{1,0:T(8,128)(2,1)S(1)}, bf16[128,4096]{1,0:T(8,128)(2,1)S(1)}) custom-call(bf16[64,4096]{1,0:T(8,128)(2,1)} %get-tuple-element.38.refs_0_, bf16[64,4096]{1,0:T(8,128)(2,1)} %get-tuple-element.39.refs_1_, bf16[64,4096]{1,0:T(8,128)(2,1)S(1)} %collective-permute-done.14.refs_2_, bf16[64,4096]{1,0:T(8,128)(2,1)S(1)} %copy-done.24, ...), custom_call_target="tpu_custom_call" | custom-call | flops 3221225472 | bytes 18874368 | tf_op jit(solution)/shard_map/pallas_call | solution.py:277
  212.5 3.3 %collective-permute-start.46 = (bf16[128,4096]{1,0:T(8,128)(2,1)S(1)}, bf16[128,4096]{1,0:T(8,128)(2,1)S(1)}, u32[]{:S(2)}, u32[]{:S(2)}) collective-permute-start(bf16[128,4096]{1,0:T(8,128)(2,1)S(1)} %add_convert_fusion), channel_id=1, source_target_pairs={{0,12},{1,13},{2,14},{3,15},{4,0},{5,1},{6,2},{7,3},{8,4},{9,5},{1... | collective-permute-start | bytes 3145736 | tf_op jit(solution)/shard_map/ppermute | solution.py:47
  215.8 11.5 %collective-permute-done.42 = bf16[64,4096]{1,0:T(8,128)(2,1)S(1)} collective-permute-done((bf16[64,4096]{1,0:T(8,128)(2,1)S(1)}, bf16[64,4096]{1,0:T(8,128)(2,1)S(1)}, u32[]{:S(2)}, u32[]{:S(2)}) %collective-permute-start.42) | collective-permute-done | bytes 524320 | tf_op jit(solution)/shard_map/ppermute | solution.py:47
  228.4 9.8 %collective-permute-done.46 = bf16[128,4096]{1,0:T(8,128)(2,1)S(1)} collective-permute-done((bf16[128,4096]{1,0:T(8,128)(2,1)S(1)}, bf16[128,4096]{1,0:T(8,128)(2,1)S(1)}, u32[]{:S(2)}, u32[]{:S(2)}) %collective-permute-start.46) | collective-permute-done | bytes 1048608 | tf_op jit(solution)/shard_map/ppermute | solution.py:47
  238.2 15.0 %collective-permute-done.43 = bf16[128,4096]{1,0:T(8,128)(2,1)S(1)} collective-permute-done((bf16[128,4096]{1,0:T(8,128)(2,1)S(1)}, bf16[128,4096]{1,0:T(8,128)(2,1)S(1)}, u32[]{:S(2)}, u32[]{:S(2)}) %collective-permute-start.43) | collective-permute-done | bytes 1048608 | tf_op jit(solution)/shard_map/ppermute | solution.py:47
  253.2 1.9 fusion
  (130 shorter events, 5.8 us)
Async XLA Ops:
  0.0 26.4 %copy-start.36 = (s32[16]{0:T(128)S(1)}, s32[16]{0:T(128)}, u32[]{:S(2)}) copy-start(s32[16]{0:T(128)} %param.12) | copy-start | bytes 196
  2.4 8.0 %collective-permute-start = (bf16[32,4096]{1,0:T(8,128)(2,1)S(1)}, bf16[32,4096]{1,0:T(8,128)(2,1)S(1)}, u32[]{:S(2)}, u32[]{:S(2)}) collective-permute-start(bf16[32,4096]{1,0:T(8,128)(2,1)S(1)} %get-tuple-element.29), channel_id=1, source_target_pairs={{0,64},{1,65},{2,66},{3,67},{4,68},{5,69},{6,70},{7,71},{8,72},{9,... | collective-permute-start | bytes 786440 | tf_op jit(solution)/shard_map/ppermute | solution.py:47
  4.1 22.4 %collective-permute-start.1 = (bf16[32,4096]{1,0:T(8,128)(2,1)S(1)}, bf16[32,4096]{1,0:T(8,128)(2,1)S(1)}, u32[]{:S(2)}, u32[]{:S(2)}) collective-permute-start(bf16[32,4096]{1,0:T(8,128)(2,1)S(1)} %get-tuple-element.30), channel_id=1, source_target_pairs={{0,48},{1,49},{2,50},{3,51},{4,52},{5,53},{6,54},{7,55},{8,56},{9,... | collective-permute-start | bytes 786440 | tf_op jit(solution)/shard_map/ppermute | solution.py:47
  7.1 24.5 %collective-permute-start.2 = (bf16[32,4096]{1,0:T(8,128)(2,1)S(1)}, bf16[32,4096]{1,0:T(8,128)(2,1)S(1)}, u32[]{:S(2)}, u32[]{:S(2)}) collective-permute-start(bf16[32,4096]{1,0:T(8,128)(2,1)S(1)} %get-tuple-element.31), channel_id=1, source_target_pairs={{0,16},{1,17},{2,18},{3,19},{4,20},{5,21},{6,22},{7,23},{8,24},{9,... | collective-permute-start | bytes 786440 | tf_op jit(solution)/shard_map/ppermute | solution.py:47
  7.1 24.5 %collective-permute-start.3 = (bf16[32,4096]{1,0:T(8,128)(2,1)S(1)}, bf16[32,4096]{1,0:T(8,128)(2,1)S(1)}, u32[]{:S(2)}, u32[]{:S(2)}) collective-permute-start(bf16[32,4096]{1,0:T(8,128)(2,1)S(1)} %get-tuple-element.32), channel_id=1, source_target_pairs={{0,112},{1,113},{2,114},{3,115},{4,116},{5,117},{6,118},{7,119},{8... | collective-permute-start | bytes 786440 | tf_op jit(solution)/shard_map/ppermute | solution.py:47
  10.3 21.3 %collective-permute-start.4 = (bf16[32,4096]{1,0:T(8,128)(2,1)S(1)}, bf16[32,4096]{1,0:T(8,128)(2,1)S(1)}, u32[]{:S(2)}, u32[]{:S(2)}) collective-permute-start(bf16[32,4096]{1,0:T(8,128)(2,1)S(1)} %get-tuple-element.33), channel_id=1, source_target_pairs={{0,80},{1,81},{2,82},{3,83},{4,84},{5,85},{6,86},{7,87},{8,88},{9,... | collective-permute-start | bytes 786440 | tf_op jit(solution)/shard_map/ppermute | solution.py:47
  10.4 21.2 %collective-permute-start.5 = (bf16[32,4096]{1,0:T(8,128)(2,1)S(1)}, bf16[32,4096]{1,0:T(8,128)(2,1)S(1)}, u32[]{:S(2)}, u32[]{:S(2)}) collective-permute-start(bf16[32,4096]{1,0:T(8,128)(2,1)S(1)} %get-tuple-element.34), channel_id=1, source_target_pairs={{0,32},{1,33},{2,34},{3,35},{4,36},{5,37},{6,38},{7,39},{8,40},{9,... | collective-permute-start | bytes 786440 | tf_op jit(solution)/shard_map/ppermute | solution.py:47
  26.4 12.3 %collective-permute-start.6 = (bf16[32,4096]{1,0:T(8,128)(2,1)S(1)}, bf16[32,4096]{1,0:T(8,128)(2,1)S(1)}, u32[]{:S(2)}, u32[]{:S(2)}) collective-permute-start(bf16[32,4096]{1,0:T(8,128)(2,1)S(1)} %get-tuple-element.35), channel_id=1, source_target_pairs={{0,96},{1,97},{2,98},{3,99},{4,100},{5,101},{6,102},{7,103},{8,104... | collective-permute-start | bytes 786440 | tf_op jit(solution)/shard_map/ppermute | solution.py:47
  38.7 47.0 %copy-start.33 = (bf16[1,1,128,4096]{3,2,1,0:T(8,128)(2,1)S(1)}, bf16[1,1,128,4096]{3,2,1,0:T(8,128)(2,1)}, u32[]{:S(2)}) copy-start(bf16[1,1,128,4096]{3,2,1,0:T(8,128)(2,1)} %param.9) | copy-start | bytes 3145732
  38.7 47.0 %copy-start.34 = (f32[4096]{0:T(1024)S(1)}, f32[4096]{0:T(1024)}, u32[]{:S(2)}) copy-start(f32[4096]{0:T(1024)} %param.14) | copy-start | bytes 49156
  38.7 47.0 %copy-start.35 = (f32[32]{0:T(128)S(1)}, f32[32]{0:T(128)}, u32[]{:S(2)}) copy-start(f32[32]{0:T(128)} %constant.140.clone.slope_ref) | copy-start | bytes 388
  38.8 17.7 %collective-permute-start.7 = (bf16[32,4096]{1,0:T(8,128)(2,1)S(1)}, bf16[32,4096]{1,0:T(8,128)(2,1)S(1)}, u32[]{:S(2)}, u32[]{:S(2)}) collective-permute-start(bf16[32,4096]{1,0:T(8,128)(2,1)S(1)} %select_select_fusion.refs_0_), channel_id=1, source_target_pairs={{0,96},{1,97},{2,98},{3,99},{4,100},{5,101},{6,102},{7,103},{8,104... | collective-permute-start | bytes 786440 | tf_op jit(solution)/shard_map/ppermute | solution.py:47
  38.9 17.6 %collective-permute-start.8 = (bf16[32,4096]{1,0:T(8,128)(2,1)S(1)}, bf16[32,4096]{1,0:T(8,128)(2,1)S(1)}, u32[]{:S(2)}, u32[]{:S(2)}) collective-permute-start(bf16[32,4096]{1,0:T(8,128)(2,1)S(1)} %select_select_fusion.refs_0_), channel_id=1, source_target_pairs={{0,32},{1,33},{2,34},{3,35},{4,36},{5,37},{6,38},{7,39},{8,40},{9,... | collective-permute-start | bytes 786440 | tf_op jit(solution)/shard_map/ppermute | solution.py:47
  40.8 17.0 %collective-permute-start.9 = (bf16[32,4096]{1,0:T(8,128)(2,1)S(1)}, bf16[32,4096]{1,0:T(8,128)(2,1)S(1)}, u32[]{:S(2)}, u32[]{:S(2)}) collective-permute-start(bf16[32,4096]{1,0:T(8,128)(2,1)S(1)} %select_select_fusion.refs_0_), channel_id=1, source_target_pairs={{0,80},{1,81},{2,82},{3,83},{4,84},{5,85},{6,86},{7,87},{8,88},{9,... | collective-permute-start | bytes 786440 | tf_op jit(solution)/shard_map/ppermute | solution.py:47
  49.3 36.5 %copy-start.22 = (bf16[1,1,3,128,4096]{4,3,2,1,0:T(8,128)(2,1)S(1)}, bf16[1,1,3,128,4096]{4,3,2,1,0:T(8,128)(2,1)}, u32[]{:S(2)}) copy-start(bf16[1,1,3,128,4096]{4,3,2,1,0:T(8,128)(2,1)} %param.10) | copy-start | bytes 9437188
  52.3 26.0 %collective-permute-start.16 = (bf16[64,4096]{1,0:T(8,128)(2,1)S(1)}, bf16[64,4096]{1,0:T(8,128)(2,1)S(1)}, u32[]{:S(2)}, u32[]{:S(2)}) collective-permute-start(bf16[64,4096]{1,0:T(8,128)(2,1)S(1)} %get-tuple-element.40), channel_id=1, source_target_pairs={{0,66},{1,67},{2,64},{3,65},{4,70},{5,71},{6,68},{7,69},{8,74},{9,... | collective-permute-start | bytes 1572872 | tf_op jit(solution)/shard_map/ppermute | solution.py:47
  54.4 7.3 %collective-permute-start.10 = (bf16[32,4096]{1,0:T(8,128)(2,1)S(1)}, bf16[32,4096]{1,0:T(8,128)(2,1)S(1)}, u32[]{:S(2)}, u32[]{:S(2)}) collective-permute-start(bf16[32,4096]{1,0:T(8,128)(2,1)S(1)} %select_select_fusion.refs_0_), channel_id=1, source_target_pairs={{0,112},{1,113},{2,114},{3,115},{4,116},{5,117},{6,118},{7,119},{8... | collective-permute-start | bytes 786440 | tf_op jit(solution)/shard_map/ppermute | solution.py:47
  56.6 9.5 %collective-permute-start.11 = (bf16[32,4096]{1,0:T(8,128)(2,1)S(1)}, bf16[32,4096]{1,0:T(8,128)(2,1)S(1)}, u32[]{:S(2)}, u32[]{:S(2)}) collective-permute-start(bf16[32,4096]{1,0:T(8,128)(2,1)S(1)} %select_select_fusion.refs_0_), channel_id=1, source_target_pairs={{0,16},{1,17},{2,18},{3,19},{4,20},{5,21},{6,22},{7,23},{8,24},{9,... | collective-permute-start | bytes 786440 | tf_op jit(solution)/shard_map/ppermute | solution.py:47
  56.6 23.0 %collective-permute-start.17 = (bf16[64,4096]{1,0:T(8,128)(2,1)S(1)}, bf16[64,4096]{1,0:T(8,128)(2,1)S(1)}, u32[]{:S(2)}, u32[]{:S(2)}) collective-permute-start(bf16[64,4096]{1,0:T(8,128)(2,1)S(1)} %get-tuple-element.41), channel_id=1, source_target_pairs={{0,66},{1,67},{2,64},{3,65},{4,70},{5,71},{6,68},{7,69},{8,74},{9,... | collective-permute-start | bytes 1572872 | tf_op jit(solution)/shard_map/ppermute | solution.py:47
  57.7 99.8 %collective-permute-start.18 = (bf16[512,4096]{1,0:T(8,128)(2,1)}, bf16[512,4096]{1,0:T(8,128)(2,1)S(1)}, u32[]{:S(2)}, u32[]{:S(2)}) collective-permute-start(bf16[512,4096]{1,0:T(8,128)(2,1)} %get-tuple-element.44), channel_id=1, source_target_pairs={{0,66},{1,67},{2,64},{3,65},{4,70},{5,71},{6,68},{7,69},{8,74},{9,... | collective-permute-start | bytes 12582920 | tf_op jit(solution)/shard_map/ppermute | solution.py:47
  61.7 16.6 %collective-permute-start.12 = (bf16[32,4096]{1,0:T(8,128)(2,1)S(1)}, bf16[32,4096]{1,0:T(8,128)(2,1)S(1)}, u32[]{:S(2)}, u32[]{:S(2)}) collective-permute-start(bf16[32,4096]{1,0:T(8,128)(2,1)S(1)} %select_select_fusion.refs_0_), channel_id=1, source_target_pairs={{0,48},{1,49},{2,50},{3,51},{4,52},{5,53},{6,54},{7,55},{8,56},{9,... | collective-permute-start | bytes 786440 | tf_op jit(solution)/shard_map/ppermute | solution.py:47
  66.1 12.2 %collective-permute-start.13 = (bf16[32,4096]{1,0:T(8,128)(2,1)S(1)}, bf16[32,4096]{1,0:T(8,128)(2,1)S(1)}, u32[]{:S(2)}, u32[]{:S(2)}) collective-permute-start(bf16[32,4096]{1,0:T(8,128)(2,1)S(1)} %select_select_fusion.refs_0_), channel_id=1, source_target_pairs={{0,64},{1,65},{2,66},{3,67},{4,68},{5,69},{6,70},{7,71},{8,72},{9,... | collective-permute-start | bytes 786440 | tf_op jit(solution)/shard_map/ppermute | solution.py:47
  79.6 99.1 %copy-start.14 = (bf16[64,4096]{1,0:T(8,128)(2,1)}, bf16[64,4096]{1,0:T(8,128)(2,1)S(1)}, u32[]{:S(2)}) copy-start(bf16[64,4096]{1,0:T(8,128)(2,1)S(1)} %collective-permute-done.17.refs_5_.refs_9_) | copy-start | bytes 1572868
  79.6 14.8 %collective-permute-start.20 = (bf16[64,4096]{1,0:T(8,128)(2,1)S(1)}, bf16[64,4096]{1,0:T(8,128)(2,1)S(1)}, u32[]{:S(2)}, u32[]{:S(2)}) collective-permute-start(bf16[64,4096]{1,0:T(8,128)(2,1)S(1)} %collective-permute-done.17.refs_5_.refs_9_), channel_id=1, source_target_pairs={{0,16},{1,17},{2,18},{3,19},{4,20},{5,21},{6,22},{7,23},{8,24},{9,... | collective-permute-start | bytes 1572872 | tf_op jit(solution)/shard_map/ppermute | solution.py:47
  79.6 16.7 %collective-permute-start.21 = (bf16[64,4096]{1,0:T(8,128)(2,1)S(1)}, bf16[64,4096]{1,0:T(8,128)(2,1)S(1)}, u32[]{:S(2)}, u32[]{:S(2)}) collective-permute-start(bf16[64,4096]{1,0:T(8,128)(2,1)S(1)} %collective-permute-done.17.refs_5_.refs_9_), channel_id=1, source_target_pairs={{0,48},{1,49},{2,50},{3,51},{4,52},{5,53},{6,54},{7,55},{8,56},{9,... | collective-permute-start | bytes 1572872 | tf_op jit(solution)/shard_map/ppermute | solution.py:47
  82.8 13.9 %collective-permute-start.22 = (bf16[64,4096]{1,0:T(8,128)(2,1)S(1)}, bf16[64,4096]{1,0:T(8,128)(2,1)S(1)}, u32[]{:S(2)}, u32[]{:S(2)}) collective-permute-start(bf16[64,4096]{1,0:T(8,128)(2,1)S(1)} %collective-permute-done.17.refs_5_.refs_9_), channel_id=1, source_target_pairs={{0,32},{1,33},{2,34},{3,35},{4,36},{5,37},{6,38},{7,39},{8,40},{9,... | collective-permute-start | bytes 1572872 | tf_op jit(solution)/shard_map/ppermute | solution.py:47
  85.7 65.6 %slice-start = ((s8[6291456]{0:T(1024)(128)(4,1)}), s8[4194304]{0:T(1024)(128)(4,1)S(1)}, s32[]{:S(2)}) async-start(s8[6291456]{0:T(1024)(128)(4,1)} %bitcast.24), calls=%async_computation | async-start | bytes 8388608
  85.8 65.6 %slice-start.1 = ((s8[6291456]{0:T(1024)(128)(4,1)}), s8[2097152]{0:T(1024)(128)(4,1)S(1)}, s32[]{:S(2)}) async-start(s8[6291456]{0:T(1024)(128)(4,1)} %bitcast.24), calls=%async_computation.1 | async-start | bytes 4194304
  92.5 11.4 %collective-permute-start.28 = (bf16[64,4096]{1,0:T(8,128)(2,1)}, bf16[64,4096]{1,0:T(8,128)(2,1)S(1)}, u32[]{:S(2)}, u32[]{:S(2)}) collective-permute-start(bf16[64,4096]{1,0:T(8,128)(2,1)} %get-tuple-element.38.refs_0_), channel_id=1, source_target_pairs={{0,4},{1,5},{2,6},{3,7},{4,8},{5,9},{6,10},{7,11},{8,12},{9,13},{1... | collective-permute-start | bytes 1572872 | tf_op jit(solution)/shard_map/ppermute | solution.py:47
  94.4 84.3 %copy-start.16 = (bf16[64,4096]{1,0:T(8,128)(2,1)}, bf16[64,4096]{1,0:T(8,128)(2,1)S(1)}, u32[]{:S(2)}) copy-start(bf16[64,4096]{1,0:T(8,128)(2,1)S(1)} %collective-permute-done.20.refs_8_.refs_12_) | copy-start | bytes 1572868
  94.4 56.9 %copy-start.2 = (bf16[768,4096]{1,0:T(8,128)(2,1)S(1)}, bf16[768,4096]{1,0:T(8,128)(2,1)}, u32[]{:S(2)}) copy-start(bf16[768,4096]{1,0:T(8,128)(2,1)} %refs_5_.3) | copy-start | bytes 18874372
  94.4 15.1 %collective-permute-start.29 = (bf16[64,4096]{1,0:T(8,128)(2,1)}, bf16[64,4096]{1,0:T(8,128)(2,1)S(1)}, u32[]{:S(2)}, u32[]{:S(2)}) collective-permute-start(bf16[64,4096]{1,0:T(8,128)(2,1)} %get-tuple-element.39.refs_1_), channel_id=1, source_target_pairs={{0,4},{1,5},{2,6},{3,7},{4,8},{5,9},{6,10},{7,11},{8,12},{9,13},{1... | collective-permute-start | bytes 1572872 | tf_op jit(solution)/shard_map/ppermute | solution.py:47
  96.3 82.3 %copy-start.18 = (bf16[64,4096]{1,0:T(8,128)(2,1)}, bf16[64,4096]{1,0:T(8,128)(2,1)S(1)}, u32[]{:S(2)}) copy-start(bf16[64,4096]{1,0:T(8,128)(2,1)S(1)} %collective-permute-done.21.refs_9_.refs_13_) | copy-start | bytes 1572868
  96.3 14.8 %collective-permute-start.19 = (bf16[64,4096]{1,0:T(8,128)(2,1)S(1)}, bf16[64,4096]{1,0:T(8,128)(2,1)S(1)}, u32[]{:S(2)}, u32[]{:S(2)}) collective-permute-start(bf16[64,4096]{1,0:T(8,128)(2,1)S(1)} %collective-permute-done.16.refs_4_.refs_8_), channel_id=1, source_target_pairs={{0,64},{1,65},{2,66},{3,67},{4,68},{5,69},{6,70},{7,71},{8,72},{9,... | collective-permute-start | bytes 1572872 | tf_op jit(solution)/shard_map/ppermute | solution.py:47
  96.7 82.0 %copy-start.20 = (bf16[64,4096]{1,0:T(8,128)(2,1)}, bf16[64,4096]{1,0:T(8,128)(2,1)S(1)}, u32[]{:S(2)}) copy-start(bf16[64,4096]{1,0:T(8,128)(2,1)S(1)} %collective-permute-done.22.refs_10_.refs_14_) | copy-start | bytes 1572868
  96.7 22.4 %collective-permute-start.30 = (bf16[64,4096]{1,0:T(8,128)(2,1)}, bf16[64,4096]{1,0:T(8,128)(2,1)S(1)}, u32[]{:S(2)}, u32[]{:S(2)}) collective-permute-start(bf16[64,4096]{1,0:T(8,128)(2,1)} %get-tuple-element.38.refs_0_), channel_id=1, source_target_pairs={{0,12},{1,13},{2,14},{3,15},{4,0},{5,1},{6,2},{7,3},{8,4},{9,5},{1... | collective-permute-start | bytes 1572872 | tf_op jit(solution)/shard_map/ppermute | solution.py:47
  103.9 11.7 %collective-permute-start.31 = (bf16[64,4096]{1,0:T(8,128)(2,1)}, bf16[64,4096]{1,0:T(8,128)(2,1)S(1)}, u32[]{:S(2)}, u32[]{:S(2)}) collective-permute-start(bf16[64,4096]{1,0:T(8,128)(2,1)} %get-tuple-element.39.refs_1_), channel_id=1, source_target_pairs={{0,12},{1,13},{2,14},{3,15},{4,0},{5,1},{6,2},{7,3},{8,4},{9,5},{1... | collective-permute-start | bytes 1572872 | tf_op jit(solution)/shard_map/ppermute | solution.py:47
  109.5 41.5 %collective-permute-start.23 = (bf16[256,4096]{1,0:T(8,128)(2,1)S(1)}, bf16[256,4096]{1,0:T(8,128)(2,1)S(1)}, u32[]{:S(2)}, u32[]{:S(2)}) collective-permute-start(bf16[256,4096]{1,0:T(8,128)(2,1)S(1)} %pad_maximum_fusion), channel_id=1, source_target_pairs={{0,64},{1,65},{2,66},{3,67},{4,68},{5,69},{6,70},{7,71},{8,72},{9,... | collective-permute-start | bytes 6291464 | tf_op jit(solution)/shard_map/ppermute | solution.py:47
  111.1 67.6 %copy-start.12 = (bf16[64,4096]{1,0:T(8,128)(2,1)}, bf16[64,4096]{1,0:T(8,128)(2,1)S(1)}, u32[]{:S(2)}) copy-start(bf16[64,4096]{1,0:T(8,128)(2,1)S(1)} %collective-permute-done.19.refs_7_.refs_11_) | copy-start | bytes 1572868
  111.1 10.4 %collective-permute-start.37 = (bf16[64,4096]{1,0:T(8,128)(2,1)S(1)}, bf16[64,4096]{1,0:T(8,128)(2,1)S(1)}, u32[]{:S(2)}, u32[]{:S(2)}) collective-permute-start(bf16[64,4096]{1,0:T(8,128)(2,1)S(1)} %collective-permute-done.28.refs_0_), channel_id=1, source_target_pairs={{0,4},{1,5},{2,6},{3,7},{4,8},{5,9},{6,10},{7,11},{8,12},{9,13},{1... | collective-permute-start | bytes 1572872 | tf_op jit(solution)/shard_map/ppermute | solution.py:47
  115.6 10.3 %collective-permute-start.38 = (bf16[64,4096]{1,0:T(8,128)(2,1)S(1)}, bf16[64,4096]{1,0:T(8,128)(2,1)S(1)}, u32[]{:S(2)}, u32[]{:S(2)}) collective-permute-start(bf16[64,4096]{1,0:T(8,128)(2,1)S(1)} %collective-permute-done.31.refs_3_), channel_id=1, source_target_pairs={{0,12},{1,13},{2,14},{3,15},{4,0},{5,1},{6,2},{7,3},{8,4},{9,5},{1... | collective-permute-start | bytes 1572872 | tf_op jit(solution)/shard_map/ppermute | solution.py:47
  119.1 18.3 %collective-permute-start.24 = (bf16[128,4096]{1,0:T(8,128)(2,1)S(1)}, bf16[128,4096]{1,0:T(8,128)(2,1)S(1)}, u32[]{:S(2)}, u32[]{:S(2)}) collective-permute-start(bf16[128,4096]{1,0:T(8,128)(2,1)S(1)} %constant_dynamic-update-slice_fusion), channel_id=1, source_target_pairs={{0,16},{1,17},{2,18},{3,19},{4,20},{5,21},{6,22},{7,23},{8,24},{9,... | collective-permute-start | bytes 3145736 | tf_op jit(solution)/shard_map/ppermute | solution.py:47
  121.5 27.4 %collective-permute-start.25 = (bf16[128,4096]{1,0:T(8,128)(2,1)S(1)}, bf16[128,4096]{1,0:T(8,128)(2,1)S(1)}, u32[]{:S(2)}, u32[]{:S(2)}) collective-permute-start(bf16[128,4096]{1,0:T(8,128)(2,1)S(1)} %constant_dynamic-update-slice_fusion), channel_id=1, source_target_pairs={{0,48},{1,49},{2,50},{3,51},{4,52},{5,53},{6,54},{7,55},{8,56},{9,... | collective-permute-start | bytes 3145736 | tf_op jit(solution)/shard_map/ppermute | solution.py:47
  125.8 23.1 %collective-permute-start.26 = (bf16[128,4096]{1,0:T(8,128)(2,1)S(1)}, bf16[128,4096]{1,0:T(8,128)(2,1)S(1)}, u32[]{:S(2)}, u32[]{:S(2)}) collective-permute-start(bf16[128,4096]{1,0:T(8,128)(2,1)S(1)} %constant_dynamic-update-slice_fusion), channel_id=1, source_target_pairs={{0,32},{1,33},{2,34},{3,35},{4,36},{5,37},{6,38},{7,39},{8,40},{9,... | collective-permute-start | bytes 3145736 | tf_op jit(solution)/shard_map/ppermute | solution.py:47
  137.4 12.0 %collective-permute-start.39 = (bf16[64,4096]{1,0:T(8,128)(2,1)S(1)}, bf16[64,4096]{1,0:T(8,128)(2,1)S(1)}, u32[]{:S(2)}, u32[]{:S(2)}) collective-permute-start(bf16[64,4096]{1,0:T(8,128)(2,1)S(1)} %collective-permute-done.37.refs_0_), channel_id=1, source_target_pairs={{0,1},{1,0},{2,3},{3,2},{4,5},{5,4},{6,7},{7,6},{8,9},{9,8},{10,11... | collective-permute-start | bytes 1572872 | tf_op jit(solution)/shard_map/ppermute | solution.py:47
  148.9 1.9 collective-permute-start.40
  148.9 16.7 %collective-permute-start.32 = (bf16[64,4096]{1,0:T(8,128)(2,1)S(1)}, bf16[64,4096]{1,0:T(8,128)(2,1)S(1)}, u32[]{:S(2)}, u32[]{:S(2)}) collective-permute-start(bf16[64,4096]{1,0:T(8,128)(2,1)S(1)} %collective-permute-done.28.refs_0_), channel_id=1, source_target_pairs={{0,1},{1,0},{2,3},{3,2},{4,5},{5,4},{6,7},{7,6},{8,9},{9,8},{10,11... | collective-permute-start | bytes 1572872 | tf_op jit(solution)/shard_map/ppermute | solution.py:47
  149.4 17.5 %collective-permute-start.35 = (bf16[64,4096]{1,0:T(8,128)(2,1)S(1)}, bf16[64,4096]{1,0:T(8,128)(2,1)S(1)}, u32[]{:S(2)}, u32[]{:S(2)}) collective-permute-start(bf16[64,4096]{1,0:T(8,128)(2,1)S(1)} %collective-permute-done.31.refs_3_), channel_id=1, source_target_pairs={{0,1},{1,0},{2,3},{3,2},{4,5},{5,4},{6,7},{7,6},{8,9},{9,8},{10,11... | collective-permute-start | bytes 1572872 | tf_op jit(solution)/shard_map/ppermute | solution.py:47
  150.8 15.2 %collective-permute-start.33 = (bf16[64,4096]{1,0:T(8,128)(2,1)S(1)}, bf16[64,4096]{1,0:T(8,128)(2,1)S(1)}, u32[]{:S(2)}, u32[]{:S(2)}) collective-permute-start(bf16[64,4096]{1,0:T(8,128)(2,1)S(1)} %collective-permute-done.29.refs_1_), channel_id=1, source_target_pairs={{0,1},{1,0},{2,3},{3,2},{4,5},{5,4},{6,7},{7,6},{8,9},{9,8},{10,11... | collective-permute-start | bytes 1572872 | tf_op jit(solution)/shard_map/ppermute | solution.py:47
  151.0 16.0 %collective-permute-start.34 = (bf16[64,4096]{1,0:T(8,128)(2,1)S(1)}, bf16[64,4096]{1,0:T(8,128)(2,1)S(1)}, u32[]{:S(2)}, u32[]{:S(2)}) collective-permute-start(bf16[64,4096]{1,0:T(8,128)(2,1)S(1)} %collective-permute-done.30.refs_2_), channel_id=1, source_target_pairs={{0,1},{1,0},{2,3},{3,2},{4,5},{5,4},{6,7},{7,6},{8,9},{9,8},{10,11... | collective-permute-start | bytes 1572872 | tf_op jit(solution)/shard_map/ppermute | solution.py:47
  157.5 40.1 %collective-permute-start.14 = (bf16[64,4096]{1,0:T(8,128)(2,1)}, bf16[64,4096]{1,0:T(8,128)(2,1)S(1)}, u32[]{:S(2)}, u32[]{:S(2)}) collective-permute-start(bf16[64,4096]{1,0:T(8,128)(2,1)} %get-tuple-element.38.refs_0_), channel_id=1, source_target_pairs={{0,1},{1,0},{2,3},{3,2},{4,5},{5,4},{6,7},{7,6},{8,9},{9,8},{10,11... | collective-permute-start | bytes 1572872 | tf_op jit(solution)/shard_map/ppermute | solution.py:47
  165.6 32.0 %collective-permute-start.15 = (bf16[64,4096]{1,0:T(8,128)(2,1)}, bf16[64,4096]{1,0:T(8,128)(2,1)S(1)}, u32[]{:S(2)}, u32[]{:S(2)}) collective-permute-start(bf16[64,4096]{1,0:T(8,128)(2,1)} %get-tuple-element.39.refs_1_), channel_id=1, source_target_pairs={{0,1},{1,0},{2,3},{3,2},{4,5},{5,4},{6,7},{7,6},{8,9},{9,8},{10,11... | collective-permute-start | bytes 1572872 | tf_op jit(solution)/shard_map/ppermute | solution.py:47
  166.8 12.7 %copy-start.6 = (bf16[256,4096]{1,0:T(8,128)(2,1)S(1)}, bf16[256,4096]{1,0:T(8,128)(2,1)}, u32[]{:S(2)}) copy-start(bf16[256,4096]{1,0:T(8,128)(2,1)} %copy-done.5) | copy-start | bytes 6291460
  166.8 12.7 %copy-start.9 = (bf16[128,4096]{1,0:T(8,128)(2,1)S(1)}, bf16[128,4096]{1,0:T(8,128)(2,1)}, u32[]{:S(2)}) copy-start(bf16[128,4096]{1,0:T(8,128)(2,1)} %copy-done.8) | copy-start | bytes 3145732
  166.8 12.7 %copy-start.11 = (bf16[128,4096]{1,0:T(8,128)(2,1)S(1)}, bf16[128,4096]{1,0:T(8,128)(2,1)}, u32[]{:S(2)}) copy-start(bf16[128,4096]{1,0:T(8,128)(2,1)} %copy-done.10) | copy-start | bytes 3145732
  166.8 24.5 %collective-permute-start.41 = (bf16[128,4096]{1,0:T(8,128)(2,1)}, bf16[128,4096]{1,0:T(8,128)(2,1)}, u32[]{:S(2)}, u32[]{:S(2)}) collective-permute-start(bf16[128,4096]{1,0:T(8,128)(2,1)} %get-tuple-element.50), channel_id=1, source_target_pairs={{0,1},{1,0},{2,3},{3,2},{4,5},{5,4},{6,7},{7,6},{8,9},{9,8},{10,11... | collective-permute-start | bytes 3145736 | tf_op jit(solution)/shard_map/ppermute | solution.py:47
  190.8 21.4 %collective-permute-start.44 = (bf16[128,4096]{1,0:T(8,128)(2,1)S(1)}, bf16[128,4096]{1,0:T(8,128)(2,1)S(1)}, u32[]{:S(2)}, u32[]{:S(2)}) collective-permute-start(bf16[128,4096]{1,0:T(8,128)(2,1)S(1)} %get-tuple-element.52), channel_id=1, source_target_pairs={{0,1},{1,0},{2,3},{3,2},{4,5},{5,4},{6,7},{7,6},{8,9},{9,8},{10,11... | collective-permute-start | bytes 3145736 | tf_op jit(solution)/shard_map/ppermute | solution.py:47
  194.0 18.2 %collective-permute-start.45 = (bf16[64,4096]{1,0:T(8,128)(2,1)}, bf16[64,4096]{1,0:T(8,128)(2,1)S(1)}, u32[]{:S(2)}, u32[]{:S(2)}) collective-permute-start(bf16[64,4096]{1,0:T(8,128)(2,1)} %get-tuple-element.54), channel_id=1, source_target_pairs={{0,12},{1,13},{2,14},{3,15},{4,0},{5,1},{6,2},{7,3},{8,4},{9,5},{1... | collective-permute-start | bytes 1572872 | tf_op jit(solution)/shard_map/ppermute | solution.py:47
  204.2 11.6 %collective-permute-start.36 = (bf16[128,4096]{1,0:T(8,128)(2,1)S(1)}, bf16[128,4096]{1,0:T(8,128)(2,1)S(1)}, u32[]{:S(2)}, u32[]{:S(2)}) collective-permute-start(bf16[128,4096]{1,0:T(8,128)(2,1)S(1)} %get-tuple-element.48), channel_id=1, source_target_pairs={{0,1},{1,0},{2,3},{3,2},{4,5},{5,4},{6,7},{7,6},{8,9},{9,8},{10,11... | collective-permute-start | bytes 3145736 | tf_op jit(solution)/shard_map/ppermute | solution.py:47
  211.6 16.8 %collective-permute-start.27 = (bf16[128,4096]{1,0:T(8,128)(2,1)S(1)}, bf16[128,4096]{1,0:T(8,128)(2,1)S(1)}, u32[]{:S(2)}, u32[]{:S(2)}) collective-permute-start(bf16[128,4096]{1,0:T(8,128)(2,1)S(1)} %get-tuple-element.46), channel_id=1, source_target_pairs={{0,1},{1,0},{2,3},{3,2},{4,5},{5,4},{6,7},{7,6},{8,9},{9,8},{10,11... | collective-permute-start | bytes 3145736 | tf_op jit(solution)/shard_map/ppermute | solution.py:47
  212.2 15.1 %collective-permute-start.42 = (bf16[64,4096]{1,0:T(8,128)(2,1)S(1)}, bf16[64,4096]{1,0:T(8,128)(2,1)S(1)}, u32[]{:S(2)}, u32[]{:S(2)}) collective-permute-start(bf16[64,4096]{1,0:T(8,128)(2,1)S(1)} %get-tuple-element.53), channel_id=1, source_target_pairs={{0,4},{1,5},{2,6},{3,7},{4,8},{5,9},{6,10},{7,11},{8,12},{9,13},{1... | collective-permute-start | bytes 1572872 | tf_op jit(solution)/shard_map/ppermute | solution.py:47
  212.5 40.7 %copy-start.31 = (bf16[128,4096]{1,0:T(8,128)(2,1)S(1)}, bf16[128,4096]{1,0:T(8,128)(2,1)}, u32[]{:S(2)}) copy-start(bf16[128,4096]{1,0:T(8,128)(2,1)} %copy-done.30) | copy-start | bytes 3145732
  212.5 25.7 %collective-permute-start.46 = (bf16[128,4096]{1,0:T(8,128)(2,1)S(1)}, bf16[128,4096]{1,0:T(8,128)(2,1)S(1)}, u32[]{:S(2)}, u32[]{:S(2)}) collective-permute-start(bf16[128,4096]{1,0:T(8,128)(2,1)S(1)} %add_convert_fusion), channel_id=1, source_target_pairs={{0,12},{1,13},{2,14},{3,15},{4,0},{5,1},{6,2},{7,3},{8,4},{9,5},{1... | collective-permute-start | bytes 3145736 | tf_op jit(solution)/shard_map/ppermute | solution.py:47
  227.6 25.6 %collective-permute-start.43 = (bf16[128,4096]{1,0:T(8,128)(2,1)S(1)}, bf16[128,4096]{1,0:T(8,128)(2,1)S(1)}, u32[]{:S(2)}, u32[]{:S(2)}) collective-permute-start(bf16[128,4096]{1,0:T(8,128)(2,1)S(1)} %add_convert_fusion.1), channel_id=1, source_target_pairs={{0,4},{1,5},{2,6},{3,7},{4,8},{5,9},{6,10},{7,11},{8,12},{9,13},{1... | collective-permute-start | bytes 3145736 | tf_op jit(solution)/shard_map/ppermute | solution.py:47
  (22 other events, 121.2 us)

commit v4 on v3

--- a/solution.py
+++ b/solution.py
@@ -114,7 +114,7 @@
         in_specs=[smem(), hbm(), hbm()],
         out_specs=[vmem()] * 3,
         scratch_shapes=[pltpu.SemaphoreType.DMA((6,))],
-        compiler_params=params(10),
+        compiler_params=params(58),
         cost_estimate=cost(0, 4 * 640 * width),
         name="weight_shares",
     )(index, up, down)
@@ -207,9 +207,11 @@
     rest = refs[len(token_rows) + source_count :]
     start_ref = rest[0] if with_acc else None
     rest = rest[1:] if with_acc else rest
-    out_count = len(split)
-    outs = rest[:out_count]
-    rows_buf, up_buf, down_buf, hidden, acc, result, token_sem, up_sem, down_sem, acc_sem, out_sem = rest[out_count:]
+    outs = rest[: len(split)]
+    rest = rest[len(split) :]
+    up_buf, down_buf = sources if not ups else rest[:2]
+    rest = rest if not ups else rest[2:]
+    rows_buf, hidden, acc, result, token_sem, up_sem, down_sem, acc_sem, out_sem = rest
     _, width = rows_buf.shape
     at = 0
     moves = []
@@ -235,13 +237,15 @@
     @pl.loop(0, up_buf.shape[0] // UNIT_TILE)
     def _(tile):
         part = pl.ds(pl.multiple_of(tile * UNIT_TILE, UNIT_TILE), UNIT_TILE)
-        pltpu.make_async_copy(up_buf.at[part, :], up_buf.at[part, :], up_sem.at[tile]).wait()
+        if ups:
+            pltpu.make_async_copy(up_buf.at[part, :], up_buf.at[part, :], up_sem.at[tile]).wait()
         pre = lax.dot_general(
             rows_buf[...], up_buf[part, :], (((1,), (1,)), ((), ())), preferred_element_type=F32
         )
         hidden[:, part] = (0.5 * pre * (1.0 + lax.erf(pre * math.sqrt(0.5)))).astype(BF16)
 
-    pltpu.make_async_copy(down_buf, down_buf, down_sem).wait()
+    if downs:
+        pltpu.make_async_copy(down_buf, down_buf, down_sem).wait()
     if with_acc:
         begin.wait()
 
@@ -269,7 +273,8 @@
 
 
 def ffn(tokens, arrays, units, start=None, split=None):
-    ups, downs, filled = unit_copies(units)
+    ups, downs, filled = unit_copies(units) if units else ((), (), arrays[0].shape[0])
+    source = pl.BlockSpec(memory_space=pltpu.HBM) if units else vmem()
     rows = tuple(token.shape[0] for token in tokens)
     total, width = sum(rows), tokens[0].shape[1]
     kind = BF16 if split else F32
@@ -277,12 +282,11 @@
     result = pl.pallas_call(
         functools.partial(ffn_kernel, rows, len(arrays), ups, downs, start is not None, split),
         out_shape=[jax.ShapeDtypeStruct((count, width), kind) for count in split],
-        in_specs=[hbm()] * (len(tokens) + len(arrays) + (start is not None)),
+        in_specs=[hbm()] * len(tokens) + [source] * len(arrays) + [hbm()] * (start is not None),
         out_specs=[hbm()] * len(split),
-        scratch_shapes=[
+        scratch_shapes=[pltpu.VMEM((filled, width), BF16)] * (2 if units else 0)
+        + [
             pltpu.VMEM((total, width), BF16),
-            pltpu.VMEM((filled, width), BF16),
-            pltpu.VMEM((filled, width), BF16),
             pltpu.VMEM((total, filled), BF16),
             pltpu.VMEM((total if start is not None else 8, width), F32),
             pltpu.VMEM((total, width), kind),
@@ -292,7 +296,7 @@
             pltpu.SemaphoreType.DMA,
             pltpu.SemaphoreType.DMA((width // COLUMN_TILE, len(split))),
         ],
-        compiler_params=params(14 + total // 256 * 10),
+        compiler_params=params((14 if units else 1) + total // 256 * 9),
         cost_estimate=cost(4 * total * filled * width, 2 * total * width * 3 + 4 * filled * width),
     )(*tokens, *arrays, *(() if start is None else (start,)))
     return result if len(split) > 1 else result[0]
@@ -324,20 +328,19 @@
     states, low, high = attention(slopes, index, suffix_proj[0, 0], residual[0, 0], norm_gain, pieces)
 
     a_own, b_own, _ = lax.optimization_barrier((first, second, tuple(pieces)))
-    a_x = send(a_own, X_LOW)
-    b_m, b_p = send(b_own, Y_UP), send(b_own, Y_DOWN)
-    b_2 = send(b_own, req_offset(0, 2))
-    b_x = send(jnp.concatenate([b_own, b_m, b_p, b_2]), X_LOW)
-    a_pair = jnp.concatenate([a_own, a_x])
-    a_m, a_p = send(a_pair, Y_UP), send(a_pair, Y_DOWN)
-    a_2 = send(a_pair, req_offset(0, 2))
-    far = [a_own, b_own, direct, a_x, b_m, b_p, b_2, b_x, a_m, a_p, a_2]
+    two = req_offset(0, 2)
+    b_m, b_p, b_2 = send(b_own, Y_UP), send(b_own, Y_DOWN), send(b_own, two)
+    a_x, b_x0 = send(a_own, X_LOW), send(b_own, X_LOW)
+    a_m, a_p, a_2 = send(a_own, Y_UP), send(a_own, Y_DOWN), send(a_own, two)
+    b_x = send(jnp.concatenate([b_m, b_p, b_2]), X_LOW)
+    a_xm, a_xp, a_x2 = send(a_x, Y_UP), send(a_x, Y_DOWN), send(a_x, two)
+    far = [a_own, b_own, direct, a_x, b_m, b_p, b_2, b_x0, a_m, a_p, a_2, a_xm, a_xp, a_x2, b_x]
     pieces_of = lambda index, count: [(index, 64 * i, index, 64 * i + 32, 32) for i in range(count)]
     far_units = [
-        *pieces_of(0, 1), *pieces_of(1, 1), (2, 0, 2, 256, 256), *pieces_of(3, 1), *pieces_of(4, 1), *pieces_of(5, 1),
-        *pieces_of(6, 1), *pieces_of(8, 2), *pieces_of(9, 2), *pieces_of(10, 2), *pieces_of(7, 4),
+        *pieces_of(0, 1), *pieces_of(1, 1), (2, 0, 2, 256, 256),
+        *(piece for index in range(3, 14) for piece in pieces_of(index, 1)), *pieces_of(14, 3),
     ]
-    near, near_units = [up, down], [(0, 0, 1, 0, 768)]
+    near, near_units = [up, down], ()
 
     low_m, high_p = send(low, Z_UP), send(high, Z_DOWN)
     high_m, low_p = send(high, Z_UP), send(low, Z_DOWN)

time: 258 us -> 383 us (1.48)
  waiting for transfers between devices: 107 us -> 182 us
  local copies, waits for them, and re-layouts: 15.8 us -> 43.9 us
  starting transfers between devices: 66.3 us -> 87.1 us
    ppermute x47 -> x51, waiting for transfers between devices: 107 us -> 182 us  [send(): return lax.ppermute(value, AXES, table)]
    unnamed x79 -> x136, local copies, waits for them, and re-layouts: 14.2 us -> 43.1 us
    ppermute x47 -> x51, starting transfers between devices: 66.3 us -> 87.1 us  [send(): return lax.ppermute(value, AXES, table)]
  transfers between devices with their start and end apart: 47 -> 51, of which waited for: 19 -> 20; matrix products, arithmetic and copies ran while one was open for 2% -> 1% of each run, Pallas kernels for 22% -> 15%
where the time goes in v4:
time: 383 us; the launch traced here: 381 us
  waiting for transfers between devices  182 us (48%)
  starting transfers between devices  87.1 us (23%)
  Pallas kernels  57.8 us (15%)
  local copies, waits for them, and re-layouts  43.9 us (11%)
  between operations  5.87 us (2%)
  other arithmetic  4.26 us (1%)
    ppermute x51, waiting for transfers between devices, send(): return lax.ppermute(value, AXES, table)  182 us
    ppermute x51, starting transfers between devices, send(): return lax.ppermute(value, AXES, table)  87.1 us
    pallas_call x6, Pallas kernels, ffn(): pl.pallas_call(functools.partial(ffn_kernel, rows, len(arrays), ups, down...  45.1 us
    unnamed x136, local copies, waits for them, and re-layouts  43.1 us
  transfers between devices with their start and end apart: 51, of which 20 were waited for; matrix products, arithmetic and copies ran while one was open for 1% of the time, Pallas kernels for 15%

profile of v4, /device:TPU:0, one launch (start us, length us, event | category | flops | bytes accessed | tf_op | source)
XLA Modules:
  0.0 381.2 jit_solution(16287620031103398385)
XLA Ops:
  0.1 1.6 copy-done.51
  2.4 1.7 collective-permute-start
  4.1 3.0 collective-permute-start.1
  7.1 3.2 collective-permute-start.3
  10.4 4.6 %collective-permute-start.5 = (bf16[32,4096]{1,0:T(8,128)(2,1)S(1)}, bf16[32,4096]{1,0:T(8,128)(2,1)S(1)}, u32[]{:S(2)}, u32[]{:S(2)}) collective-permute-start(bf16[32,4096]{1,0:T(8,128)(2,1)S(1)} %get-tuple-element.34), channel_id=1, source_target_pairs={{0,32},{1,33},{2,34},{3,35},{4,36},{5,37},{6,38},{7,39},{8,40},{9,... | collective-permute-start | bytes 786440 | tf_op jit(solution)/shard_map/ppermute | solution.py:47
  15.0 11.5 %collective-permute-done.1 = bf16[32,4096]{1,0:T(8,128)(2,1)S(1)} collective-permute-done((bf16[32,4096]{1,0:T(8,128)(2,1)S(1)}, bf16[32,4096]{1,0:T(8,128)(2,1)S(1)}, u32[]{:S(2)}, u32[]{:S(2)}) %collective-permute-start.1) | collective-permute-done | bytes 262176 | tf_op jit(solution)/shard_map/ppermute | solution.py:47
  31.6 7.1 %collective-permute-done.6 = bf16[32,4096]{1,0:T(8,128)(2,1)S(1)} collective-permute-done((bf16[32,4096]{1,0:T(8,128)(2,1)S(1)}, bf16[32,4096]{1,0:T(8,128)(2,1)S(1)}, u32[]{:S(2)}, u32[]{:S(2)}) %collective-permute-start.6) | collective-permute-done | bytes 262176 | tf_op jit(solution)/shard_map/ppermute | solution.py:47
  38.9 1.8 collective-permute-start.8
  40.8 4.0 %collective-permute-start.9 = (bf16[32,4096]{1,0:T(8,128)(2,1)S(1)}, bf16[32,4096]{1,0:T(8,128)(2,1)S(1)}, u32[]{:S(2)}, u32[]{:S(2)}) collective-permute-start(bf16[32,4096]{1,0:T(8,128)(2,1)S(1)} %select_select_fusion.refs_0_), channel_id=1, source_target_pairs={{0,80},{1,81},{2,82},{3,83},{4,84},{5,85},{6,86},{7,87},{8,88},{9,... | collective-permute-start | bytes 786440 | tf_op jit(solution)/shard_map/ppermute | solution.py:47
  44.7 2.7 collective-permute-start.10
  47.8 6.2 %collective-permute-start.12 = (bf16[32,4096]{1,0:T(8,128)(2,1)S(1)}, bf16[32,4096]{1,0:T(8,128)(2,1)}, u32[]{:S(2)}, u32[]{:S(2)}) collective-permute-start(bf16[32,4096]{1,0:T(8,128)(2,1)S(1)} %select_select_fusion.refs_0_), channel_id=1, source_target_pairs={{0,48},{1,49},{2,50},{3,51},{4,52},{5,53},{6,54},{7,55},{8,56},{9,... | collective-permute-start | bytes 786440 | tf_op jit(solution)/shard_map/ppermute | solution.py:47
  54.5 5.6 %weight_shares.1 = (bf16[64,4096]{1,0:T(8,128)(2,1)}, bf16[64,4096]{1,0:T(8,128)(2,1)}, bf16[512,4096]{1,0:T(8,128)(2,1)}) custom-call(s32[17]{0:T(128)} %copy-done.60, bf16[768,4096]{1,0:T(8,128)(2,1)} %refs_4_.3, bf16[768,4096]{1,0:T(8,128)(2,1)} %refs_5_.3), custom_call_target="tpu_custom_call" | custom-call | bytes 10485760 | tf_op jit(solution)/shard_map/weight_shares/pallas_call | solution.py:111
  60.9 2.9 collective-permute-start.18
  64.1 2.9 collective-permute-start.17
  67.1 1.9 copy-done.34
  69.9 6.3 %attention.1 = (bf16[128,4096]{1,0:T(8,128)(2,1)S(1)}, bf16[64,4096]{1,0:T(8,128)(2,1)}, bf16[64,4096]{1,0:T(8,128)(2,1)}) custom-call(f32[32]{0:T(128)S(1)} %copy-done.62, s32[17]{0:T(128)S(1)} %copy-done.61, bf16[3,128,4096]{2,1,0:T(8,128)(2,1)S(1)} %bitcast.28, bf16[128,4096]{1,0:T(8,128)(2,1)S(1)} %bitcast.30, f32[1,4096]{1,0:T(1,128)S(1)} %bitcast.31, ...), custom_call_target="tpu_custom_call" | custom-call | flops 1073741824 | bytes 8388608 | tf_op jit(solution)/shard_map/attention/pallas_call | solution.py:174
  76.2 1.9 collective-permute-start.32
  78.2 1.9 collective-permute-start.33
  80.1 81.8 %collective-permute-done.16.refs_4_.refs_8_ = bf16[64,4096]{1,0:T(8,128)(2,1)S(1)} collective-permute-done((bf16[64,4096]{1,0:T(8,128)(2,1)}, bf16[64,4096]{1,0:T(8,128)(2,1)S(1)}, u32[]{:S(2)}, u32[]{:S(2)}) %collective-permute-start.16) | collective-permute-done | bytes 524320 | tf_op jit(solution)/shard_map/ppermute | solution.py:47
  161.8 4.0 %collective-permute-start.34 = (bf16[64,4096]{1,0:T(8,128)(2,1)}, bf16[64,4096]{1,0:T(8,128)(2,1)S(1)}, u32[]{:S(2)}, u32[]{:S(2)}) collective-permute-start(bf16[64,4096]{1,0:T(8,128)(2,1)} %get-tuple-element.38.refs_0_), channel_id=1, source_target_pairs={{0,12},{1,13},{2,14},{3,15},{4,0},{5,1},{6,2},{7,3},{8,4},{9,5},{1... | collective-permute-start | bytes 1572872 | tf_op jit(solution)/shard_map/ppermute | solution.py:47
  165.9 1.6 collective-permute-done.17.refs_5_.refs_9_
  167.5 4.0 %collective-permute-start.35 = (bf16[64,4096]{1,0:T(8,128)(2,1)}, bf16[64,4096]{1,0:T(8,128)(2,1)S(1)}, u32[]{:S(2)}, u32[]{:S(2)}) collective-permute-start(bf16[64,4096]{1,0:T(8,128)(2,1)} %get-tuple-element.39.refs_1_), channel_id=1, source_target_pairs={{0,12},{1,13},{2,14},{3,15},{4,0},{5,1},{6,2},{7,3},{8,4},{9,5},{1... | collective-permute-start | bytes 1572872 | tf_op jit(solution)/shard_map/ppermute | solution.py:47
  171.6 1.3 collective-permute-done.34.refs_2_
  172.9 2.5 collective-permute-start.21
  175.4 3.2 collective-permute-done.35.refs_3_
  178.5 4.9 %collective-permute-start.22 = (bf16[64,4096]{1,0:T(8,128)(2,1)S(1)}, bf16[64,4096]{1,0:T(8,128)(2,1)S(1)}, u32[]{:S(2)}, u32[]{:S(2)}) collective-permute-start(bf16[64,4096]{1,0:T(8,128)(2,1)S(1)} %collective-permute-done.17.refs_5_.refs_9_), channel_id=1, source_target_pairs={{0,32},{1,33},{2,34},{3,35},{4,36},{5,37},{6,38},{7,39},{8,40},{9,... | collective-permute-start | bytes 1572872 | tf_op jit(solution)/shard_map/ppermute | solution.py:47
  183.4 2.1 collective-permute-done.19.refs_7_.refs_11_
  185.5 8.6 %collective-permute-done.20.refs_8_.refs_12_ = bf16[64,4096]{1,0:T(8,128)(2,1)S(1)} collective-permute-done((bf16[64,4096]{1,0:T(8,128)(2,1)S(1)}, bf16[64,4096]{1,0:T(8,128)(2,1)S(1)}, u32[]{:S(2)}, u32[]{:S(2)}) %collective-permute-start.20) | collective-permute-done | bytes 524320 | tf_op jit(solution)/shard_map/ppermute | solution.py:47
  194.1 9.8 %collective-permute-start.24 = (bf16[64,4096]{1,0:T(8,128)(2,1)S(1)}, bf16[64,4096]{1,0:T(8,128)(2,1)S(1)}, u32[]{:S(2)}, u32[]{:S(2)}) collective-permute-start(bf16[64,4096]{1,0:T(8,128)(2,1)S(1)} %collective-permute-done.16.refs_4_.refs_8_), channel_id=1, source_target_pairs={{0,16},{1,17},{2,18},{3,19},{4,20},{5,21},{6,22},{7,23},{8,24},{9,... | collective-permute-start | bytes 1572872 | tf_op jit(solution)/shard_map/ppermute | solution.py:47
  203.9 4.5 %collective-permute-start.26 = (bf16[64,4096]{1,0:T(8,128)(2,1)S(1)}, bf16[64,4096]{1,0:T(8,128)(2,1)S(1)}, u32[]{:S(2)}, u32[]{:S(2)}) collective-permute-start(bf16[64,4096]{1,0:T(8,128)(2,1)S(1)} %collective-permute-done.16.refs_4_.refs_8_), channel_id=1, source_target_pairs={{0,32},{1,33},{2,34},{3,35},{4,36},{5,37},{6,38},{7,39},{8,40},{9,... | collective-permute-start | bytes 1572872 | tf_op jit(solution)/shard_map/ppermute | solution.py:47
  208.6 5.1 %collective-permute-done.24.refs_12_.refs_16_ = bf16[64,4096]{1,0:T(8,128)(2,1)S(1)} collective-permute-done((bf16[64,4096]{1,0:T(8,128)(2,1)S(1)}, bf16[64,4096]{1,0:T(8,128)(2,1)S(1)}, u32[]{:S(2)}, u32[]{:S(2)}) %collective-permute-start.24) | collective-permute-done | bytes 524320 | tf_op jit(solution)/shard_map/ppermute | solution.py:47
  214.1 11.7 %collective-permute-done.25.refs_13_.refs_17_ = bf16[64,4096]{1,0:T(8,128)(2,1)S(1)} collective-permute-done((bf16[64,4096]{1,0:T(8,128)(2,1)S(1)}, bf16[64,4096]{1,0:T(8,128)(2,1)S(1)}, u32[]{:S(2)}, u32[]{:S(2)}) %collective-permute-start.25) | collective-permute-done | bytes 524320 | tf_op jit(solution)/shard_map/ppermute | solution.py:47
  225.8 3.7 collective-permute-start.28
  229.7 3.5 collective-permute-start.42
  233.2 3.0 collective-permute-done.28.refs_16_.refs_20_
  236.2 1.9 collective-permute-start.29
  238.1 2.1 collective-permute-done.41.refs_0_
  240.7 6.1 %collective-permute-done.29.refs_17_.refs_21_ = bf16[64,4096]{1,0:T(8,128)(2,1)S(1)} collective-permute-done((bf16[64,4096]{1,0:T(8,128)(2,1)S(1)}, bf16[64,4096]{1,0:T(8,128)(2,1)S(1)}, u32[]{:S(2)}, u32[]{:S(2)}) %collective-permute-start.29) | collective-permute-done | bytes 524320 | tf_op jit(solution)/shard_map/ppermute | solution.py:47
  247.9 2.8 copy-done
  250.7 2.8 copy-done.1
  253.5 5.3 %shard_map.95.refs_19_ = f32[256,4096]{1,0:T(8,128)S(1)} custom-call(bf16[64,4096]{1,0:T(8,128)(2,1)S(1)} %collective-permute-done.41.refs_0_, bf16[64,4096]{1,0:T(8,128)(2,1)S(1)} %collective-permute-done.42.refs_1_, bf16[64,4096]{1,0:T(8,128)(2,1)S(1)} %collective-permute-done.43.refs_2_, bf16[64,4096]{1,0:T(8,128)(2,1)S(1)} %collective-permute-done.44.refs_3_, ...), custom_call_target="tpu_custom_call" | custom-call | flops 3221225472 | bytes 18874368 | tf_op jit(solution)/shard_map/pallas_call | solution.py:282
  259.1 6.8 %shard_map.96 = (bf16[128,4096]{1,0:T(8,128)(2,1)S(1)}, bf16[128,4096]{1,0:T(8,128)(2,1)}) custom-call(bf16[64,4096]{1,0:T(8,128)(2,1)S(1)} %collective-permute-done.41.refs_0_, bf16[64,4096]{1,0:T(8,128)(2,1)S(1)} %collective-permute-done.42.refs_1_, bf16[64,4096]{1,0:T(8,128)(2,1)S(1)} %collective-permute-done.43.refs_2_, ...), custom_call_target="tpu_custom_call" | custom-call | flops 3221225472 | bytes 18874368 | tf_op jit(solution)/shard_map/pallas_call | solution.py:282
  269.3 10.3 %shard_map.93.refs_23_ = f32[512,4096]{1,0:T(8,128)S(1)} custom-call(bf16[64,4096]{1,0:T(8,128)(2,1)S(1)} %collective-permute-done.32.refs_0_, bf16[64,4096]{1,0:T(8,128)(2,1)S(1)} %collective-permute-done.33.refs_1_, bf16[64,4096]{1,0:T(8,128)(2,1)S(1)} %collective-permute-done.34.refs_2_, bf16[64,4096]{1,0:T(8,128)(2,1)S(1)} %collective-permute-done.35.refs_3_, ...), custom_call_target="tpu_custom_call" | custom-call | flops 6442450944 | bytes 25165824 | tf_op jit(solution)/shard_map/pallas_call | solution.py:282
  279.6 3.3 copy-done.3
  285.5 1.0 copy-done.5
  286.5 1.0 copy-done.8
  288.6 1.0 copy-done.14
  289.7 1.0 copy-done.17
  290.7 1.0 copy-done.19
  292.8 1.0 copy-done.23
  293.8 1.0 copy-done.25
  297.0 1.0 copy-done.31
  298.0 1.0 copy-done.33
  306.3 9.6 %shard_map.94 = (bf16[128,4096]{1,0:T(8,128)(2,1)S(1)}, bf16[128,4096]{1,0:T(8,128)(2,1)S(1)}, bf16[128,4096]{1,0:T(8,128)(2,1)S(1)}, bf16[128,4096]{1,0:T(8,128)(2,1)S(1)}) custom-call(bf16[64,4096]{1,0:T(8,128)(2,1)S(1)} %copy-done.36, bf16[64,4096]{1,0:T(8,128)(2,1)S(1)} %copy-done.38, bf16[64,4096]{1,0:T(8,128)(2,1)S(1)} %copy-done.40, ...), custom_call_target="tpu_custom_call" | custom-call | flops 6442450944 | bytes 25165824 | tf_op jit(solution)/shard_map/pallas_call | solution.py:282
  316.5 1.5 add_convert_fusion.2
  318.1 3.6 collective-permute-start.49
  321.7 2.8 copy-done.2
  324.5 6.6 %shard_map.91.refs_19_ = f32[256,4096]{1,0:T(8,128)S(1)} custom-call(bf16[64,4096]{1,0:T(8,128)(2,1)} %get-tuple-element.38.refs_0_, bf16[64,4096]{1,0:T(8,128)(2,1)} %get-tuple-element.39.refs_1_, bf16[64,4096]{1,0:T(8,128)(2,1)} %collective-permute-done.14.refs_2_, bf16[64,4096]{1,0:T(8,128)(2,1)} %collective-permute-done.15.refs_3_, ...), custom_call_target="tpu_custom_call" | custom-call | flops 3221225472 | bytes 18874368 | tf_op jit(solution)/shard_map/pallas_call | solution.py:282
  331.3 6.4 %shard_map.92 = (bf16[128,4096]{1,0:T(8,128)(2,1)S(1)}, bf16[128,4096]{1,0:T(8,128)(2,1)S(1)}) custom-call(bf16[64,4096]{1,0:T(8,128)(2,1)} %get-tuple-element.38.refs_0_, bf16[64,4096]{1,0:T(8,128)(2,1)} %get-tuple-element.39.refs_1_, bf16[64,4096]{1,0:T(8,128)(2,1)} %collective-permute-done.14.refs_2_, bf16[64,4096]{1,0:T(8,128)(2,1)} %collective-permute-done.15.refs_3_, ...), custom_call_target="tpu_custom_call" | custom-call | flops 3221225472 | bytes 18874368 | tf_op jit(solution)/shard_map/pallas_call | solution.py:282
  338.7 3.3 collective-permute-start.50
  342.0 11.4 %collective-permute-done.46 = bf16[64,4096]{1,0:T(8,128)(2,1)S(1)} collective-permute-done((bf16[64,4096]{1,0:T(8,128)(2,1)S(1)}, bf16[64,4096]{1,0:T(8,128)(2,1)S(1)}, u32[]{:S(2)}, u32[]{:S(2)}) %collective-permute-start.46) | collective-permute-done | bytes 524320 | tf_op jit(solution)/shard_map/ppermute | solution.py:47
  354.5 9.8 %collective-permute-done.50 = bf16[128,4096]{1,0:T(8,128)(2,1)S(1)} collective-permute-done((bf16[128,4096]{1,0:T(8,128)(2,1)S(1)}, bf16[128,4096]{1,0:T(8,128)(2,1)S(1)}, u32[]{:S(2)}, u32[]{:S(2)}) %collective-permute-start.50) | collective-permute-done | bytes 1048608 | tf_op jit(solution)/shard_map/ppermute | solution.py:47
  364.4 15.0 %collective-permute-done.47 = bf16[128,4096]{1,0:T(8,128)(2,1)S(1)} collective-permute-done((bf16[128,4096]{1,0:T(8,128)(2,1)S(1)}, bf16[128,4096]{1,0:T(8,128)(2,1)S(1)}, u32[]{:S(2)}, u32[]{:S(2)}) %collective-permute-start.47) | collective-permute-done | bytes 1048608 | tf_op jit(solution)/shard_map/ppermute | solution.py:47
  379.4 1.9 fusion
  (195 shorter events, 26.5 us)
Async XLA Ops:
  2.4 8.0 %collective-permute-start = (bf16[32,4096]{1,0:T(8,128)(2,1)S(1)}, bf16[32,4096]{1,0:T(8,128)(2,1)S(1)}, u32[]{:S(2)}, u32[]{:S(2)}) collective-permute-start(bf16[32,4096]{1,0:T(8,128)(2,1)S(1)} %get-tuple-element.29), channel_id=1, source_target_pairs={{0,64},{1,65},{2,66},{3,67},{4,68},{5,69},{6,70},{7,71},{8,72},{9,... | collective-permute-start | bytes 786440 | tf_op jit(solution)/shard_map/ppermute | solution.py:47
  4.1 22.4 %collective-permute-start.1 = (bf16[32,4096]{1,0:T(8,128)(2,1)S(1)}, bf16[32,4096]{1,0:T(8,128)(2,1)S(1)}, u32[]{:S(2)}, u32[]{:S(2)}) collective-permute-start(bf16[32,4096]{1,0:T(8,128)(2,1)S(1)} %get-tuple-element.30), channel_id=1, source_target_pairs={{0,48},{1,49},{2,50},{3,51},{4,52},{5,53},{6,54},{7,55},{8,56},{9,... | collective-permute-start | bytes 786440 | tf_op jit(solution)/shard_map/ppermute | solution.py:47
  7.1 24.5 %collective-permute-start.2 = (bf16[32,4096]{1,0:T(8,128)(2,1)S(1)}, bf16[32,4096]{1,0:T(8,128)(2,1)S(1)}, u32[]{:S(2)}, u32[]{:S(2)}) collective-permute-start(bf16[32,4096]{1,0:T(8,128)(2,1)S(1)} %get-tuple-element.31), channel_id=1, source_target_pairs={{0,16},{1,17},{2,18},{3,19},{4,20},{5,21},{6,22},{7,23},{8,24},{9,... | collective-permute-start | bytes 786440 | tf_op jit(solution)/shard_map/ppermute | solution.py:47
  7.1 24.5 %collective-permute-start.3 = (bf16[32,4096]{1,0:T(8,128)(2,1)S(1)}, bf16[32,4096]{1,0:T(8,128)(2,1)S(1)}, u32[]{:S(2)}, u32[]{:S(2)}) collective-permute-start(bf16[32,4096]{1,0:T(8,128)(2,1)S(1)} %get-tuple-element.32), channel_id=1, source_target_pairs={{0,112},{1,113},{2,114},{3,115},{4,116},{5,117},{6,118},{7,119},{8... | collective-permute-start | bytes 786440 | tf_op jit(solution)/shard_map/ppermute | solution.py:47
  10.3 21.3 %collective-permute-start.4 = (bf16[32,4096]{1,0:T(8,128)(2,1)S(1)}, bf16[32,4096]{1,0:T(8,128)(2,1)S(1)}, u32[]{:S(2)}, u32[]{:S(2)}) collective-permute-start(bf16[32,4096]{1,0:T(8,128)(2,1)S(1)} %get-tuple-element.33), channel_id=1, source_target_pairs={{0,80},{1,81},{2,82},{3,83},{4,84},{5,85},{6,86},{7,87},{8,88},{9,... | collective-permute-start | bytes 786440 | tf_op jit(solution)/shard_map/ppermute | solution.py:47
  10.4 21.2 %collective-permute-start.5 = (bf16[32,4096]{1,0:T(8,128)(2,1)S(1)}, bf16[32,4096]{1,0:T(8,128)(2,1)S(1)}, u32[]{:S(2)}, u32[]{:S(2)}) collective-permute-start(bf16[32,4096]{1,0:T(8,128)(2,1)S(1)} %get-tuple-element.34), channel_id=1, source_target_pairs={{0,32},{1,33},{2,34},{3,35},{4,36},{5,37},{6,38},{7,39},{8,40},{9,... | collective-permute-start | bytes 786440 | tf_op jit(solution)/shard_map/ppermute | solution.py:47
  26.4 12.2 %collective-permute-start.6 = (bf16[32,4096]{1,0:T(8,128)(2,1)S(1)}, bf16[32,4096]{1,0:T(8,128)(2,1)S(1)}, u32[]{:S(2)}, u32[]{:S(2)}) collective-permute-start(bf16[32,4096]{1,0:T(8,128)(2,1)S(1)} %get-tuple-element.35), channel_id=1, source_target_pairs={{0,96},{1,97},{2,98},{3,99},{4,100},{5,101},{6,102},{7,103},{8,104... | collective-permute-start | bytes 786440 | tf_op jit(solution)/shard_map/ppermute | solution.py:47
  38.8 9.0 %collective-permute-start.7 = (bf16[32,4096]{1,0:T(8,128)(2,1)S(1)}, bf16[32,4096]{1,0:T(8,128)(2,1)S(1)}, u32[]{:S(2)}, u32[]{:S(2)}) collective-permute-start(bf16[32,4096]{1,0:T(8,128)(2,1)S(1)} %select_select_fusion.refs_0_), channel_id=1, source_target_pairs={{0,96},{1,97},{2,98},{3,99},{4,100},{5,101},{6,102},{7,103},{8,104... | collective-permute-start | bytes 786440 | tf_op jit(solution)/shard_map/ppermute | solution.py:47
  38.9 15.4 %collective-permute-start.8 = (bf16[32,4096]{1,0:T(8,128)(2,1)S(1)}, bf16[32,4096]{1,0:T(8,128)(2,1)S(1)}, u32[]{:S(2)}, u32[]{:S(2)}) collective-permute-start(bf16[32,4096]{1,0:T(8,128)(2,1)S(1)} %select_select_fusion.refs_0_), channel_id=1, source_target_pairs={{0,32},{1,33},{2,34},{3,35},{4,36},{5,37},{6,38},{7,39},{8,40},{9,... | collective-permute-start | bytes 786440 | tf_op jit(solution)/shard_map/ppermute | solution.py:47
  40.8 19.4 %collective-permute-start.9 = (bf16[32,4096]{1,0:T(8,128)(2,1)S(1)}, bf16[32,4096]{1,0:T(8,128)(2,1)S(1)}, u32[]{:S(2)}, u32[]{:S(2)}) collective-permute-start(bf16[32,4096]{1,0:T(8,128)(2,1)S(1)} %select_select_fusion.refs_0_), channel_id=1, source_target_pairs={{0,80},{1,81},{2,82},{3,83},{4,84},{5,85},{6,86},{7,87},{8,88},{9,... | collective-permute-start | bytes 786440 | tf_op jit(solution)/shard_map/ppermute | solution.py:47
  44.7 19.1 %collective-permute-start.10 = (bf16[32,4096]{1,0:T(8,128)(2,1)S(1)}, bf16[32,4096]{1,0:T(8,128)(2,1)}, u32[]{:S(2)}, u32[]{:S(2)}) collective-permute-start(bf16[32,4096]{1,0:T(8,128)(2,1)S(1)} %select_select_fusion.refs_0_), channel_id=1, source_target_pairs={{0,112},{1,113},{2,114},{3,115},{4,116},{5,117},{6,118},{7,119},{8... | collective-permute-start | bytes 786440 | tf_op jit(solution)/shard_map/ppermute | solution.py:47
  47.4 16.7 %collective-permute-start.11 = (bf16[32,4096]{1,0:T(8,128)(2,1)S(1)}, bf16[32,4096]{1,0:T(8,128)(2,1)}, u32[]{:S(2)}, u32[]{:S(2)}) collective-permute-start(bf16[32,4096]{1,0:T(8,128)(2,1)S(1)} %select_select_fusion.refs_0_), channel_id=1, source_target_pairs={{0,16},{1,17},{2,18},{3,19},{4,20},{5,21},{6,22},{7,23},{8,24},{9,... | collective-permute-start | bytes 786440 | tf_op jit(solution)/shard_map/ppermute | solution.py:47
  47.8 19.3 %collective-permute-start.12 = (bf16[32,4096]{1,0:T(8,128)(2,1)S(1)}, bf16[32,4096]{1,0:T(8,128)(2,1)}, u32[]{:S(2)}, u32[]{:S(2)}) collective-permute-start(bf16[32,4096]{1,0:T(8,128)(2,1)S(1)} %select_select_fusion.refs_0_), channel_id=1, source_target_pairs={{0,48},{1,49},{2,50},{3,51},{4,52},{5,53},{6,54},{7,55},{8,56},{9,... | collective-permute-start | bytes 786440 | tf_op jit(solution)/shard_map/ppermute | solution.py:47
  54.3 12.7 %collective-permute-start.13 = (bf16[32,4096]{1,0:T(8,128)(2,1)S(1)}, bf16[32,4096]{1,0:T(8,128)(2,1)}, u32[]{:S(2)}, u32[]{:S(2)}) collective-permute-start(bf16[32,4096]{1,0:T(8,128)(2,1)S(1)} %select_select_fusion.refs_0_), channel_id=1, source_target_pairs={{0,64},{1,65},{2,66},{3,67},{4,68},{5,69},{6,70},{7,71},{8,72},{9,... | collective-permute-start | bytes 786440 | tf_op jit(solution)/shard_map/ppermute | solution.py:47
  60.9 197.9 %collective-permute-start.18 = (bf16[512,4096]{1,0:T(8,128)(2,1)}, bf16[512,4096]{1,0:T(8,128)(2,1)S(1)}, u32[]{:S(2)}, u32[]{:S(2)}) collective-permute-start(bf16[512,4096]{1,0:T(8,128)(2,1)} %get-tuple-element.44), channel_id=1, source_target_pairs={{0,66},{1,67},{2,64},{3,65},{4,70},{5,71},{6,68},{7,69},{8,74},{9,... | collective-permute-start | bytes 12582920 | tf_op jit(solution)/shard_map/ppermute | solution.py:47
  63.8 98.0 %collective-permute-start.16 = (bf16[64,4096]{1,0:T(8,128)(2,1)}, bf16[64,4096]{1,0:T(8,128)(2,1)S(1)}, u32[]{:S(2)}, u32[]{:S(2)}) collective-permute-start(bf16[64,4096]{1,0:T(8,128)(2,1)} %get-tuple-element.40), channel_id=1, source_target_pairs={{0,66},{1,67},{2,64},{3,65},{4,70},{5,71},{6,68},{7,69},{8,74},{9,... | collective-permute-start | bytes 1572872 | tf_op jit(solution)/shard_map/ppermute | solution.py:47
  64.1 103.3 %collective-permute-start.17 = (bf16[64,4096]{1,0:T(8,128)(2,1)}, bf16[64,4096]{1,0:T(8,128)(2,1)S(1)}, u32[]{:S(2)}, u32[]{:S(2)}) collective-permute-start(bf16[64,4096]{1,0:T(8,128)(2,1)} %get-tuple-element.41), channel_id=1, source_target_pairs={{0,66},{1,67},{2,64},{3,65},{4,70},{5,71},{6,68},{7,69},{8,74},{9,... | collective-permute-start | bytes 1572872 | tf_op jit(solution)/shard_map/ppermute | solution.py:47
  76.2 171.2 %copy-start.52 = (bf16[128,4096]{1,0:T(8,128)(2,1)}, bf16[128,4096]{1,0:T(8,128)(2,1)S(1)}, u32[]{:S(2)}) copy-start(bf16[128,4096]{1,0:T(8,128)(2,1)S(1)} %get-tuple-element.37) | copy-start | bytes 3145732
  76.2 95.3 %collective-permute-start.32 = (bf16[64,4096]{1,0:T(8,128)(2,1)}, bf16[64,4096]{1,0:T(8,128)(2,1)S(1)}, u32[]{:S(2)}, u32[]{:S(2)}) collective-permute-start(bf16[64,4096]{1,0:T(8,128)(2,1)} %get-tuple-element.38.refs_0_), channel_id=1, source_target_pairs={{0,4},{1,5},{2,6},{3,7},{4,8},{5,9},{6,10},{7,11},{8,12},{9,13},{1... | collective-permute-start | bytes 1572872 | tf_op jit(solution)/shard_map/ppermute | solution.py:47
  78.2 93.4 %collective-permute-start.33 = (bf16[64,4096]{1,0:T(8,128)(2,1)}, bf16[64,4096]{1,0:T(8,128)(2,1)S(1)}, u32[]{:S(2)}, u32[]{:S(2)}) collective-permute-start(bf16[64,4096]{1,0:T(8,128)(2,1)} %get-tuple-element.39.refs_1_), channel_id=1, source_target_pairs={{0,4},{1,5},{2,6},{3,7},{4,8},{5,9},{6,10},{7,11},{8,12},{9,13},{1... | collective-permute-start | bytes 1572872 | tf_op jit(solution)/shard_map/ppermute | solution.py:47
  161.8 97.1 %copy-start.13 = (bf16[64,4096]{1,0:T(8,128)(2,1)}, bf16[64,4096]{1,0:T(8,128)(2,1)S(1)}, u32[]{:S(2)}) copy-start(bf16[64,4096]{1,0:T(8,128)(2,1)S(1)} %collective-permute-done.16.refs_4_.refs_8_) | copy-start | bytes 1572868
  161.8 11.1 %collective-permute-start.34 = (bf16[64,4096]{1,0:T(8,128)(2,1)}, bf16[64,4096]{1,0:T(8,128)(2,1)S(1)}, u32[]{:S(2)}, u32[]{:S(2)}) collective-permute-start(bf16[64,4096]{1,0:T(8,128)(2,1)} %get-tuple-element.38.refs_0_), channel_id=1, source_target_pairs={{0,12},{1,13},{2,14},{3,15},{4,0},{5,1},{6,2},{7,3},{8,4},{9,5},{1... | collective-permute-start | bytes 1572872 | tf_op jit(solution)/shard_map/ppermute | solution.py:47
  167.5 91.5 %copy-start.16 = (bf16[64,4096]{1,0:T(8,128)(2,1)}, bf16[64,4096]{1,0:T(8,128)(2,1)S(1)}, u32[]{:S(2)}) copy-start(bf16[64,4096]{1,0:T(8,128)(2,1)S(1)} %collective-permute-done.17.refs_5_.refs_9_) | copy-start | bytes 1572868
  167.5 11.1 %collective-permute-start.35 = (bf16[64,4096]{1,0:T(8,128)(2,1)}, bf16[64,4096]{1,0:T(8,128)(2,1)S(1)}, u32[]{:S(2)}, u32[]{:S(2)}) collective-permute-start(bf16[64,4096]{1,0:T(8,128)(2,1)} %get-tuple-element.39.refs_1_), channel_id=1, source_target_pairs={{0,12},{1,13},{2,14},{3,15},{4,0},{5,1},{6,2},{7,3},{8,4},{9,5},{1... | collective-permute-start | bytes 1572872 | tf_op jit(solution)/shard_map/ppermute | solution.py:47
  171.5 96.7 %copy-start.35 = (bf16[64,4096]{1,0:T(8,128)(2,1)}, bf16[64,4096]{1,0:T(8,128)(2,1)S(1)}, u32[]{:S(2)}) copy-start(bf16[64,4096]{1,0:T(8,128)(2,1)S(1)} %collective-permute-done.32.refs_0_) | copy-start | bytes 1572868
  171.5 14.0 %collective-permute-start.19 = (bf16[64,4096]{1,0:T(8,128)(2,1)S(1)}, bf16[64,4096]{1,0:T(8,128)(2,1)S(1)}, u32[]{:S(2)}, u32[]{:S(2)}) collective-permute-start(bf16[64,4096]{1,0:T(8,128)(2,1)S(1)} %collective-permute-done.16.refs_4_.refs_8_), channel_id=1, source_target_pairs={{0,64},{1,65},{2,66},{3,67},{4,68},{5,69},{6,70},{7,71},{8,72},{9,... | collective-permute-start | bytes 1572872 | tf_op jit(solution)/shard_map/ppermute | solution.py:47
  171.5 96.7 %copy-start.37 = (bf16[64,4096]{1,0:T(8,128)(2,1)}, bf16[64,4096]{1,0:T(8,128)(2,1)S(1)}, u32[]{:S(2)}) copy-start(bf16[64,4096]{1,0:T(8,128)(2,1)S(1)} %collective-permute-done.33.refs_1_) | copy-start | bytes 1572868
  171.5 22.6 %collective-permute-start.20 = (bf16[64,4096]{1,0:T(8,128)(2,1)S(1)}, bf16[64,4096]{1,0:T(8,128)(2,1)S(1)}, u32[]{:S(2)}, u32[]{:S(2)}) collective-permute-start(bf16[64,4096]{1,0:T(8,128)(2,1)S(1)} %collective-permute-done.17.refs_5_.refs_9_), channel_id=1, source_target_pairs={{0,16},{1,17},{2,18},{3,19},{4,20},{5,21},{6,22},{7,23},{8,24},{9,... | collective-permute-start | bytes 1572872 | tf_op jit(solution)/shard_map/ppermute | solution.py:47
  172.9 95.3 %copy-start.39 = (bf16[64,4096]{1,0:T(8,128)(2,1)}, bf16[64,4096]{1,0:T(8,128)(2,1)S(1)}, u32[]{:S(2)}) copy-start(bf16[64,4096]{1,0:T(8,128)(2,1)S(1)} %collective-permute-done.34.refs_2_) | copy-start | bytes 1572868
  172.9 31.0 %collective-permute-start.21 = (bf16[64,4096]{1,0:T(8,128)(2,1)S(1)}, bf16[64,4096]{1,0:T(8,128)(2,1)S(1)}, u32[]{:S(2)}, u32[]{:S(2)}) collective-permute-start(bf16[64,4096]{1,0:T(8,128)(2,1)S(1)} %collective-permute-done.17.refs_5_.refs_9_), channel_id=1, source_target_pairs={{0,48},{1,49},{2,50},{3,51},{4,52},{5,53},{6,54},{7,55},{8,56},{9,... | collective-permute-start | bytes 1572872 | tf_op jit(solution)/shard_map/ppermute | solution.py:47
  178.5 89.7 %copy-start.41 = (bf16[64,4096]{1,0:T(8,128)(2,1)}, bf16[64,4096]{1,0:T(8,128)(2,1)S(1)}, u32[]{:S(2)}) copy-start(bf16[64,4096]{1,0:T(8,128)(2,1)S(1)} %collective-permute-done.35.refs_3_) | copy-start | bytes 1572868
  178.5 25.4 %collective-permute-start.22 = (bf16[64,4096]{1,0:T(8,128)(2,1)S(1)}, bf16[64,4096]{1,0:T(8,128)(2,1)S(1)}, u32[]{:S(2)}, u32[]{:S(2)}) collective-permute-start(bf16[64,4096]{1,0:T(8,128)(2,1)S(1)} %collective-permute-done.17.refs_5_.refs_9_), channel_id=1, source_target_pairs={{0,32},{1,33},{2,34},{3,35},{4,36},{5,37},{6,38},{7,39},{8,40},{9,... | collective-permute-start | bytes 1572872 | tf_op jit(solution)/shard_map/ppermute | solution.py:47
  185.5 73.5 %copy-start.18 = (bf16[64,4096]{1,0:T(8,128)(2,1)}, bf16[64,4096]{1,0:T(8,128)(2,1)S(1)}, u32[]{:S(2)}) copy-start(bf16[64,4096]{1,0:T(8,128)(2,1)S(1)} %collective-permute-done.19.refs_7_.refs_11_) | copy-start | bytes 1572868
  185.5 23.0 %collective-permute-start.23 = (bf16[64,4096]{1,0:T(8,128)(2,1)S(1)}, bf16[64,4096]{1,0:T(8,128)(2,1)S(1)}, u32[]{:S(2)}, u32[]{:S(2)}) collective-permute-start(bf16[64,4096]{1,0:T(8,128)(2,1)S(1)} %collective-permute-done.17.refs_5_.refs_9_), channel_id=1, source_target_pairs={{0,64},{1,65},{2,66},{3,67},{4,68},{5,69},{6,70},{7,71},{8,72},{9,... | collective-permute-start | bytes 1572872 | tf_op jit(solution)/shard_map/ppermute | solution.py:47
  194.1 64.9 %copy-start.4 = (bf16[64,4096]{1,0:T(8,128)(2,1)}, bf16[64,4096]{1,0:T(8,128)(2,1)S(1)}, u32[]{:S(2)}) copy-start(bf16[64,4096]{1,0:T(8,128)(2,1)S(1)} %collective-permute-done.20.refs_8_.refs_12_) | copy-start | bytes 1572868
  194.1 19.6 %collective-permute-start.24 = (bf16[64,4096]{1,0:T(8,128)(2,1)S(1)}, bf16[64,4096]{1,0:T(8,128)(2,1)S(1)}, u32[]{:S(2)}, u32[]{:S(2)}) collective-permute-start(bf16[64,4096]{1,0:T(8,128)(2,1)S(1)} %collective-permute-done.16.refs_4_.refs_8_), channel_id=1, source_target_pairs={{0,16},{1,17},{2,18},{3,19},{4,20},{5,21},{6,22},{7,23},{8,24},{9,... | collective-permute-start | bytes 1572872 | tf_op jit(solution)/shard_map/ppermute | solution.py:47
  203.9 55.1 %copy-start.7 = (bf16[64,4096]{1,0:T(8,128)(2,1)}, bf16[64,4096]{1,0:T(8,128)(2,1)S(1)}, u32[]{:S(2)}) copy-start(bf16[64,4096]{1,0:T(8,128)(2,1)S(1)} %collective-permute-done.21.refs_9_.refs_13_) | copy-start | bytes 1572868
  203.9 21.9 %collective-permute-start.25 = (bf16[64,4096]{1,0:T(8,128)(2,1)S(1)}, bf16[64,4096]{1,0:T(8,128)(2,1)S(1)}, u32[]{:S(2)}, u32[]{:S(2)}) collective-permute-start(bf16[64,4096]{1,0:T(8,128)(2,1)S(1)} %collective-permute-done.16.refs_4_.refs_8_), channel_id=1, source_target_pairs={{0,48},{1,49},{2,50},{3,51},{4,52},{5,53},{6,54},{7,55},{8,56},{9,... | collective-permute-start | bytes 1572872 | tf_op jit(solution)/shard_map/ppermute | solution.py:47
  203.9 55.1 %copy-start.10 = (bf16[64,4096]{1,0:T(8,128)(2,1)}, bf16[64,4096]{1,0:T(8,128)(2,1)S(1)}, u32[]{:S(2)}) copy-start(bf16[64,4096]{1,0:T(8,128)(2,1)S(1)} %collective-permute-done.22.refs_10_.refs_14_) | copy-start | bytes 1572868
  203.9 25.5 %collective-permute-start.26 = (bf16[64,4096]{1,0:T(8,128)(2,1)S(1)}, bf16[64,4096]{1,0:T(8,128)(2,1)S(1)}, u32[]{:S(2)}, u32[]{:S(2)}) collective-permute-start(bf16[64,4096]{1,0:T(8,128)(2,1)S(1)} %collective-permute-done.16.refs_4_.refs_8_), channel_id=1, source_target_pairs={{0,32},{1,33},{2,34},{3,35},{4,36},{5,37},{6,38},{7,39},{8,40},{9,... | collective-permute-start | bytes 1572872 | tf_op jit(solution)/shard_map/ppermute | solution.py:47
  208.5 50.5 %copy-start.20 = (bf16[64,4096]{1,0:T(8,128)(2,1)}, bf16[64,4096]{1,0:T(8,128)(2,1)S(1)}, u32[]{:S(2)}) copy-start(bf16[64,4096]{1,0:T(8,128)(2,1)S(1)} %collective-permute-done.23.refs_11_.refs_15_) | copy-start | bytes 1572868
  208.5 21.2 %collective-permute-start.27 = (bf16[64,4096]{1,0:T(8,128)(2,1)S(1)}, bf16[64,4096]{1,0:T(8,128)(2,1)S(1)}, u32[]{:S(2)}, u32[]{:S(2)}) collective-permute-start(bf16[64,4096]{1,0:T(8,128)(2,1)S(1)} %collective-permute-done.19.refs_7_.refs_11_), channel_id=1, source_target_pairs={{0,16},{1,17},{2,18},{3,19},{4,20},{5,21},{6,22},{7,23},{8,24},{9,... | collective-permute-start | bytes 1572872 | tf_op jit(solution)/shard_map/ppermute | solution.py:47
  213.7 45.3 %copy-start.22 = (bf16[64,4096]{1,0:T(8,128)(2,1)}, bf16[64,4096]{1,0:T(8,128)(2,1)S(1)}, u32[]{:S(2)}) copy-start(bf16[64,4096]{1,0:T(8,128)(2,1)S(1)} %collective-permute-done.24.refs_12_.refs_16_) | copy-start | bytes 1572868
  213.7 33.7 %collective-permute-start.30 = (bf16[192,4096]{1,0:T(8,128)(2,1)S(1)}, bf16[192,4096]{1,0:T(8,128)(2,1)S(1)}, u32[]{:S(2)}, u32[]{:S(2)}) collective-permute-start(bf16[192,4096]{1,0:T(8,128)(2,1)S(1)} %pad_maximum_fusion), channel_id=1, source_target_pairs={{0,64},{1,65},{2,66},{3,67},{4,68},{5,69},{6,70},{7,71},{8,72},{9,... | collective-permute-start | bytes 4718600 | tf_op jit(solution)/shard_map/ppermute | solution.py:47
  225.8 10.4 %collective-permute-start.28 = (bf16[64,4096]{1,0:T(8,128)(2,1)S(1)}, bf16[64,4096]{1,0:T(8,128)(2,1)S(1)}, u32[]{:S(2)}, u32[]{:S(2)}) collective-permute-start(bf16[64,4096]{1,0:T(8,128)(2,1)S(1)} %collective-permute-done.19.refs_7_.refs_11_), channel_id=1, source_target_pairs={{0,48},{1,49},{2,50},{3,51},{4,52},{5,53},{6,54},{7,55},{8,56},{9,... | collective-permute-start | bytes 1572872 | tf_op jit(solution)/shard_map/ppermute | solution.py:47
  229.5 10.7 %collective-permute-start.41 = (bf16[64,4096]{1,0:T(8,128)(2,1)S(1)}, bf16[64,4096]{1,0:T(8,128)(2,1)S(1)}, u32[]{:S(2)}, u32[]{:S(2)}) collective-permute-start(bf16[64,4096]{1,0:T(8,128)(2,1)S(1)} %collective-permute-done.32.refs_0_), channel_id=1, source_target_pairs={{0,4},{1,5},{2,6},{3,7},{4,8},{5,9},{6,10},{7,11},{8,12},{9,13},{1... | collective-permute-start | bytes 1572872 | tf_op jit(solution)/shard_map/ppermute | solution.py:47
  229.7 10.6 %collective-permute-start.42 = (bf16[64,4096]{1,0:T(8,128)(2,1)S(1)}, bf16[64,4096]{1,0:T(8,128)(2,1)S(1)}, u32[]{:S(2)}, u32[]{:S(2)}) collective-permute-start(bf16[64,4096]{1,0:T(8,128)(2,1)S(1)} %collective-permute-done.35.refs_3_), channel_id=1, source_target_pairs={{0,12},{1,13},{2,14},{3,15},{4,0},{5,1},{6,2},{7,3},{8,4},{9,5},{1... | collective-permute-start | bytes 1572872 | tf_op jit(solution)/shard_map/ppermute | solution.py:47
  236.2 10.7 %collective-permute-start.29 = (bf16[64,4096]{1,0:T(8,128)(2,1)S(1)}, bf16[64,4096]{1,0:T(8,128)(2,1)S(1)}, u32[]{:S(2)}, u32[]{:S(2)}) collective-permute-start(bf16[64,4096]{1,0:T(8,128)(2,1)S(1)} %collective-permute-done.19.refs_7_.refs_11_), channel_id=1, source_target_pairs={{0,32},{1,33},{2,34},{3,35},{4,36},{5,37},{6,38},{7,39},{8,40},{9,... | collective-permute-start | bytes 1572872 | tf_op jit(solution)/shard_map/ppermute | solution.py:47
  240.2 6.6 %collective-permute-start.43 = (bf16[64,4096]{1,0:T(8,128)(2,1)S(1)}, bf16[64,4096]{1,0:T(8,128)(2,1)S(1)}, u32[]{:S(2)}, u32[]{:S(2)}) collective-permute-start(bf16[64,4096]{1,0:T(8,128)(2,1)S(1)} %collective-permute-done.41.refs_0_), channel_id=1, source_target_pairs={{0,1},{1,0},{2,3},{3,2},{4,5},{5,4},{6,7},{7,6},{8,9},{9,8},{10,11... | collective-permute-start | bytes 1572872 | tf_op jit(solution)/shard_map/ppermute | solution.py:47
  240.2 7.2 %collective-permute-start.44 = (bf16[64,4096]{1,0:T(8,128)(2,1)S(1)}, bf16[64,4096]{1,0:T(8,128)(2,1)S(1)}, u32[]{:S(2)}, u32[]{:S(2)}) collective-permute-start(bf16[64,4096]{1,0:T(8,128)(2,1)S(1)} %collective-permute-done.42.refs_1_), channel_id=1, source_target_pairs={{0,1},{1,0},{2,3},{3,2},{4,5},{5,4},{6,7},{7,6},{8,9},{9,8},{10,11... | collective-permute-start | bytes 1572872 | tf_op jit(solution)/shard_map/ppermute | solution.py:47
  246.9 20.0 %collective-permute-start.36 = (bf16[64,4096]{1,0:T(8,128)(2,1)S(1)}, bf16[64,4096]{1,0:T(8,128)(2,1)S(1)}, u32[]{:S(2)}, u32[]{:S(2)}) collective-permute-start(bf16[64,4096]{1,0:T(8,128)(2,1)S(1)} %collective-permute-done.32.refs_0_), channel_id=1, source_target_pairs={{0,1},{1,0},{2,3},{3,2},{4,5},{5,4},{6,7},{7,6},{8,9},{9,8},{10,11... | collective-permute-start | bytes 1572872 | tf_op jit(solution)/shard_map/ppermute | solution.py:47
  246.9 21.3 %collective-permute-start.39 = (bf16[64,4096]{1,0:T(8,128)(2,1)S(1)}, bf16[64,4096]{1,0:T(8,128)(2,1)S(1)}, u32[]{:S(2)}, u32[]{:S(2)}) collective-permute-start(bf16[64,4096]{1,0:T(8,128)(2,1)S(1)} %collective-permute-done.35.refs_3_), channel_id=1, source_target_pairs={{0,1},{1,0},{2,3},{3,2},{4,5},{5,4},{6,7},{7,6},{8,9},{9,8},{10,11... | collective-permute-start | bytes 1572872 | tf_op jit(solution)/shard_map/ppermute | solution.py:47
  247.4 19.9 %collective-permute-start.37 = (bf16[64,4096]{1,0:T(8,128)(2,1)S(1)}, bf16[64,4096]{1,0:T(8,128)(2,1)S(1)}, u32[]{:S(2)}, u32[]{:S(2)}) collective-permute-start(bf16[64,4096]{1,0:T(8,128)(2,1)S(1)} %collective-permute-done.33.refs_1_), channel_id=1, source_target_pairs={{0,1},{1,0},{2,3},{3,2},{4,5},{5,4},{6,7},{7,6},{8,9},{9,8},{10,11... | collective-permute-start | bytes 1572872 | tf_op jit(solution)/shard_map/ppermute | solution.py:47
  247.5 20.7 %collective-permute-start.38 = (bf16[64,4096]{1,0:T(8,128)(2,1)S(1)}, bf16[64,4096]{1,0:T(8,128)(2,1)S(1)}, u32[]{:S(2)}, u32[]{:S(2)}) collective-permute-start(bf16[64,4096]{1,0:T(8,128)(2,1)S(1)} %collective-permute-done.34.refs_2_), channel_id=1, source_target_pairs={{0,1},{1,0},{2,3},{3,2},{4,5},{5,4},{6,7},{7,6},{8,9},{9,8},{10,11... | collective-permute-start | bytes 1572872 | tf_op jit(solution)/shard_map/ppermute | solution.py:47
  258.8 62.9 %collective-permute-start.14 = (bf16[64,4096]{1,0:T(8,128)(2,1)}, bf16[64,4096]{1,0:T(8,128)(2,1)}, u32[]{:S(2)}, u32[]{:S(2)}) collective-permute-start(bf16[64,4096]{1,0:T(8,128)(2,1)} %get-tuple-element.38.refs_0_), channel_id=1, source_target_pairs={{0,1},{1,0},{2,3},{3,2},{4,5},{5,4},{6,7},{7,6},{8,9},{9,8},{10,11... | collective-permute-start | bytes 1572872 | tf_op jit(solution)/shard_map/ppermute | solution.py:47
  266.9 54.9 %collective-permute-start.15 = (bf16[64,4096]{1,0:T(8,128)(2,1)}, bf16[64,4096]{1,0:T(8,128)(2,1)}, u32[]{:S(2)}, u32[]{:S(2)}) collective-permute-start(bf16[64,4096]{1,0:T(8,128)(2,1)} %get-tuple-element.39.refs_1_), channel_id=1, source_target_pairs={{0,1},{1,0},{2,3},{3,2},{4,5},{5,4},{6,7},{7,6},{8,9},{9,8},{10,11... | collective-permute-start | bytes 1572872 | tf_op jit(solution)/shard_map/ppermute | solution.py:47
  268.1 48.4 %collective-permute-start.45 = (bf16[128,4096]{1,0:T(8,128)(2,1)}, bf16[128,4096]{1,0:T(8,128)(2,1)}, u32[]{:S(2)}, u32[]{:S(2)}) collective-permute-start(bf16[128,4096]{1,0:T(8,128)(2,1)} %get-tuple-element.50), channel_id=1, source_target_pairs={{0,1},{1,0},{2,3},{3,2},{4,5},{5,4},{6,7},{7,6},{8,9},{9,8},{10,11... | collective-permute-start | bytes 3145736 | tf_op jit(solution)/shard_map/ppermute | solution.py:47
  316.0 22.4 %collective-permute-start.48 = (bf16[128,4096]{1,0:T(8,128)(2,1)S(1)}, bf16[128,4096]{1,0:T(8,128)(2,1)S(1)}, u32[]{:S(2)}, u32[]{:S(2)}) collective-permute-start(bf16[128,4096]{1,0:T(8,128)(2,1)S(1)} %get-tuple-element.52), channel_id=1, source_target_pairs={{0,1},{1,0},{2,3},{3,2},{4,5},{5,4},{6,7},{7,6},{8,9},{9,8},{10,11... | collective-permute-start | bytes 3145736 | tf_op jit(solution)/shard_map/ppermute | solution.py:47
  318.1 20.2 %collective-permute-start.49 = (bf16[64,4096]{1,0:T(8,128)(2,1)S(1)}, bf16[64,4096]{1,0:T(8,128)(2,1)S(1)}, u32[]{:S(2)}, u32[]{:S(2)}) collective-permute-start(bf16[64,4096]{1,0:T(8,128)(2,1)S(1)} %get-tuple-element.54), channel_id=1, source_target_pairs={{0,12},{1,13},{2,14},{3,15},{4,0},{5,1},{6,2},{7,3},{8,4},{9,5},{1... | collective-permute-start | bytes 1572872 | tf_op jit(solution)/shard_map/ppermute | solution.py:47
  331.2 10.8 %collective-permute-start.40 = (bf16[128,4096]{1,0:T(8,128)(2,1)S(1)}, bf16[128,4096]{1,0:T(8,128)(2,1)S(1)}, u32[]{:S(2)}, u32[]{:S(2)}) collective-permute-start(bf16[128,4096]{1,0:T(8,128)(2,1)S(1)} %get-tuple-element.48), channel_id=1, source_target_pairs={{0,1},{1,0},{2,3},{3,2},{4,5},{5,4},{6,7},{7,6},{8,9},{9,8},{10,11... | collective-permute-start | bytes 3145736 | tf_op jit(solution)/shard_map/ppermute | solution.py:47
  337.8 16.8 %collective-permute-start.31 = (bf16[128,4096]{1,0:T(8,128)(2,1)S(1)}, bf16[128,4096]{1,0:T(8,128)(2,1)S(1)}, u32[]{:S(2)}, u32[]{:S(2)}) collective-permute-start(bf16[128,4096]{1,0:T(8,128)(2,1)S(1)} %get-tuple-element.46), channel_id=1, source_target_pairs={{0,1},{1,0},{2,3},{3,2},{4,5},{5,4},{6,7},{7,6},{8,9},{9,8},{10,11... | collective-permute-start | bytes 3145736 | tf_op jit(solution)/shard_map/ppermute | solution.py:47
  338.3 15.1 %collective-permute-start.46 = (bf16[64,4096]{1,0:T(8,128)(2,1)S(1)}, bf16[64,4096]{1,0:T(8,128)(2,1)S(1)}, u32[]{:S(2)}, u32[]{:S(2)}) collective-permute-start(bf16[64,4096]{1,0:T(8,128)(2,1)S(1)} %get-tuple-element.53), channel_id=1, source_target_pairs={{0,4},{1,5},{2,6},{3,7},{4,8},{5,9},{6,10},{7,11},{8,12},{9,13},{1... | collective-permute-start | bytes 1572872 | tf_op jit(solution)/shard_map/ppermute | solution.py:47
  338.7 25.7 %collective-permute-start.50 = (bf16[128,4096]{1,0:T(8,128)(2,1)S(1)}, bf16[128,4096]{1,0:T(8,128)(2,1)S(1)}, u32[]{:S(2)}, u32[]{:S(2)}) collective-permute-start(bf16[128,4096]{1,0:T(8,128)(2,1)S(1)} %add_convert_fusion), channel_id=1, source_target_pairs={{0,12},{1,13},{2,14},{3,15},{4,0},{5,1},{6,2},{7,3},{8,4},{9,5},{1... | collective-permute-start | bytes 3145736 | tf_op jit(solution)/shard_map/ppermute | solution.py:47
  353.8 25.6 %collective-permute-start.47 = (bf16[128,4096]{1,0:T(8,128)(2,1)S(1)}, bf16[128,4096]{1,0:T(8,128)(2,1)S(1)}, u32[]{:S(2)}, u32[]{:S(2)}) collective-permute-start(bf16[128,4096]{1,0:T(8,128)(2,1)S(1)} %add_convert_fusion.1), channel_id=1, source_target_pairs={{0,4},{1,5},{2,6},{3,7},{4,8},{5,9},{6,10},{7,11},{8,12},{9,13},{1... | collective-permute-start | bytes 3145736 | tf_op jit(solution)/shard_map/ppermute | solution.py:47
  (55 other events, 501.0 us)
